TPU v7x, 512 devices: a whole 4x8x8 slice. The times are simulated.
512 devices in a mesh: ab: 16 (over y, x_lo), cd: 32 (over z, x_hi, core).
Axes of the slice: x: 4 (x_hi: 2, x_lo: 2; x = x_hi * 2 + x_lo), y: 8, z: 8, core: 2. Of those that a mesh axis runs over, the one named last changes fastest.
Arguments:
- factors: bfloat16 [128, 128, 2048], P('ab', 'cd'), may hold values from -0.25 to 0.25
- amplitudes: float32 [256, 128, 128], P('cd', 'ab'), may hold values from -4 to 4
- driving: float32 [256, 128, 128], P('cd', 'ab'), may hold values from -8 to 8
- occ_energy: float32 [32], replicated, may hold values from -2 to -0.5
- vir_energy: float32 [128], replicated, may hold values from 0.5 to 3
Outputs:
- new_amplitudes: float32 [256, 128, 128], P('cd', 'ab')
- residual: float32 [256, 128, 128], P('cd', 'ab')
All inputs are finite; a program needn't handle non-finite values.
Results may differ from a plain program's by a relative error of at most 0.0036.
Values may be sent and summed in bfloat16 or wider, within the bound.
No kernel may reach another device: no remote copies, remote signals or barrier semaphores. Data moves between devices by JAX's collectives and lax.ppermute only.
A program may use at most 64 MiB of HBM per device.

v0:
```python
import jax
import jax.numpy as jnp
from jax import lax
from jax.sharding import PartitionSpec as P

ITERS = 2


def local(factors, amplitudes, driving, occ_energy, vir_energy):
    rows = amplitudes.shape[0]
    a_local = amplitudes.shape[1]
    virtuals = amplitudes.shape[2]
    aux_width = factors.shape[2]
    n_cd = lax.axis_size("cd")
    d_local = factors.shape[1]
    pairs = rows * n_cd
    cd_index = lax.axis_index("cd")
    ab_index = lax.axis_index("ab")
    left_rows = lax.all_gather(factors, "cd", axis=1, tiled=True)
    left_flat = left_rows.reshape(a_local * virtuals, aux_width)
    piece = lax.all_gather(factors, "ab", axis=0, tiled=True)
    count = piece.shape[0]
    product = lax.dot_general(
        left_flat,
        piece.reshape(count * d_local, aux_width),
        (((1,), (1,)), ((), ())),
        preferred_element_type=jnp.float32,
    )
    product = product.reshape(a_local, virtuals, count, d_local)
    tiles = (
        product.transpose(0, 2, 3, 1)
        .reshape(a_local, count, d_local * virtuals)
        .astype(jnp.bfloat16)
    )
    tiles = tiles.reshape(a_local * virtuals, d_local * virtuals)
    n_occ = occ_energy.shape[0]
    row_ids = cd_index * rows + lax.iota(jnp.int32, rows)
    orbitals = lax.iota(jnp.int32, n_occ)
    first_hot = (row_ids[:, None] // n_occ == orbitals[None, :]).astype(jnp.float32)
    second_hot = (row_ids[:, None] % n_occ == orbitals[None, :]).astype(jnp.float32)
    occ_pair = jnp.sum((first_hot + second_hot) * occ_energy[None, :], axis=1)
    vir_rows = lax.dynamic_slice_in_dim(vir_energy, ab_index * a_local, a_local)
    denominator = vir_rows[None, :, None] + vir_energy[None, None, :] - occ_pair[:, None, None]
    current = amplitudes
    residual = amplitudes
    for step in range(ITERS):
        rounded = current.astype(jnp.bfloat16)
        every_row = lax.all_gather(rounded, "cd", axis=0, tiled=True)
        columns = lax.dynamic_slice_in_dim(every_row, cd_index * d_local, d_local, 2)
        own_block = columns.transpose(2, 1, 0)
        gathered = lax.all_gather(own_block, "ab", axis=1, tiled=True)
        flat_amps = gathered.reshape(d_local * virtuals, pairs)
        summed = lax.psum_scatter(
            lax.dot_general(
                flat_amps, tiles, (((0,), (1,)), ((), ())), preferred_element_type=jnp.float32
            ),
            "cd",
            scatter_dimension=0,
            tiled=True,
        ).reshape(rows, a_local, virtuals)
        mirrored = lax.all_to_all(summed, "ab", split_axis=2, concat_axis=1, tiled=True).transpose(
            0, 2, 1
        )
        symmetric = 0.5 * (summed + mirrored)
        residual = driving + denominator * current + symmetric
        current = current - residual / denominator
    return (current, residual)


def solution(mesh):
    placed = (P("ab", "cd", None), P("cd", "ab", None), P("cd", "ab", None), P(), P())
    return jax.shard_map(
        local,
        mesh=mesh,
        in_specs=placed,
        out_specs=(P("cd", "ab", None), P("cd", "ab", None)),
        check_vma=False,
    )
```

profile of v0, /device:TPU:1, one launch (start us, length us, event | category | flops | bytes accessed | tf_op | source)
XLA Modules:
  0.0 554.4 jit_solution(14078645966678964496)
XLA Ops:
  7.2 1.6 copy.37
  8.9 0.7 all-gather.3.cloned.1.call-update
  9.7 0.8 convert_element_type.25
  10.4 50.9 %all_gather.18 = bf16[256,8,128]{2,1,0:T(8,128)(2,1)S(1)} all-gather(bf16[8,8,128]{2,1,0:T(8,128)(2,1)S(1)} %convert_element_type.25), channel_id=1, replica_groups=mesh['ab'=16,'cd'=32] {'cd'}, dimensions={0}, use_global_device_ids=true | all-gather | bytes 540672 | tf_op jit(solution)/shard_map/all_gather | solution.py:48
  61.6 0.3 copy.57
  61.9 31.0 %all_gather.19 = bf16[4,128,256]{2,1,0:T(8,128)(2,1)S(1)} all-gather(bf16[4,8,256]{2,1,0:T(8,128)(2,1)S(1)} %bitcast.73), channel_id=1, replica_groups=mesh['ab'=16,'cd'=32] {'ab'}, dimensions={1}, use_global_device_ids=true | all-gather | bytes 278528 | tf_op jit(solution)/shard_map/all_gather | solution.py:51
  92.9 96.3 %all-gather.3.cloned.1.call-done = bf16[8,128,2048]{2,0,1:T(8,128)(2,1)} async-done(((bf16[8,4,2048]{2,0,1:T(8,128)(2,1)}), bf16[8,128,2048]{2,0,1:T(8,128)(2,1)}) %all-gather.3.cloned.1.call-update) | async-done | bytes 4194320 | tf_op jit(solution)/shard_map/all_gather | solution.py:19
  189.2 7.7 %fusion.8 = bf16[8,128,4,128]{1,3,2,0:T(8,128)(2,1)S(1)} fusion(bf16[128,4,2048]{2,0,1:T(8,128)(2,1)} %all-gather.5.cloned.1.call-done, bf16[8,128,2048,1]{2,0,1,3:T(8,128)(2,1)} %bitcast.75), kind=kOutput, calls=%fused_computation.4 | convolution fusion | flops 2148007936 | bytes 7340032 | tf_op jit(solution)/shard_map/dot_general | solution.py:23
  196.9 0.7 copy.40
  197.6 1.4 fusion.15
  199.3 115.4 %reduce-scatter.3.cloned.1.call-done = f32[8,1024]{1,0:T(8,128)} async-done(((f32[256,1024]{1,0:T(8,128)}), f32[8,1024]{1,0:T(8,128)}) %reduce-scatter.3.cloned.1.call-update) | async-done | bytes 32784 | tf_op jit(solution)/shard_map/reduce_scatter | solution.py:53
  314.7 1.0 copy.41
  315.7 0.9 reshape.124
  316.6 6.6 %all-to-all-start = ((f32[16,1,512]{2,1,0:T(1,128)}), f32[16,1,512]{2,1,0:T(1,128)S(1)}, u32[]{:S(2)}, u32[]{:S(2)}) async-start(f32[16,1,512]{2,1,0:T(1,128)} %reshape.124), calls=%async_computation.1 | async-start | bytes 65536 | tf_op jit(solution)/shard_map/all_to_all | solution.py:61
  323.4 7.4 %all-to-all-done = f32[16,1,512]{2,1,0:T(1,128)S(1)} async-done(((f32[16,1,512]{2,1,0:T(1,128)}), f32[16,1,512]{2,1,0:T(1,128)S(1)}, u32[]{:S(2)}, u32[]{:S(2)}) %all-to-all-start) | async-done | bytes 32800 | tf_op jit(solution)/shard_map/all_to_all | solution.py:61
  330.8 0.5 broadcast.123
  331.3 0.7 reduce
  332.0 0.3 reshape.125
  332.4 0.3 copy.43
  332.9 0.8 fusion.28
  333.8 48.4 %all_gather.22 = bf16[256,8,128]{2,1,0:T(8,128)(2,1)S(1)} all-gather(bf16[8,8,128]{2,1,0:T(8,128)(2,1)S(1)} %get-tuple-element.4), channel_id=1, replica_groups=mesh['ab'=16,'cd'=32] {'cd'}, dimensions={0}, use_global_device_ids=true | all-gather | bytes 540672 | tf_op jit(solution)/shard_map/all_gather | solution.py:48
  382.4 0.4 copy.58
  382.8 24.1 %all_gather.23 = bf16[4,128,256]{2,1,0:T(8,128)(2,1)S(1)} all-gather(bf16[4,8,256]{2,1,0:T(8,128)(2,1)S(1)} %bitcast.74), channel_id=1, replica_groups=mesh['ab'=16,'cd'=32] {'ab'}, dimensions={1}, use_global_device_ids=true | all-gather | bytes 278528 | tf_op jit(solution)/shard_map/all_gather | solution.py:51
  406.9 1.4 fusion.13
  408.4 121.2 %reduce-scatter.5.cloned.1.call-done = f32[8,1024]{1,0:T(8,128)} async-done(((f32[256,1024]{1,0:T(8,128)}), f32[8,1024]{1,0:T(8,128)}) %reduce-scatter.5.cloned.1.call-update) | async-done | bytes 32784 | tf_op jit(solution)/shard_map/reduce_scatter | solution.py:53
  529.6 1.0 copy.46
  530.6 0.3 reshape.126
  530.9 14.0 %all_to_all.36 = f32[16,1,512]{2,1,0:T(1,128)S(1)} all-to-all(f32[16,1,512]{2,1,0:T(1,128)S(1)} %reshape.126), channel_id=1, replica_groups=mesh['ab'=16,'cd'=32] {'ab'}, dimensions={0} | all-to-all | bytes 65536 | tf_op jit(solution)/shard_map/all_to_all | solution.py:61
  544.8 0.7 reduce.1
  545.6 0.3 reshape.127
  545.9 0.3 copy.48
  546.4 1.5 fusion.24
  (24 shorter events, 1.5 us)
Async XLA Ops:
  7.2 85.8 %all-gather.5.cloned.1.call-start = ((), (), s32[]{:S(2)}) async-start(), calls=%async_computation.5 | async-start | bytes 2228224 | tf_op jit(solution)/shard_map/all_gather | solution.py:21
  8.9 180.4 %all-gather.3.cloned.1.call-start = ((), (), s32[]{:S(2)}) async-start(), calls=%async_computation.4 | async-start | bytes 4325376 | tf_op jit(solution)/shard_map/all_gather | solution.py:19
  9.6 305.1 %reduce-scatter.3.cloned.1.call-start = ((), (), s32[]{:S(2)}) async-start(), calls=%async_computation.6 | async-start | bytes 1081344 | tf_op jit(solution)/shard_map/reduce_scatter | solution.py:53
  196.9 2.2 copy-start.2
  196.9 126.3 %copy-start.3 = (f32[32]{0:T(128)S(1)}, f32[32]{0:T(128)}, u32[]{:S(2)}) copy-start(f32[32]{0:T(128)} %param.8) | copy-start | bytes 388
  196.9 136.0 %copy-start = (f32[8,8,128]{2,1,0:T(8,128)S(1)}, f32[8,8,128]{2,1,0:T(8,128)}, u32[]{:S(2)}) copy-start(f32[8,8,128]{2,1,0:T(8,128)} %param.7) | copy-start | bytes 98308
  196.9 136.0 %copy-start.1 = (f32[8,8,128]{2,1,0:T(8,128)S(1)}, f32[8,8,128]{2,1,0:T(8,128)}, u32[]{:S(2)}) copy-start(f32[8,8,128]{2,1,0:T(8,128)} %param.6) | copy-start | bytes 98308
  316.6 14.2 %all-to-all-start = ((f32[16,1,512]{2,1,0:T(1,128)}), f32[16,1,512]{2,1,0:T(1,128)S(1)}, u32[]{:S(2)}, u32[]{:S(2)}) async-start(f32[16,1,512]{2,1,0:T(1,128)} %reshape.124), calls=%async_computation.1 | async-start | bytes 65536 | tf_op jit(solution)/shard_map/all_to_all | solution.py:61
  323.2 206.4 %reduce-scatter.5.cloned.1.call-start = ((), (), s32[]{:S(2)}) async-start(), calls=%async_computation.7 | async-start | bytes 1081344 | tf_op jit(solution)/shard_map/reduce_scatter | solution.py:53
Sparse Core Ops, SparseCore 0:
  10.1 74.8 all-gather.4
  88.3 100.9 all-gather.2
  199.2 115.4 reduce-scatter.2
  408.5 121.0 reduce-scatter.4
where the time goes:
time: 560 us; the launch traced here: 554 us
  waiting for transfers between devices  341 us (61%)
  blocking collectives  168 us (30%)
  between operations  13.9 us (2%)
  matrix products  10.5 us (2%)
  local copies, waits for them, and re-layouts  8.95 us (2%)
  starting transfers between devices  6.75 us (1%)
    reduce_scatter x2, waiting for transfers between devices, local(): lax.psum_scatter(lax.dot_general(flat_amps, tiles, (((0,), (1,)), ((), ()...  237 us
    all_gather x2, blocking collectives, local(): every_row = lax.all_gather(rounded, 'cd', axis=0, tiled=True)  99.4 us
    all_gather x1, waiting for transfers between devices, local(): left_rows = lax.all_gather(factors, 'cd', axis=1, tiled=True)  96.3 us
    all_gather x2, blocking collectives, local(): gathered = lax.all_gather(own_block, 'ab', axis=1, tiled=True)  55.1 us
    all_to_all x1, blocking collectives, local(): lax.all_to_all(summed, 'ab', split_axis=2, concat_axis=1, tiled=True)  14 us
  transfers between devices with their start and end apart: 5, of which 4 were waited for; matrix products, arithmetic and copies ran while one was open for 0% of the time, Pallas kernels for 0%

commit v1 on v0

v1 whole, which is shorter than its diff:
```python
import jax
import jax.numpy as jnp
from jax import lax
from jax.experimental import pallas as pl
from jax.experimental.pallas import tpu as pltpu
from jax.sharding import Mesh, PartitionSpec as P

ITERS = 2
AB = ("y", "xl")
CD = ("z", "xh", "k")


def pair_layout(stacked, n_cd):
    count, rows, a_local, virtuals = stacked.shape
    width = virtuals // n_cd
    split = stacked.reshape(count, rows, a_local, n_cd, width).transpose(3, 0, 4, 2, 1)
    swapped = lax.all_to_all(split.reshape(n_cd, -1), CD, 0, 0, tiled=True)
    swapped = swapped.reshape(n_cd, count, width * a_local, rows).transpose(1, 2, 0, 3)
    return swapped.reshape(count, width * a_local, n_cd * rows)


def spread(block, n_ab):
    copies = jnp.broadcast_to(block[None], (n_ab,) + block.shape)
    return lax.all_to_all(copies, AB, 0, 0, tiled=True).reshape(-1, block.shape[1])


LANES = 128


def tile_kernel(left_ref, piece_ref, inward_ref, tiles_ref, message_ref, gram_ref, tile_ref, sum_ref):
    n_z, n_k, n_xh, block, aux_width = left_ref.shape
    a_local = 8
    rows = n_z * n_k * n_xh * block
    d_local = piece_ref.shape[0] // LANES
    left = jnp.concatenate(
        [left_ref[z, k, xh] for z in range(n_z) for xh in range(n_xh) for k in range(n_k)], axis=0
    )
    for d in range(d_local):
        gram_ref[d] = lax.dot_general(
            left,
            piece_ref[d * LANES : (d + 1) * LANES, :],
            (((1,), (1,)), ((), ())),
            preferred_element_type=jnp.float32,
        )
    groups = rows // (a_local * 8)
    for a in range(a_local):
        for d in range(d_local):
            part = gram_ref[d, pl.ds(a, rows // a_local, stride=a_local), :]
            tile_ref[:, d, :, a * LANES : (a + 1) * LANES] = part.reshape(groups, 8, LANES)
    tiles = tile_ref[...].reshape(groups * d_local * 8, a_local * LANES).astype(jnp.bfloat16)
    tiles_ref[...] = tiles
    first = pl.program_id(0) == 0
    for half in range(2):
        lanes = inward_ref[:, half * LANES : (half + 1) * LANES]
        for a in range(a_local):
            out = lax.dot_general(
                tiles[:, a * LANES : (a + 1) * LANES],
                lanes,
                (((0,), (0,)), ((), ())),
                preferred_element_type=jnp.float32,
            )
            at = pl.ds(a, LANES, stride=a_local)
            before = sum_ref[half, at, :]
            sum_ref[half, at, :] = jnp.where(first, out, before + out)
        message_ref[:, half * LANES : (half + 1) * LANES] = sum_ref[half].astype(jnp.bfloat16)


def tiles_and_ladder(left, piece, inward):
    n_z, n_k, n_xh, block, aux_width = left.shape
    steps = 2
    contracted = inward.shape[0]
    wide = 8 * LANES
    part = contracted // steps
    d_local = piece.shape[0] // LANES
    return pl.pallas_call(
        tile_kernel,
        grid=(steps,),
        in_specs=[
            pl.BlockSpec((n_z // steps, n_k, n_xh, block, aux_width), lambda s: (s, 0, 0, 0, 0)),
            pl.BlockSpec(piece.shape, lambda s: (0, 0)),
            pl.BlockSpec((part, inward.shape[1]), lambda s: (s, 0)),
        ],
        out_specs=[
            pl.BlockSpec((part, wide), lambda s: (s, 0)),
            pl.BlockSpec((wide, inward.shape[1]), lambda s: (0, 0)),
        ],
        out_shape=[
            jax.ShapeDtypeStruct((contracted, wide), jnp.bfloat16),
            jax.ShapeDtypeStruct((wide, inward.shape[1]), jnp.bfloat16),
        ],
        scratch_shapes=[
            pltpu.VMEM((d_local, 2 * part, LANES), jnp.float32),
            pltpu.VMEM((part // (8 * d_local), d_local, 8, wide), jnp.float32),
            pltpu.VMEM((2, wide, LANES), jnp.float32),
        ],
        name="tiles_and_ladder",
    )(left, piece, inward)


def local(factors, amplitudes, driving, occ_energy, vir_energy):
    rows, a_local, virtuals = amplitudes.shape
    d_local, aux_width = factors.shape[1:]
    n_z, n_xh, n_k = (lax.axis_size(name) for name in CD)
    n_ab, n_cd = virtuals // a_local, virtuals // d_local
    pairs = rows * n_cd
    cd_index = lax.axis_index(CD)
    ab_index = lax.axis_index(AB)

    turned = factors.transpose(1, 0, 2)
    heads = lax.all_gather(turned[None], "xl", axis=0, tiled=True)
    piece = lax.all_gather(heads, "y", axis=0, tiled=True)
    columns = lax.all_gather(turned[None], "xh", axis=0, tiled=True)
    left = lax.all_gather(columns[None], ("z", "k"), axis=0, tiled=True)
    left = left.reshape(n_z, n_k, n_xh, d_local * a_local, aux_width)
    piece = piece.transpose(1, 0, 2, 3).reshape(d_local * virtuals, aux_width)

    n_occ = occ_energy.shape[0]
    occ_pairs = (occ_energy[: pairs // n_occ, None] + occ_energy[None, :]).reshape(pairs)
    occ_rows = lax.dynamic_slice_in_dim(occ_pairs, cd_index * rows, rows)
    vir_a = lax.dynamic_slice_in_dim(vir_energy, ab_index * a_local, a_local)
    vir_d = lax.dynamic_slice_in_dim(vir_energy, cd_index * d_local, d_local)
    denom_rows = vir_a[None, :, None] + vir_energy[None, None, :] - occ_rows[:, None, None]
    vir_block = (vir_d[:, None] + vir_a[None, :]).reshape(-1, 1)
    denom_block = vir_block - occ_pairs[None, :]

    rounded = amplitudes.astype(jnp.bfloat16).astype(jnp.float32)
    both = jnp.stack([amplitudes, driving])
    mirror = lax.all_to_all(both, AB, split_axis=3, concat_axis=2, tiled=True).transpose(0, 1, 3, 2)
    even = 0.5 * (both + mirror)
    even_rounded = 0.5 * (rounded + mirror[0].astype(jnp.bfloat16).astype(jnp.float32))
    blocks = pair_layout(jnp.concatenate([even, even_rounded[None]]), n_cd)
    current, drive = blocks[0], blocks[1]
    inward = spread(blocks[2].astype(jnp.bfloat16), n_ab)

    tiles, first = tiles_and_ladder(left, piece, inward)
    parts = lax.all_to_all(first.reshape(n_cd, -1, pairs), CD, 0, 0, tiled=True)
    ladder = jnp.sum(parts.astype(jnp.float32), axis=0)
    current = current - (drive + denom_block * current + ladder) / denom_block

    inward = spread(current.astype(jnp.bfloat16), n_ab)
    second = lax.dot_general(
        inward, tiles, (((0,), (0,)), ((), ())), preferred_element_type=jnp.float32
    ).astype(jnp.bfloat16)
    high = ladder.astype(jnp.bfloat16)
    low = (ladder - high.astype(jnp.float32)).astype(jnp.bfloat16)
    extra = jnp.stack([high, low]).reshape(2 * ladder.shape[0], n_cd, rows).transpose(1, 2, 0)
    message = jnp.concatenate([second.reshape(n_cd, rows, -1), extra], axis=2)
    parts = lax.all_to_all(message, CD, 0, 0, tiled=True)
    wide = virtuals * a_local
    ladder_second = jnp.sum(parts[:, :, :wide].astype(jnp.float32), axis=0)
    ladder_second = ladder_second.reshape(rows, a_local, virtuals)
    ladder_first = parts[:, :, wide:].astype(jnp.float32).reshape(n_cd, rows, 2, d_local, a_local)
    ladder_first = jnp.sum(ladder_first, axis=2).transpose(1, 3, 0, 2).reshape(rows, a_local, virtuals)

    current = amplitudes - (driving + denom_rows * amplitudes + ladder_first) / denom_rows
    residual = driving + denom_rows * current + ladder_second
    return (current - residual / denom_rows, residual)


def solution(mesh):
    fine = Mesh(mesh.devices.reshape(8, 2, 8, 2, 2), AB + CD)
    placed = (P(AB, CD, None), P(CD, AB, None), P(CD, AB, None), P(), P())
    return jax.shard_map(
        local,
        mesh=fine,
        in_specs=placed,
        out_specs=(P(CD, AB, None), P(CD, AB, None)),
        check_vma=False,
    )
```

time: 560 us -> 200 us (0.36)
  waiting for transfers between devices: 341 us -> 69.9 us
  blocking collectives: 168 us -> 69.9 us
  starting transfers between devices: 6.75 us -> 22.1 us
  matrix products: 10.5 us -> 0.45 us
  Pallas kernels: 0 us -> 9.74 us
    reduce_scatter x2 -> x0, waiting for transfers between devices: 237 us -> none  [local(): lax.psum_scatter(lax.dot_general(flat_amps, tiles, (((0,), (1,)), ((), ()...]
    all_gather x4 -> x2, blocking collectives: 154 us -> 11.7 us  [the longest x1 6.67 us: local(): columns = lax.all_gather(turned[None], 'xh', axis=0, tiled=True)]
    all_gather x2, waiting for transfers between devices: 96.3 us -> 25.7 us  [the longest x1 25.7 us: local(): left = lax.all_gather(columns[None], ('z', 'k'), axis=0, tiled=True)]
    all_to_all x1 -> x3, blocking collectives: 14 us -> 58.1 us  [the longest x1 27.6 us: pair_layout(): swapped = lax.all_to_all(split.reshape(n_cd, -1), CD, 0, 0, tiled=True)]
    all_to_all x1 -> x3, waiting for transfers between devices: 7.38 us -> 44.1 us  [the longest x1 18.3 us: local(): parts = lax.all_to_all(message, CD, 0, 0, tiled=True)]
    all_to_all x1 -> x3, starting transfers between devices: 6.59 us -> 22 us  [the longest x1 8.49 us: local(): parts = lax.all_to_all(message, CD, 0, 0, tiled=True)]
    dot_general x3 -> x1, matrix products: 10.5 us -> 0.45 us  [local(): lax.dot_general(inward, tiles, (((0,), (0,)), ((), ())), preferred_elemen...]
    pallas_call x0 -> x1, Pallas kernels: none -> 9.74 us  [tiles_and_ladder(): pl.pallas_call(tile_kernel, grid=(steps,), in_specs=[pl.BlockSpec((n_z //...]
  transfers between devices with their start and end apart: 5 -> 5, of which waited for: 4 -> 4; matrix products, arithmetic and copies ran while one was open for 0% -> 4% of each run, Pallas kernels for 0% -> 0%
where the time goes in v1:
time: 200 us; the launch traced here: 199 us
  blocking collectives  69.9 us (35%)
  waiting for transfers between devices  69.9 us (35%)
  starting transfers between devices  22.1 us (11%)
  between operations  14.3 us (7%)
  local copies, waits for them, and re-layouts  9.8 us (5%)
  Pallas kernels  9.74 us (5%)
  other arithmetic  2.96 us (1%)
    all_to_all x1, blocking collectives, pair_layout(): swapped = lax.all_to_all(split.reshape(n_cd, -1), CD, 0, 0, tiled=True)  27.6 us
    all_gather x1, waiting for transfers between devices, local(): left = lax.all_gather(columns[None], ('z', 'k'), axis=0, tiled=True)  25.7 us
    all_to_all x1, waiting for transfers between devices, local(): parts = lax.all_to_all(message, CD, 0, 0, tiled=True)  18.3 us
    all_to_all x1, waiting for transfers between devices, local(): parts = lax.all_to_all(first.reshape(n_cd, -1, pairs), CD, 0, 0, tiled=True)  15.9 us
    all_to_all x1, blocking collectives, local(): lax.all_to_all(both, AB, split_axis=3, concat_axis=2, tiled=True)  15.8 us
    all_to_all x1, blocking collectives, spread(): lax.all_to_all(copies, AB, 0, 0, tiled=True).reshape(-1, block.shape[1])  14.8 us
    all_to_all x1, waiting for transfers between devices, spread(): lax.all_to_all(copies, AB, 0, 0, tiled=True).reshape(-1, block.shape[1])  9.92 us
    pallas_call x1, Pallas kernels, tiles_and_ladder(): pl.pallas_call(tile_kernel, grid=(steps,), in_specs=[pl.BlockSpec((n_z //...  9.74 us
  transfers between devices with their start and end apart: 5, of which 4 were waited for; matrix products, arithmetic and copies ran while one was open for 4% of the time, Pallas kernels for 0%

profile of v1, /device:TPU:1, one launch (start us, length us, event | category | flops | bytes accessed | tf_op | source)
XLA Modules:
  0.0 199.1 jit_solution(16244199352686422465)
XLA Ops:
  7.2 1.0 copy.113
  8.2 5.0 %all-gather.2 = bf16[8,8,2048]{2,1,0:T(8,128)(2,1)S(1)} all-gather(bf16[4,8,2048]{2,1,0:T(8,128)(2,1)S(1)} %bitcast.74), channel_id=4, replica_groups=mesh['y'=8,'xl'=2,'z'=8,'xh'=2,'k'=2] {'xl'}, dimensions={0}, use_global_device_ids=true | all-gather | bytes 393216 | tf_op jit(solution)/shard_map/all_gather | solution.py:110
  13.3 0.7 copy.98
  14.0 6.7 %all-gather = bf16[8,8,2048]{2,1,0:T(8,128)(2,1)} all-gather(bf16[4,8,2048]{2,1,0:T(8,128)(2,1)S(1)} %bitcast.75), channel_id=2, replica_groups=mesh['y'=8,'xl'=2,'z'=8,'xh'=2,'k'=2] {'xh'}, dimensions={0}, use_global_device_ids=true | all-gather | bytes 393216 | tf_op jit(solution)/shard_map/all_gather | solution.py:112
  20.8 0.5 copy.83
  21.3 0.5 reshape.219
  21.8 15.8 %all_to_all.47 = f32[16,1,1024]{2,1,0:T(1,128)S(1)} all-to-all(f32[16,1,1024]{2,1,0:T(1,128)S(1)} %reshape.219), channel_id=1, replica_groups=mesh['y'=8,'xl'=2,'z'=8,'xh'=2,'k'=2] {'y','xl'}, dimensions={0} | all-to-all | bytes 131072 | tf_op jit(solution)/shard_map/all_to_all | solution.py:128
  37.6 0.5 broadcast.56
  38.1 0.8 reduce
  38.9 0.6 reshape.220
  39.5 0.6 copy.85
  40.1 0.5 all_to_all.34
  40.6 0.2 copy.87
  40.9 0.3 copy.89
  41.2 0.4 copy.86
  41.6 0.6 copy.88
  42.2 0.2 copy.90
  42.6 27.6 %all_to_all.48 = f32[32,1,768]{2,1,0:T(1,128)S(1)} all-to-all(f32[32,1,768]{2,1,0:T(1,128)S(1)} %copy.91), channel_id=1, replica_groups=mesh['y'=8,'xl'=2,'z'=8,'xh'=2,'k'=2] {'z','xh','k'}, dimensions={0} | all-to-all | bytes 196608 | tf_op jit(solution)/shard_map/all_to_all | solution.py:17
  70.6 14.8 %all_to_all.49 = bf16[16,32,256]{2,1,0:T(8,128)(2,1)} all-to-all(bf16[16,32,256]{2,1,0:T(8,128)(2,1)S(1)} %broadcast_in_dim.10), channel_id=1, replica_groups=mesh['y'=8,'xl'=2,'z'=8,'xh'=2,'k'=2] {'y','xl'}, dimensions={0} | all-to-all | bytes 524288 | tf_op jit(solution)/shard_map/all_to_all | solution.py:24
  85.4 25.7 %all-gather.8.cloned.1.call-done = bf16[32,4,8,2048]{3,2,1,0:T(8,128)(2,1)} async-done(((bf16[2,4,8,2048]{3,2,1,0:T(8,128)(2,1)}), bf16[32,4,8,2048]{3,2,1,0:T(8,128)(2,1)}) %all-gather.8.cloned.1.call-update) | async-done | bytes 4194320 | tf_op jit(solution)/shard_map/all_gather | solution.py:113
  111.1 9.7 %tiles_and_ladder.1 = (bf16[512,1024]{1,0:T(8,128)(2,1)}, bf16[1024,256]{1,0:T(8,128)(2,1)}) custom-call(bf16[8,2,2,32,2048]{4,3,2,1,0:T(8,128)(2,1)} %bitcast.65, bf16[512,2048]{1,0:T(8,128)(2,1)} %bitcast.68, bf16[512,256]{1,0:T(8,128)(2,1)} %bitcast.77), custom_call_target="tpu_custom_call" | custom-call | tf_op jit(solution)/shard_map/tiles_and_ladder/pallas_call | solution.py:75
  120.8 7.0 %all-to-all-start.3 = ((bf16[32,32,256]{2,1,0:T(8,128)(2,1)}), bf16[32,32,256]{2,1,0:T(8,128)(2,1)S(1)}, u32[]{:S(2)}, u32[]{:S(2)}) async-start(bf16[32,32,256]{2,1,0:T(8,128)(2,1)} %bitcast.83), calls=%async_computation.3 | async-start | bytes 1048576 | tf_op jit(solution)/shard_map/all_to_all | solution.py:136
  128.7 15.9 %all-to-all-done.3 = bf16[32,32,256]{2,1,0:T(8,128)(2,1)S(1)} async-done(((bf16[32,32,256]{2,1,0:T(8,128)(2,1)}), bf16[32,32,256]{2,1,0:T(8,128)(2,1)S(1)}, u32[]{:S(2)}, u32[]{:S(2)}) %all-to-all-start.3) | async-done | bytes 524320 | tf_op jit(solution)/shard_map/all_to_all | solution.py:136
  144.8 0.7 broadcast_in_dim.11
  145.6 6.6 %all-to-all-start.4 = ((bf16[16,32,256]{2,1,0:T(8,128)(2,1)}), bf16[16,32,256]{2,1,0:T(8,128)(2,1)S(1)}, u32[]{:S(2)}, u32[]{:S(2)}) async-start(bf16[16,32,256]{2,1,0:T(8,128)(2,1)} %broadcast_in_dim.11), calls=%async_computation.4 | async-start | bytes 524288 | tf_op jit(solution)/shard_map/all_to_all | solution.py:24
  152.4 9.9 %all-to-all-done.4 = bf16[16,32,256]{2,1,0:T(8,128)(2,1)S(1)} async-done(((bf16[16,32,256]{2,1,0:T(8,128)(2,1)}), bf16[16,32,256]{2,1,0:T(8,128)(2,1)S(1)}, u32[]{:S(2)}, u32[]{:S(2)}) %all-to-all-start.4) | async-done | bytes 262176 | tf_op jit(solution)/shard_map/all_to_all | solution.py:24
  162.3 0.5 fusion
  162.8 0.9 pad_maximum_fusion
  163.7 8.5 %all-to-all-start.5 = ((bf16[32,8,1088]{2,1,0:T(8,128)(2,1)}), bf16[32,8,1088]{2,1,0:T(8,128)(2,1)S(1)}, u32[]{:S(2)}, u32[]{:S(2)}) async-start(bf16[32,8,1088]{2,1,0:T(8,128)(2,1)} %pad_maximum_fusion), calls=%async_computation.5 | async-start | bytes 1179648 | tf_op jit(solution)/shard_map/all_to_all | solution.py:148
  172.3 18.3 %all-to-all-done.5 = bf16[32,8,1088]{2,1,0:T(8,128)(2,1)S(1)} async-done(((bf16[32,8,1088]{2,1,0:T(8,128)(2,1)}), bf16[32,8,1088]{2,1,0:T(8,128)(2,1)S(1)}, u32[]{:S(2)}, u32[]{:S(2)}) %all-to-all-start.5) | async-done | bytes 557088 | tf_op jit(solution)/shard_map/all_to_all | solution.py:148
  190.8 0.5 copy.104
  191.5 0.7 fusion.9
  (49 shorter events, 2.6 us)
Async XLA Ops:
  7.2 13.6 %copy-start.1 = (f32[8,8,128]{2,1,0:T(8,128)S(1)}, f32[8,8,128]{2,1,0:T(8,128)}, u32[]{:S(2)}) copy-start(f32[8,8,128]{2,1,0:T(8,128)} %param.6) | copy-start | bytes 98308
  7.2 13.6 %copy-start.2 = (f32[8,8,128]{2,1,0:T(8,128)S(1)}, f32[8,8,128]{2,1,0:T(8,128)}, u32[]{:S(2)}) copy-start(f32[8,8,128]{2,1,0:T(8,128)} %param.7) | copy-start | bytes 98308
  7.2 78.2 %all-gather.6.cloned.1.call-start = ((), (), s32[]{:S(2)}) async-start(), calls=%async_computation.6 | async-start | bytes 2359296 | tf_op jit(solution)/shard_map/all_gather | solution.py:111
  14.0 97.1 %all-gather.8.cloned.1.call-start = ((), (), s32[]{:S(2)}) async-start(), calls=%async_computation.7 | async-start | bytes 4456448 | tf_op jit(solution)/shard_map/all_gather | solution.py:113
  111.1 16.7 %copy-start.4 = (f32[128]{0:T(128)S(1)}, f32[128]{0:T(128)}, u32[]{:S(2)}) copy-start(f32[128]{0:T(128)} %param.9) | copy-start | bytes 1540
  111.1 17.0 %copy-start.3 = (f32[32]{0:T(128)S(1)}, f32[32]{0:T(128)}, u32[]{:S(2)}) copy-start(f32[32]{0:T(128)} %param.8) | copy-start | bytes 388
  120.8 23.8 %all-to-all-start.3 = ((bf16[32,32,256]{2,1,0:T(8,128)(2,1)}), bf16[32,32,256]{2,1,0:T(8,128)(2,1)S(1)}, u32[]{:S(2)}, u32[]{:S(2)}) async-start(bf16[32,32,256]{2,1,0:T(8,128)(2,1)} %bitcast.83), calls=%async_computation.3 | async-start | bytes 1048576 | tf_op jit(solution)/shard_map/all_to_all | solution.py:136
  128.5 33.8 %copy-start = (bf16[512,1024]{1,0:T(8,128)(2,1)S(1)}, bf16[512,1024]{1,0:T(8,128)(2,1)}, u32[]{:S(2)}) copy-start(bf16[512,1024]{1,0:T(8,128)(2,1)} %get-tuple-element.5) | copy-start | bytes 3145732
  145.6 16.8 %all-to-all-start.4 = ((bf16[16,32,256]{2,1,0:T(8,128)(2,1)}), bf16[16,32,256]{2,1,0:T(8,128)(2,1)S(1)}, u32[]{:S(2)}, u32[]{:S(2)}) async-start(bf16[16,32,256]{2,1,0:T(8,128)(2,1)} %broadcast_in_dim.11), calls=%async_computation.4 | async-start | bytes 524288 | tf_op jit(solution)/shard_map/all_to_all | solution.py:24
  163.7 26.9 %all-to-all-start.5 = ((bf16[32,8,1088]{2,1,0:T(8,128)(2,1)}), bf16[32,8,1088]{2,1,0:T(8,128)(2,1)S(1)}, u32[]{:S(2)}, u32[]{:S(2)}) async-start(bf16[32,8,1088]{2,1,0:T(8,128)(2,1)} %pad_maximum_fusion), calls=%async_computation.5 | async-start | bytes 1179648 | tf_op jit(solution)/shard_map/all_to_all | solution.py:148
Sparse Core Ops, SparseCore 0:
  14.1 46.0 all-gather.5
  62.3 48.7 all-gather.7

commit v2 on v1

--- a/solution.py
+++ b/solution.py
@@ -107,13 +107,10 @@
     ab_index = lax.axis_index(AB)
 
     turned = factors.transpose(1, 0, 2)
-    heads = lax.all_gather(turned[None], "xl", axis=0, tiled=True)
-    piece = lax.all_gather(heads, "y", axis=0, tiled=True)
     columns = lax.all_gather(turned[None], "xh", axis=0, tiled=True)
+    mine = lax.all_gather(turned[None], "y", axis=0, tiled=True)
     left = lax.all_gather(columns[None], ("z", "k"), axis=0, tiled=True)
     left = left.reshape(n_z, n_k, n_xh, d_local * a_local, aux_width)
-    piece = piece.transpose(1, 0, 2, 3).reshape(d_local * virtuals, aux_width)
-
     n_occ = occ_energy.shape[0]
     occ_pairs = (occ_energy[: pairs // n_occ, None] + occ_energy[None, :]).reshape(pairs)
     occ_rows = lax.dynamic_slice_in_dim(occ_pairs, cd_index * rows, rows)
@@ -126,11 +123,17 @@
     rounded = amplitudes.astype(jnp.bfloat16).astype(jnp.float32)
     both = jnp.stack([amplitudes, driving])
     mirror = lax.all_to_all(both, AB, split_axis=3, concat_axis=2, tiled=True).transpose(0, 1, 3, 2)
-    even = 0.5 * (both + mirror)
-    even_rounded = 0.5 * (rounded + mirror[0].astype(jnp.bfloat16).astype(jnp.float32))
-    blocks = pair_layout(jnp.concatenate([even, even_rounded[None]]), n_cd)
+    rounded_mirror = mirror[0].astype(jnp.bfloat16).astype(jnp.float32)
+    even = 0.5 * jnp.stack([rounded + rounded_mirror, both[1] + mirror[1]])
+    theirs = lax.ppermute(lax.optimization_barrier((mine, even))[0], "xl", [(0, 1), (1, 0)])
+    even_member = lax.axis_index("xl") == 0
+    piece = jnp.stack(
+        [jnp.where(even_member, mine, theirs), jnp.where(even_member, theirs, mine)], axis=1
+    )
+    piece = piece.transpose(2, 0, 1, 3, 4).reshape(d_local * virtuals, aux_width)
+    blocks = pair_layout(even, n_cd)
     current, drive = blocks[0], blocks[1]
-    inward = spread(blocks[2].astype(jnp.bfloat16), n_ab)
+    inward = spread(current.astype(jnp.bfloat16), n_ab)
 
     tiles, first = tiles_and_ladder(left, piece, inward)
     parts = lax.all_to_all(first.reshape(n_cd, -1, pairs), CD, 0, 0, tiled=True)

time: 200 us -> 194 us (0.970)
  blocking collectives: 69.9 us -> 8.38 us
  starting transfers between devices: 22.1 us -> 51.6 us
  waiting for transfers between devices: 69.9 us -> 89 us
  local copies, waits for them, and re-layouts: 9.8 us -> 14.1 us
  other arithmetic: 2.96 us -> 5.42 us
    all_to_all x3 -> x0, blocking collectives: 58.1 us -> none  [the longest x1 27.6 us: pair_layout(): swapped = lax.all_to_all(split.reshape(n_cd, -1), CD, 0, 0, tiled=True)]
    all_gather x1, waiting for transfers between devices: 25.7 us -> 0.01 us  [local(): left = lax.all_gather(columns[None], ('z', 'k'), axis=0, tiled=True)]
    all_gather x1, waiting for transfers between devices: 0.01 us -> 24.5 us  [local(): mine = lax.all_gather(turned[None], 'y', axis=0, tiled=True)]
    all_to_all x0 -> x2, starting transfers between devices: none -> 22.9 us  [the longest x1 15.1 us: pair_layout(): swapped = lax.all_to_all(split.reshape(n_cd, -1), CD, 0, 0, tiled=True)]
    all_to_all x0 -> x2, waiting for transfers between devices: none -> 10.8 us  [the longest x1 10.8 us: pair_layout(): swapped = lax.all_to_all(split.reshape(n_cd, -1), CD, 0, 0, tiled=True)]
    all_to_all x1 -> x2, waiting for transfers between devices: 9.92 us -> 19.2 us  [spread(): lax.all_to_all(copies, AB, 0, 0, tiled=True).reshape(-1, block.shape[1])]
    all_gather x1 -> x0, blocking collectives: 5.04 us -> none  [local(): heads = lax.all_gather(turned[None], 'xl', axis=0, tiled=True)]
    all_to_all x1 -> x2, starting transfers between devices: 6.56 us -> 10.9 us  [spread(): lax.all_to_all(copies, AB, 0, 0, tiled=True).reshape(-1, block.shape[1])]
  transfers between devices with their start and end apart: 5 -> 9, of which waited for: 4 -> 6; matrix products, arithmetic and copies ran while one was open for 4% -> 7% of each run, Pallas kernels for 0% -> 0%
where the time goes in v2:
time: 194 us; the launch traced here: 193 us
  waiting for transfers between devices  89 us (46%)
  starting transfers between devices  51.6 us (27%)
  between operations  14.4 us (7%)
  local copies, waits for them, and re-layouts  14.1 us (7%)
  Pallas kernels  9.75 us (5%)
  blocking collectives  8.38 us (4%)
  other arithmetic  5.42 us (3%)
    all_gather x1, waiting for transfers between devices, local(): mine = lax.all_gather(turned[None], 'y', axis=0, tiled=True)  24.5 us
    all_to_all x2, waiting for transfers between devices, spread(): lax.all_to_all(copies, AB, 0, 0, tiled=True).reshape(-1, block.shape[1])  19.2 us
    all_to_all x1, waiting for transfers between devices, local(): parts = lax.all_to_all(message, CD, 0, 0, tiled=True)  18.3 us
    all_to_all x1, waiting for transfers between devices, local(): parts = lax.all_to_all(first.reshape(n_cd, -1, pairs), CD, 0, 0, tiled=True)  16.1 us
    all_to_all x1, starting transfers between devices, pair_layout(): swapped = lax.all_to_all(split.reshape(n_cd, -1), CD, 0, 0, tiled=True)  15.1 us
    all_to_all x2, starting transfers between devices, spread(): lax.all_to_all(copies, AB, 0, 0, tiled=True).reshape(-1, block.shape[1])  10.9 us
    all_to_all x1, waiting for transfers between devices, pair_layout(): swapped = lax.all_to_all(split.reshape(n_cd, -1), CD, 0, 0, tiled=True)  10.8 us
    pallas_call x1, Pallas kernels, tiles_and_ladder(): pl.pallas_call(tile_kernel, grid=(steps,), in_specs=[pl.BlockSpec((n_z //...  9.75 us
  transfers between devices with their start and end apart: 9, of which 6 were waited for; matrix products, arithmetic and copies ran while one was open for 7% of the time, Pallas kernels for 0%

profile of v2, /device:TPU:1, one launch (start us, length us, event | category | flops | bytes accessed | tf_op | source)
XLA Modules:
  0.0 193.0 jit_solution(15877773434496909095)
XLA Ops:
  7.2 1.6 copy.160
  8.9 8.4 %all-gather = bf16[8,8,2048]{2,1,0:T(8,128)(2,1)} all-gather(bf16[4,8,2048]{2,1,0:T(8,128)(2,1)} %bitcast.84), channel_id=2, replica_groups=mesh['y'=8,'xl'=2,'z'=8,'xh'=2,'k'=2] {'xh'}, dimensions={0}, use_global_device_ids=true | all-gather | bytes 393216 | tf_op jit(solution)/shard_map/all_gather | solution.py:110
  17.3 0.8 pad_maximum_fusion.2
  18.1 0.5 copy.126
  18.6 1.1 reshape.217
  19.7 7.8 %all-to-all-start = ((f32[16,1,1024]{2,1,0:T(1,128)}), f32[16,1,1024]{2,1,0:T(1,128)S(1)}, u32[]{:S(2)}, u32[]{:S(2)}) async-start(f32[16,1,1024]{2,1,0:T(1,128)} %reshape.217), calls=%async_computation | async-start | bytes 131072 | tf_op jit(solution)/shard_map/all_to_all | solution.py:125
  27.5 24.5 %all-gather.8.cloned.1.call-done = bf16[32,8,2048]{2,1,0:T(8,128)(2,1)} async-done(((bf16[4,8,2048]{2,1,0:T(8,128)(2,1)}), bf16[32,8,2048]{2,1,0:T(8,128)(2,1)}) %all-gather.8.cloned.1.call-update) | async-done | bytes 1048592 | tf_op jit(solution)/shard_map/all_gather | solution.py:111
  52.1 2.3 %copy.141 = bf16[8,4,8,2048]{3,2,0,1:T(8,128)(2,1)} copy(bf16[8,4,8,2048]{3,2,1,0:T(8,128)(2,1)} %bitcast.74) | data formatting | bytes 2097152 | tf_op jit(solution)/shard_map/optimization_barrier | solution.py:128
  54.4 3.0 %collective-permute-start = (bf16[8,4,8,2048]{3,2,0,1:T(8,128)(2,1)}, bf16[8,4,8,2048]{3,2,0,1:T(8,128)(2,1)S(1)}, u32[]{:S(2)}, u32[]{:S(2)}) collective-permute-start(bf16[8,4,8,2048]{3,2,0,1:T(8,128)(2,1)} %copy.141), channel_id=1, source_target_pairs={{0,32},{32,0},{1,33},{33,1},{2,34},{34,2},{3,35},{35,3},{4,36},{36... | collective-permute-start | bytes 3145736 | tf_op jit(solution)/shard_map/ppermute | solution.py:128
  57.4 0.5 broadcast.57
  57.9 0.8 reduce
  58.7 0.6 reshape.218
  59.3 0.6 copy.128
  60.0 0.5 all_to_all.34
  61.8 0.7 copy.134
  62.6 15.1 %all-to-all-start.1 = ((f32[32,1,512]{2,1,0:T(1,128)}), f32[32,1,512]{2,1,0:T(1,128)S(1)}, u32[]{:S(2)}, u32[]{:S(2)}) async-start(f32[32,1,512]{2,1,0:T(1,128)} %copy.134), calls=%async_computation.1 | async-start | bytes 131072 | tf_op jit(solution)/shard_map/all_to_all | solution.py:17
  77.6 10.8 %all-to-all-done.1 = f32[32,1,512]{2,1,0:T(1,128)S(1)} async-done(((f32[32,1,512]{2,1,0:T(1,128)}), f32[32,1,512]{2,1,0:T(1,128)S(1)}, u32[]{:S(2)}, u32[]{:S(2)}) %all-to-all-start.1) | async-done | bytes 65568 | tf_op jit(solution)/shard_map/all_to_all | solution.py:17
  88.9 0.8 broadcast_in_dim.10
  89.6 4.4 %all-to-all-start.2 = ((bf16[16,32,256]{2,1,0:T(8,128)(2,1)}), bf16[16,32,256]{2,1,0:T(8,128)(2,1)S(1)}, u32[]{:S(2)}, u32[]{:S(2)}) async-start(bf16[16,32,256]{2,1,0:T(8,128)(2,1)} %broadcast_in_dim.10), calls=%async_computation.2 | async-start | bytes 524288 | tf_op jit(solution)/shard_map/all_to_all | solution.py:24
  94.2 1.5 pad_maximum_fusion
  95.8 9.3 %all-to-all-done.2 = bf16[16,32,256]{2,1,0:T(8,128)(2,1)S(1)} async-done(((bf16[16,32,256]{2,1,0:T(8,128)(2,1)}), bf16[16,32,256]{2,1,0:T(8,128)(2,1)S(1)}, u32[]{:S(2)}, u32[]{:S(2)}) %all-to-all-start.2) | async-done | bytes 262176 | tf_op jit(solution)/shard_map/all_to_all | solution.py:24
  105.1 0.7 copy-done.2
  105.8 9.7 %tiles_and_ladder.1 = (bf16[512,1024]{1,0:T(8,128)(2,1)}, bf16[1024,256]{1,0:T(8,128)(2,1)}) custom-call(bf16[8,2,2,32,2048]{4,3,2,1,0:T(8,128)(2,1)} %bitcast.76, bf16[512,2048]{1,0:T(8,128)(2,1)} %bitcast.73, bf16[512,256]{1,0:T(8,128)(2,1)} %bitcast.85), custom_call_target="tpu_custom_call" | custom-call | tf_op jit(solution)/shard_map/tiles_and_ladder/pallas_call | solution.py:75
  115.6 6.3 %all-to-all-start.3 = ((bf16[32,32,256]{2,1,0:T(8,128)(2,1)}), bf16[32,32,256]{2,1,0:T(8,128)(2,1)S(1)}, u32[]{:S(2)}, u32[]{:S(2)}) async-start(bf16[32,32,256]{2,1,0:T(8,128)(2,1)} %bitcast.92), calls=%async_computation.3 | async-start | bytes 1048576 | tf_op jit(solution)/shard_map/all_to_all | solution.py:139
  122.6 16.1 %all-to-all-done.3 = bf16[32,32,256]{2,1,0:T(8,128)(2,1)S(1)} async-done(((bf16[32,32,256]{2,1,0:T(8,128)(2,1)}), bf16[32,32,256]{2,1,0:T(8,128)(2,1)S(1)}, u32[]{:S(2)}, u32[]{:S(2)}) %all-to-all-start.3) | async-done | bytes 524320 | tf_op jit(solution)/shard_map/all_to_all | solution.py:139
  138.9 0.7 broadcast_in_dim.11
  139.6 6.5 %all-to-all-start.4 = ((bf16[16,32,256]{2,1,0:T(8,128)(2,1)}), bf16[16,32,256]{2,1,0:T(8,128)(2,1)S(1)}, u32[]{:S(2)}, u32[]{:S(2)}) async-start(bf16[16,32,256]{2,1,0:T(8,128)(2,1)} %broadcast_in_dim.11), calls=%async_computation.4 | async-start | bytes 524288 | tf_op jit(solution)/shard_map/all_to_all | solution.py:24
  146.3 9.9 %all-to-all-done.4 = bf16[16,32,256]{2,1,0:T(8,128)(2,1)S(1)} async-done(((bf16[16,32,256]{2,1,0:T(8,128)(2,1)}), bf16[16,32,256]{2,1,0:T(8,128)(2,1)S(1)}, u32[]{:S(2)}, u32[]{:S(2)}) %all-to-all-start.4) | async-done | bytes 262176 | tf_op jit(solution)/shard_map/all_to_all | solution.py:24
  156.7 0.9 pad_maximum_fusion.1
  157.6 8.5 %all-to-all-start.5 = ((bf16[32,8,1088]{2,1,0:T(8,128)(2,1)}), bf16[32,8,1088]{2,1,0:T(8,128)(2,1)S(1)}, u32[]{:S(2)}, u32[]{:S(2)}) async-start(bf16[32,8,1088]{2,1,0:T(8,128)(2,1)} %pad_maximum_fusion.1), calls=%async_computation.5 | async-start | bytes 1179648 | tf_op jit(solution)/shard_map/all_to_all | solution.py:151
  166.2 18.3 %all-to-all-done.5 = bf16[32,8,1088]{2,1,0:T(8,128)(2,1)S(1)} async-done(((bf16[32,8,1088]{2,1,0:T(8,128)(2,1)}), bf16[32,8,1088]{2,1,0:T(8,128)(2,1)S(1)}, u32[]{:S(2)}, u32[]{:S(2)}) %all-to-all-start.5) | async-done | bytes 557088 | tf_op jit(solution)/shard_map/all_to_all | solution.py:151
  185.5 0.7 fusion.10
  (57 shorter events, 4.6 us)
Async XLA Ops:
  7.2 44.9 %all-gather.8.cloned.1.call-start = ((), (), s32[]{:S(2)}) async-start(), calls=%async_computation.7 | async-start | bytes 1179648 | tf_op jit(solution)/shard_map/all_gather | solution.py:111
  8.9 96.2 %all-gather.6.cloned.1.call-start = ((), (), s32[]{:S(2)}) async-start(), calls=%async_computation.6 | async-start | bytes 4456448 | tf_op jit(solution)/shard_map/all_gather | solution.py:112
  19.7 37.7 %all-to-all-start = ((f32[16,1,1024]{2,1,0:T(1,128)}), f32[16,1,1024]{2,1,0:T(1,128)S(1)}, u32[]{:S(2)}, u32[]{:S(2)}) async-start(f32[16,1,1024]{2,1,0:T(1,128)} %reshape.217), calls=%async_computation | async-start | bytes 131072 | tf_op jit(solution)/shard_map/all_to_all | solution.py:125
  54.4 39.7 %collective-permute-start = (bf16[8,4,8,2048]{3,2,0,1:T(8,128)(2,1)}, bf16[8,4,8,2048]{3,2,0,1:T(8,128)(2,1)S(1)}, u32[]{:S(2)}, u32[]{:S(2)}) collective-permute-start(bf16[8,4,8,2048]{3,2,0,1:T(8,128)(2,1)} %copy.141), channel_id=1, source_target_pairs={{0,32},{32,0},{1,33},{33,1},{2,34},{34,2},{3,35},{35,3},{4,36},{36... | collective-permute-start | bytes 3145736 | tf_op jit(solution)/shard_map/ppermute | solution.py:128
  58.7 1.7 copy-start.3
  58.7 1.7 copy-start.4
  61.3 32.8 %copy-start = (bf16[32,8,2048]{2,1,0:T(8,128)(2,1)S(1)}, bf16[32,8,2048]{2,1,0:T(8,128)(2,1)}, u32[]{:S(2)}) copy-start(bf16[32,8,2048]{2,1,0:T(8,128)(2,1)} %all-gather.8.cloned.1.call-done) | copy-start | bytes 3145732
  62.6 25.9 %all-to-all-start.1 = ((f32[32,1,512]{2,1,0:T(1,128)}), f32[32,1,512]{2,1,0:T(1,128)S(1)}, u32[]{:S(2)}, u32[]{:S(2)}) async-start(f32[32,1,512]{2,1,0:T(1,128)} %copy.134), calls=%async_computation.1 | async-start | bytes 131072 | tf_op jit(solution)/shard_map/all_to_all | solution.py:17
  89.6 15.4 %all-to-all-start.2 = ((bf16[16,32,256]{2,1,0:T(8,128)(2,1)}), bf16[16,32,256]{2,1,0:T(8,128)(2,1)S(1)}, u32[]{:S(2)}, u32[]{:S(2)}) async-start(bf16[16,32,256]{2,1,0:T(8,128)(2,1)} %broadcast_in_dim.10), calls=%async_computation.2 | async-start | bytes 524288 | tf_op jit(solution)/shard_map/all_to_all | solution.py:24
  105.1 0.7 copy-start.2
  105.8 16.0 %copy-start.6 = (f32[128]{0:T(128)S(1)}, f32[128]{0:T(128)}, u32[]{:S(2)}) copy-start(f32[128]{0:T(128)} %param.9) | copy-start | bytes 1540
  105.8 16.4 %copy-start.5 = (f32[32]{0:T(128)S(1)}, f32[32]{0:T(128)}, u32[]{:S(2)}) copy-start(f32[32]{0:T(128)} %param.8) | copy-start | bytes 388
  115.6 40.7 %copy-start.1 = (bf16[512,1024]{1,0:T(8,128)(2,1)S(1)}, bf16[512,1024]{1,0:T(8,128)(2,1)}, u32[]{:S(2)}) copy-start(bf16[512,1024]{1,0:T(8,128)(2,1)} %get-tuple-element.5) | copy-start | bytes 3145732
  115.6 23.1 %all-to-all-start.3 = ((bf16[32,32,256]{2,1,0:T(8,128)(2,1)}), bf16[32,32,256]{2,1,0:T(8,128)(2,1)S(1)}, u32[]{:S(2)}, u32[]{:S(2)}) async-start(bf16[32,32,256]{2,1,0:T(8,128)(2,1)} %bitcast.92), calls=%async_computation.3 | async-start | bytes 1048576 | tf_op jit(solution)/shard_map/all_to_all | solution.py:139
  139.6 16.7 %all-to-all-start.4 = ((bf16[16,32,256]{2,1,0:T(8,128)(2,1)}), bf16[16,32,256]{2,1,0:T(8,128)(2,1)S(1)}, u32[]{:S(2)}, u32[]{:S(2)}) async-start(bf16[16,32,256]{2,1,0:T(8,128)(2,1)} %broadcast_in_dim.11), calls=%async_computation.4 | async-start | bytes 524288 | tf_op jit(solution)/shard_map/all_to_all | solution.py:24
  157.6 26.9 %all-to-all-start.5 = ((bf16[32,8,1088]{2,1,0:T(8,128)(2,1)}), bf16[32,8,1088]{2,1,0:T(8,128)(2,1)S(1)}, u32[]{:S(2)}, u32[]{:S(2)}) async-start(bf16[32,8,1088]{2,1,0:T(8,128)(2,1)} %pad_maximum_fusion.1), calls=%async_computation.5 | async-start | bytes 1179648 | tf_op jit(solution)/shard_map/all_to_all | solution.py:151
Sparse Core Ops, SparseCore 0:
  10.0 41.9 all-gather.7
  54.2 50.0 all-gather.5

commit v3 on v2

--- a/solution.py
+++ b/solution.py
@@ -5,7 +5,7 @@
 from jax.experimental.pallas import tpu as pltpu
 from jax.sharding import Mesh, PartitionSpec as P
 
-ITERS = 2
+
 AB = ("y", "xl")
 CD = ("z", "xh", "k")
 
@@ -28,20 +28,18 @@
 
 
 def tile_kernel(left_ref, piece_ref, inward_ref, tiles_ref, message_ref, gram_ref, tile_ref, sum_ref):
-    n_z, n_k, n_xh, block, aux_width = left_ref.shape
+    n_z, n_k, n_xh, block, _ = left_ref.shape
     a_local = 8
     rows = n_z * n_k * n_xh * block
     d_local = piece_ref.shape[0] // LANES
     left = jnp.concatenate(
         [left_ref[z, k, xh] for z in range(n_z) for xh in range(n_xh) for k in range(n_k)], axis=0
     )
+    gram = lax.dot_general(
+        left, piece_ref[...], (((1,), (1,)), ((), ())), preferred_element_type=jnp.float32
+    )
     for d in range(d_local):
-        gram_ref[d] = lax.dot_general(
-            left,
-            piece_ref[d * LANES : (d + 1) * LANES, :],
-            (((1,), (1,)), ((), ())),
-            preferred_element_type=jnp.float32,
-        )
+        gram_ref[d] = gram[:, d * LANES : (d + 1) * LANES]
     groups = rows // (a_local * 8)
     for a in range(a_local):
         for d in range(d_local):
@@ -50,19 +48,17 @@
     tiles = tile_ref[...].reshape(groups * d_local * 8, a_local * LANES).astype(jnp.bfloat16)
     tiles_ref[...] = tiles
     first = pl.program_id(0) == 0
+    product = lax.dot_general(
+        tiles, inward_ref[...], (((0,), (0,)), ((), ())), preferred_element_type=jnp.float32
+    )
     for half in range(2):
-        lanes = inward_ref[:, half * LANES : (half + 1) * LANES]
+        lanes = slice(half * LANES, (half + 1) * LANES)
         for a in range(a_local):
-            out = lax.dot_general(
-                tiles[:, a * LANES : (a + 1) * LANES],
-                lanes,
-                (((0,), (0,)), ((), ())),
-                preferred_element_type=jnp.float32,
-            )
+            out = product[a * LANES : (a + 1) * LANES, lanes]
             at = pl.ds(a, LANES, stride=a_local)
             before = sum_ref[half, at, :]
             sum_ref[half, at, :] = jnp.where(first, out, before + out)
-        message_ref[:, half * LANES : (half + 1) * LANES] = sum_ref[half].astype(jnp.bfloat16)
+        message_ref[:, lanes] = sum_ref[half].astype(jnp.bfloat16)
 
 
 def tiles_and_ladder(left, piece, inward):
@@ -77,7 +73,7 @@
         grid=(steps,),
         in_specs=[
             pl.BlockSpec((n_z // steps, n_k, n_xh, block, aux_width), lambda s: (s, 0, 0, 0, 0)),
-            pl.BlockSpec(piece.shape, lambda s: (0, 0)),
+            pl.BlockSpec(memory_space=pltpu.VMEM),
             pl.BlockSpec((part, inward.shape[1]), lambda s: (s, 0)),
         ],
         out_specs=[
@@ -125,7 +121,7 @@
     mirror = lax.all_to_all(both, AB, split_axis=3, concat_axis=2, tiled=True).transpose(0, 1, 3, 2)
     rounded_mirror = mirror[0].astype(jnp.bfloat16).astype(jnp.float32)
     even = 0.5 * jnp.stack([rounded + rounded_mirror, both[1] + mirror[1]])
-    theirs = lax.ppermute(lax.optimization_barrier((mine, even))[0], "xl", [(0, 1), (1, 0)])
+    theirs = lax.ppermute(mine, "xl", [(0, 1), (1, 0)])
     even_member = lax.axis_index("xl") == 0
     piece = jnp.stack(
         [jnp.where(even_member, mine, theirs), jnp.where(even_member, theirs, mine)], axis=1

time: 194 us -> 192 us (0.990)
    all_gather x0 -> x1, local copies, waits for them, and re-layouts: none -> 2.34 us  [local(): mine = lax.all_gather(turned[None], 'y', axis=0, tiled=True)]
    optimization_barrier x1 -> x0, local copies, waits for them, and re-layouts: 2.34 us -> none  [local(): lax.optimization_barrier((mine, even))[0]]
where the time goes in v3:
time: 192 us; the launch traced here: 191 us
  waiting for transfers between devices  89 us (46%)
  starting transfers between devices  51.6 us (27%)
  between operations  14.4 us (8%)
  local copies, waits for them, and re-layouts  14.1 us (7%)
  blocking collectives  8.38 us (4%)
  Pallas kernels  7.9 us (4%)
  other arithmetic  5.42 us (3%)
    all_gather x1, waiting for transfers between devices, local(): mine = lax.all_gather(turned[None], 'y', axis=0, tiled=True)  24.5 us
    all_to_all x2, waiting for transfers between devices, spread(): lax.all_to_all(copies, AB, 0, 0, tiled=True).reshape(-1, block.shape[1])  19.2 us
    all_to_all x1, waiting for transfers between devices, local(): parts = lax.all_to_all(message, CD, 0, 0, tiled=True)  18.3 us
    all_to_all x1, waiting for transfers between devices, local(): parts = lax.all_to_all(first.reshape(n_cd, -1, pairs), CD, 0, 0, tiled=True)  16.1 us
    all_to_all x1, starting transfers between devices, pair_layout(): swapped = lax.all_to_all(split.reshape(n_cd, -1), CD, 0, 0, tiled=True)  15.1 us
    all_to_all x2, starting transfers between devices, spread(): lax.all_to_all(copies, AB, 0, 0, tiled=True).reshape(-1, block.shape[1])  10.9 us
    all_to_all x1, waiting for transfers between devices, pair_layout(): swapped = lax.all_to_all(split.reshape(n_cd, -1), CD, 0, 0, tiled=True)  10.8 us
    all_to_all x1, starting transfers between devices, local(): parts = lax.all_to_all(message, CD, 0, 0, tiled=True)  8.49 us
  transfers between devices with their start and end apart: 9, of which 6 were waited for; matrix products, arithmetic and copies ran while one was open for 7% of the time, Pallas kernels for 0%

profile of v3, /device:TPU:1, one launch (start us, length us, event | category | flops | bytes accessed | tf_op | source)
XLA Modules:
  0.0 191.2 jit_solution(1526771618757026994)
XLA Ops:
  7.2 1.6 copy.160
  8.9 8.4 %all-gather = bf16[8,8,2048]{2,1,0:T(8,128)(2,1)} all-gather(bf16[4,8,2048]{2,1,0:T(8,128)(2,1)} %bitcast.84), channel_id=2, replica_groups=mesh['y'=8,'xl'=2,'z'=8,'xh'=2,'k'=2] {'xh'}, dimensions={0}, use_global_device_ids=true | all-gather | bytes 393216 | tf_op jit(solution)/shard_map/all_gather | solution.py:106
  17.3 0.8 pad_maximum_fusion.2
  18.1 0.5 copy.126
  18.6 1.1 reshape.217
  19.7 7.8 %all-to-all-start = ((f32[16,1,1024]{2,1,0:T(1,128)}), f32[16,1,1024]{2,1,0:T(1,128)S(1)}, u32[]{:S(2)}, u32[]{:S(2)}) async-start(f32[16,1,1024]{2,1,0:T(1,128)} %reshape.217), calls=%async_computation | async-start | bytes 131072 | tf_op jit(solution)/shard_map/all_to_all | solution.py:121
  27.5 24.5 %all-gather.8.cloned.1.call-done = bf16[32,8,2048]{2,1,0:T(8,128)(2,1)} async-done(((bf16[4,8,2048]{2,1,0:T(8,128)(2,1)}), bf16[32,8,2048]{2,1,0:T(8,128)(2,1)}) %all-gather.8.cloned.1.call-update) | async-done | bytes 1048592 | tf_op jit(solution)/shard_map/all_gather | solution.py:107
  52.1 2.3 %copy.142 = bf16[8,4,8,2048]{3,2,0,1:T(8,128)(2,1)} copy(bf16[8,4,8,2048]{3,2,1,0:T(8,128)(2,1)} %bitcast.74) | data formatting | bytes 2097152 | tf_op jit(solution)/shard_map/all_gather | solution.py:107
  54.4 3.0 %collective-permute-start = (bf16[8,4,8,2048]{3,2,0,1:T(8,128)(2,1)}, bf16[8,4,8,2048]{3,2,0,1:T(8,128)(2,1)S(1)}, u32[]{:S(2)}, u32[]{:S(2)}) collective-permute-start(bf16[8,4,8,2048]{3,2,0,1:T(8,128)(2,1)} %copy.142), channel_id=1, source_target_pairs={{0,32},{32,0},{1,33},{33,1},{2,34},{34,2},{3,35},{35,3},{4,36},{36... | collective-permute-start | bytes 3145736 | tf_op jit(solution)/shard_map/ppermute | solution.py:124
  57.4 0.5 broadcast.57
  57.9 0.8 reduce
  58.7 0.6 reshape.218
  59.3 0.6 copy.128
  60.0 0.5 all_to_all.34
  61.8 0.7 copy.134
  62.6 15.1 %all-to-all-start.1 = ((f32[32,1,512]{2,1,0:T(1,128)}), f32[32,1,512]{2,1,0:T(1,128)S(1)}, u32[]{:S(2)}, u32[]{:S(2)}) async-start(f32[32,1,512]{2,1,0:T(1,128)} %copy.134), calls=%async_computation.1 | async-start | bytes 131072 | tf_op jit(solution)/shard_map/all_to_all | solution.py:17
  77.6 10.8 %all-to-all-done.1 = f32[32,1,512]{2,1,0:T(1,128)S(1)} async-done(((f32[32,1,512]{2,1,0:T(1,128)}), f32[32,1,512]{2,1,0:T(1,128)S(1)}, u32[]{:S(2)}, u32[]{:S(2)}) %all-to-all-start.1) | async-done | bytes 65568 | tf_op jit(solution)/shard_map/all_to_all | solution.py:17
  88.9 0.8 broadcast_in_dim.10
  89.6 4.4 %all-to-all-start.2 = ((bf16[16,32,256]{2,1,0:T(8,128)(2,1)}), bf16[16,32,256]{2,1,0:T(8,128)(2,1)S(1)}, u32[]{:S(2)}, u32[]{:S(2)}) async-start(bf16[16,32,256]{2,1,0:T(8,128)(2,1)} %broadcast_in_dim.10), calls=%async_computation.2 | async-start | bytes 524288 | tf_op jit(solution)/shard_map/all_to_all | solution.py:24
  94.2 1.5 pad_maximum_fusion
  95.8 9.3 %all-to-all-done.2 = bf16[16,32,256]{2,1,0:T(8,128)(2,1)S(1)} async-done(((bf16[16,32,256]{2,1,0:T(8,128)(2,1)}), bf16[16,32,256]{2,1,0:T(8,128)(2,1)S(1)}, u32[]{:S(2)}, u32[]{:S(2)}) %all-to-all-start.2) | async-done | bytes 262176 | tf_op jit(solution)/shard_map/all_to_all | solution.py:24
  105.1 0.7 copy-done.2
  105.8 7.9 %tiles_and_ladder.1 = (bf16[512,1024]{1,0:T(8,128)(2,1)}, bf16[1024,256]{1,0:T(8,128)(2,1)}) custom-call(bf16[8,2,2,32,2048]{4,3,2,1,0:T(8,128)(2,1)} %bitcast.76, bf16[512,2048]{1,0:T(8,128)(2,1)} %bitcast.73, bf16[512,256]{1,0:T(8,128)(2,1)} %bitcast.85), custom_call_target="tpu_custom_call" | custom-call | tf_op jit(solution)/shard_map/tiles_and_ladder/pallas_call | solution.py:71
  113.7 6.3 %all-to-all-start.3 = ((bf16[32,32,256]{2,1,0:T(8,128)(2,1)}), bf16[32,32,256]{2,1,0:T(8,128)(2,1)S(1)}, u32[]{:S(2)}, u32[]{:S(2)}) async-start(bf16[32,32,256]{2,1,0:T(8,128)(2,1)} %bitcast.92), calls=%async_computation.3 | async-start | bytes 1048576 | tf_op jit(solution)/shard_map/all_to_all | solution.py:135
  120.7 16.1 %all-to-all-done.3 = bf16[32,32,256]{2,1,0:T(8,128)(2,1)S(1)} async-done(((bf16[32,32,256]{2,1,0:T(8,128)(2,1)}), bf16[32,32,256]{2,1,0:T(8,128)(2,1)S(1)}, u32[]{:S(2)}, u32[]{:S(2)}) %all-to-all-start.3) | async-done | bytes 524320 | tf_op jit(solution)/shard_map/all_to_all | solution.py:135
  137.0 0.7 broadcast_in_dim.11
  137.7 6.5 %all-to-all-start.4 = ((bf16[16,32,256]{2,1,0:T(8,128)(2,1)}), bf16[16,32,256]{2,1,0:T(8,128)(2,1)S(1)}, u32[]{:S(2)}, u32[]{:S(2)}) async-start(bf16[16,32,256]{2,1,0:T(8,128)(2,1)} %broadcast_in_dim.11), calls=%async_computation.4 | async-start | bytes 524288 | tf_op jit(solution)/shard_map/all_to_all | solution.py:24
  144.5 9.9 %all-to-all-done.4 = bf16[16,32,256]{2,1,0:T(8,128)(2,1)S(1)} async-done(((bf16[16,32,256]{2,1,0:T(8,128)(2,1)}), bf16[16,32,256]{2,1,0:T(8,128)(2,1)S(1)}, u32[]{:S(2)}, u32[]{:S(2)}) %all-to-all-start.4) | async-done | bytes 262176 | tf_op jit(solution)/shard_map/all_to_all | solution.py:24
  154.9 0.9 pad_maximum_fusion.1
  155.7 8.5 %all-to-all-start.5 = ((bf16[32,8,1088]{2,1,0:T(8,128)(2,1)}), bf16[32,8,1088]{2,1,0:T(8,128)(2,1)S(1)}, u32[]{:S(2)}, u32[]{:S(2)}) async-start(bf16[32,8,1088]{2,1,0:T(8,128)(2,1)} %pad_maximum_fusion.1), calls=%async_computation.5 | async-start | bytes 1179648 | tf_op jit(solution)/shard_map/all_to_all | solution.py:147
  164.4 18.3 %all-to-all-done.5 = bf16[32,8,1088]{2,1,0:T(8,128)(2,1)S(1)} async-done(((bf16[32,8,1088]{2,1,0:T(8,128)(2,1)}), bf16[32,8,1088]{2,1,0:T(8,128)(2,1)S(1)}, u32[]{:S(2)}, u32[]{:S(2)}) %all-to-all-start.5) | async-done | bytes 557088 | tf_op jit(solution)/shard_map/all_to_all | solution.py:147
  183.6 0.7 fusion.10
  (57 shorter events, 4.6 us)
Async XLA Ops:
  7.2 44.9 %all-gather.8.cloned.1.call-start = ((), (), s32[]{:S(2)}) async-start(), calls=%async_computation.7 | async-start | bytes 1179648 | tf_op jit(solution)/shard_map/all_gather | solution.py:107
  8.9 96.2 %all-gather.6.cloned.1.call-start = ((), (), s32[]{:S(2)}) async-start(), calls=%async_computation.6 | async-start | bytes 4456448 | tf_op jit(solution)/shard_map/all_gather | solution.py:108
  19.7 37.7 %all-to-all-start = ((f32[16,1,1024]{2,1,0:T(1,128)}), f32[16,1,1024]{2,1,0:T(1,128)S(1)}, u32[]{:S(2)}, u32[]{:S(2)}) async-start(f32[16,1,1024]{2,1,0:T(1,128)} %reshape.217), calls=%async_computation | async-start | bytes 131072 | tf_op jit(solution)/shard_map/all_to_all | solution.py:121
  54.4 39.7 %collective-permute-start = (bf16[8,4,8,2048]{3,2,0,1:T(8,128)(2,1)}, bf16[8,4,8,2048]{3,2,0,1:T(8,128)(2,1)S(1)}, u32[]{:S(2)}, u32[]{:S(2)}) collective-permute-start(bf16[8,4,8,2048]{3,2,0,1:T(8,128)(2,1)} %copy.142), channel_id=1, source_target_pairs={{0,32},{32,0},{1,33},{33,1},{2,34},{34,2},{3,35},{35,3},{4,36},{36... | collective-permute-start | bytes 3145736 | tf_op jit(solution)/shard_map/ppermute | solution.py:124
  58.7 1.7 copy-start.3
  58.7 1.7 copy-start.4
  61.3 32.8 %copy-start = (bf16[32,8,2048]{2,1,0:T(8,128)(2,1)S(1)}, bf16[32,8,2048]{2,1,0:T(8,128)(2,1)}, u32[]{:S(2)}) copy-start(bf16[32,8,2048]{2,1,0:T(8,128)(2,1)} %all-gather.8.cloned.1.call-done) | copy-start | bytes 3145732
  62.6 25.9 %all-to-all-start.1 = ((f32[32,1,512]{2,1,0:T(1,128)}), f32[32,1,512]{2,1,0:T(1,128)S(1)}, u32[]{:S(2)}, u32[]{:S(2)}) async-start(f32[32,1,512]{2,1,0:T(1,128)} %copy.134), calls=%async_computation.1 | async-start | bytes 131072 | tf_op jit(solution)/shard_map/all_to_all | solution.py:17
  89.6 15.4 %all-to-all-start.2 = ((bf16[16,32,256]{2,1,0:T(8,128)(2,1)}), bf16[16,32,256]{2,1,0:T(8,128)(2,1)S(1)}, u32[]{:S(2)}, u32[]{:S(2)}) async-start(bf16[16,32,256]{2,1,0:T(8,128)(2,1)} %broadcast_in_dim.10), calls=%async_computation.2 | async-start | bytes 524288 | tf_op jit(solution)/shard_map/all_to_all | solution.py:24
  105.1 0.7 copy-start.2
  105.8 14.2 %copy-start.6 = (f32[128]{0:T(128)S(1)}, f32[128]{0:T(128)}, u32[]{:S(2)}) copy-start(f32[128]{0:T(128)} %param.9) | copy-start | bytes 1540
  105.8 14.5 %copy-start.5 = (f32[32]{0:T(128)S(1)}, f32[32]{0:T(128)}, u32[]{:S(2)}) copy-start(f32[32]{0:T(128)} %param.8) | copy-start | bytes 388
  113.7 40.7 %copy-start.1 = (bf16[512,1024]{1,0:T(8,128)(2,1)S(1)}, bf16[512,1024]{1,0:T(8,128)(2,1)}, u32[]{:S(2)}) copy-start(bf16[512,1024]{1,0:T(8,128)(2,1)} %get-tuple-element.5) | copy-start | bytes 3145732
  113.7 23.1 %all-to-all-start.3 = ((bf16[32,32,256]{2,1,0:T(8,128)(2,1)}), bf16[32,32,256]{2,1,0:T(8,128)(2,1)S(1)}, u32[]{:S(2)}, u32[]{:S(2)}) async-start(bf16[32,32,256]{2,1,0:T(8,128)(2,1)} %bitcast.92), calls=%async_computation.3 | async-start | bytes 1048576 | tf_op jit(solution)/shard_map/all_to_all | solution.py:135
  137.7 16.7 %all-to-all-start.4 = ((bf16[16,32,256]{2,1,0:T(8,128)(2,1)}), bf16[16,32,256]{2,1,0:T(8,128)(2,1)S(1)}, u32[]{:S(2)}, u32[]{:S(2)}) async-start(bf16[16,32,256]{2,1,0:T(8,128)(2,1)} %broadcast_in_dim.11), calls=%async_computation.4 | async-start | bytes 524288 | tf_op jit(solution)/shard_map/all_to_all | solution.py:24
  155.7 26.9 %all-to-all-start.5 = ((bf16[32,8,1088]{2,1,0:T(8,128)(2,1)}), bf16[32,8,1088]{2,1,0:T(8,128)(2,1)S(1)}, u32[]{:S(2)}, u32[]{:S(2)}) async-start(bf16[32,8,1088]{2,1,0:T(8,128)(2,1)} %pad_maximum_fusion.1), calls=%async_computation.5 | async-start | bytes 1179648 | tf_op jit(solution)/shard_map/all_to_all | solution.py:147
Sparse Core Ops, SparseCore 0:
  10.0 41.9 all-gather.7
  54.2 50.0 all-gather.5

commit v4 on v3

--- a/solution.py
+++ b/solution.py
@@ -25,18 +25,30 @@
 
 
 LANES = 128
+SHIFTS = (0, 4, 3, -3, 2, -2, 1, -1)
 
 
-def tile_kernel(left_ref, piece_ref, inward_ref, tiles_ref, message_ref, gram_ref, tile_ref, sum_ref):
-    n_z, n_k, n_xh, block, _ = left_ref.shape
+def tile_kernel(y_ref, left_ref, inward_ref, *refs):
+    n_blocks = len(SHIFTS)
+    block_refs, (tiles_ref, message_ref, piece_ref, gram_ref, tile_ref, sum_ref) = refs[:n_blocks], refs[n_blocks:]
+    n_z, n_k, n_xh, block, aux_width = left_ref.shape
     a_local = 8
     rows = n_z * n_k * n_xh * block
-    d_local = piece_ref.shape[0] // LANES
+    n_xl, d_local, b_local, _ = block_refs[0].shape
+
+    @pl.when(pl.program_id(0) == 0)
+    def _():
+        for shift, block_ref in zip(SHIFTS, block_refs):
+            y = (y_ref[0] + n_blocks - shift) % n_blocks
+            for d in range(d_local):
+                for xl in range(n_xl):
+                    piece_ref[d, y, xl * b_local : (xl + 1) * b_local, :] = block_ref[xl, d]
+
     left = jnp.concatenate(
         [left_ref[z, k, xh] for z in range(n_z) for xh in range(n_xh) for k in range(n_k)], axis=0
     )
     gram = lax.dot_general(
-        left, piece_ref[...], (((1,), (1,)), ((), ())), preferred_element_type=jnp.float32
+        left, piece_ref[...].reshape(d_local * LANES, aux_width), (((1,), (1,)), ((), ())), preferred_element_type=jnp.float32
     )
     for d in range(d_local):
         gram_ref[d] = gram[:, d * LANES : (d + 1) * LANES]
@@ -61,21 +73,22 @@
         message_ref[:, lanes] = sum_ref[half].astype(jnp.bfloat16)
 
 
-def tiles_and_ladder(left, piece, inward):
+def tiles_and_ladder(y_index, left, inward, blocks):
     n_z, n_k, n_xh, block, aux_width = left.shape
     steps = 2
     contracted = inward.shape[0]
     wide = 8 * LANES
     part = contracted // steps
-    d_local = piece.shape[0] // LANES
+    n_xl, d_local, b_local, _ = blocks[0].shape
     return pl.pallas_call(
         tile_kernel,
         grid=(steps,),
         in_specs=[
+            pl.BlockSpec(memory_space=pltpu.SMEM),
             pl.BlockSpec((n_z // steps, n_k, n_xh, block, aux_width), lambda s: (s, 0, 0, 0, 0)),
-            pl.BlockSpec(memory_space=pltpu.VMEM),
             pl.BlockSpec((part, inward.shape[1]), lambda s: (s, 0)),
-        ],
+        ]
+        + [pl.BlockSpec(blocks[0].shape, lambda s: (0, 0, 0, 0), pipeline_mode=pl.Buffered(1)) for _ in blocks],
         out_specs=[
             pl.BlockSpec((part, wide), lambda s: (s, 0)),
             pl.BlockSpec((wide, inward.shape[1]), lambda s: (0, 0)),
@@ -85,12 +98,13 @@
             jax.ShapeDtypeStruct((wide, inward.shape[1]), jnp.bfloat16),
         ],
         scratch_shapes=[
+            pltpu.VMEM((d_local, len(blocks), n_xl * b_local, aux_width), jnp.bfloat16),
             pltpu.VMEM((d_local, 2 * part, LANES), jnp.float32),
             pltpu.VMEM((part // (8 * d_local), d_local, 8, wide), jnp.float32),
             pltpu.VMEM((2, wide, LANES), jnp.float32),
         ],
         name="tiles_and_ladder",
-    )(left, piece, inward)
+    )(y_index.reshape(1), left, inward, *blocks)
 
 
 def local(factors, amplitudes, driving, occ_energy, vir_energy):
@@ -103,10 +117,17 @@
     ab_index = lax.axis_index(AB)
 
     turned = factors.transpose(1, 0, 2)
+    theirs = lax.ppermute(turned, "xl", [(0, 1), (1, 0)])
     columns = lax.all_gather(turned[None], "xh", axis=0, tiled=True)
-    mine = lax.all_gather(turned[None], "y", axis=0, tiled=True)
     left = lax.all_gather(columns[None], ("z", "k"), axis=0, tiled=True)
     left = left.reshape(n_z, n_k, n_xh, d_local * a_local, aux_width)
+    even_member = lax.axis_index("xl") == 0
+    pair = jnp.stack([jnp.where(even_member, turned, theirs), jnp.where(even_member, theirs, turned)])
+    n_y = lax.axis_size("y")
+    y_blocks = [pair]
+    for shift in SHIFTS[1:]:
+        y_blocks.append(lax.ppermute(pair, "y", [(i, (i + shift) % n_y) for i in range(n_y)]))
+
     n_occ = occ_energy.shape[0]
     occ_pairs = (occ_energy[: pairs // n_occ, None] + occ_energy[None, :]).reshape(pairs)
     occ_rows = lax.dynamic_slice_in_dim(occ_pairs, cd_index * rows, rows)
@@ -118,20 +139,15 @@
 
     rounded = amplitudes.astype(jnp.bfloat16).astype(jnp.float32)
     both = jnp.stack([amplitudes, driving])
-    mirror = lax.all_to_all(both, AB, split_axis=3, concat_axis=2, tiled=True).transpose(0, 1, 3, 2)
+    mirror = lax.all_to_all(both, AB, split_axis=3, concat_axis=2, tiled=True)
+    mirror = mirror.transpose(0, 1, 3, 2)
     rounded_mirror = mirror[0].astype(jnp.bfloat16).astype(jnp.float32)
     even = 0.5 * jnp.stack([rounded + rounded_mirror, both[1] + mirror[1]])
-    theirs = lax.ppermute(mine, "xl", [(0, 1), (1, 0)])
-    even_member = lax.axis_index("xl") == 0
-    piece = jnp.stack(
-        [jnp.where(even_member, mine, theirs), jnp.where(even_member, theirs, mine)], axis=1
-    )
-    piece = piece.transpose(2, 0, 1, 3, 4).reshape(d_local * virtuals, aux_width)
     blocks = pair_layout(even, n_cd)
     current, drive = blocks[0], blocks[1]
     inward = spread(current.astype(jnp.bfloat16), n_ab)
 
-    tiles, first = tiles_and_ladder(left, piece, inward)
+    tiles, first = tiles_and_ladder(lax.axis_index("y"), left, inward, y_blocks)
     parts = lax.all_to_all(first.reshape(n_cd, -1, pairs), CD, 0, 0, tiled=True)
     ladder = jnp.sum(parts.astype(jnp.float32), axis=0)
     current = current - (drive + denom_block * current + ladder) / denom_block

time: 192 us -> 199 us (1.036)
  starting transfers between devices: 51.6 us -> 77.2 us
  waiting for transfers between devices: 89 us -> 76.6 us
  local copies, waits for them, and re-layouts: 14.1 us -> 11.2 us
    ppermute x1 -> x8, starting transfers between devices: 2.99 us -> 28 us  [the longest x7 24.8 us: local(): lax.ppermute(pair, 'y', [(i, (i + shift) % n_y) for i in range(n_y)])]
    all_gather x1 -> x0, waiting for transfers between devices: 24.5 us -> none  [local(): mine = lax.all_gather(turned[None], 'y', axis=0, tiled=True)]
    ppermute x1 -> x8, waiting for transfers between devices: 0.01 us -> 24.4 us  [the longest x7 24.4 us: local(): lax.ppermute(pair, 'y', [(i, (i + shift) % n_y) for i in range(n_y)])]
    all_to_all x2, waiting for transfers between devices: 19.2 us -> 9.84 us  [spread(): lax.all_to_all(copies, AB, 0, 0, tiled=True).reshape(-1, block.shape[1])]
    all_to_all x1, waiting for transfers between devices: 10.8 us -> 3.25 us  [pair_layout(): swapped = lax.all_to_all(split.reshape(n_cd, -1), CD, 0, 0, tiled=True)]
    all_to_all x1, waiting for transfers between devices: 0.01 us -> 4.62 us  [local(): mirror = lax.all_to_all(both, AB, split_axis=3, concat_axis=2, tiled=True)]
    all_to_all x2, starting transfers between devices: 10.9 us -> 7.06 us  [spread(): lax.all_to_all(copies, AB, 0, 0, tiled=True).reshape(-1, block.shape[1])]
    all_to_all x1, starting transfers between devices: 6.27 us -> 9.88 us  [local(): parts = lax.all_to_all(first.reshape(n_cd, -1, pairs), CD, 0, 0, tiled=True)]
  transfers between devices with their start and end apart: 9 -> 15, of which waited for: 6 -> 9; matrix products, arithmetic and copies ran while one was open for 7% -> 5% of each run, Pallas kernels for 0% -> 0%
where the time goes in v4:
time: 199 us; the launch traced here: 198 us
  starting transfers between devices  77.2 us (39%)
  waiting for transfers between devices  76.6 us (38%)
  between operations  14.5 us (7%)
  local copies, waits for them, and re-layouts  11.2 us (6%)
  Pallas kernels  7.34 us (4%)
  blocking collectives  6.68 us (3%)
  other arithmetic  3.83 us (2%)
    ppermute x7, starting transfers between devices, local(): lax.ppermute(pair, 'y', [(i, (i + shift) % n_y) for i in range(n_y)])  24.8 us
    ppermute x7, waiting for transfers between devices, local(): lax.ppermute(pair, 'y', [(i, (i + shift) % n_y) for i in range(n_y)])  24.4 us
    all_to_all x1, waiting for transfers between devices, local(): parts = lax.all_to_all(message, CD, 0, 0, tiled=True)  18.3 us
    all_to_all x1, waiting for transfers between devices, local(): parts = lax.all_to_all(first.reshape(n_cd, -1, pairs), CD, 0, 0, tiled=True)  16.1 us
    all_to_all x1, starting transfers between devices, pair_layout(): swapped = lax.all_to_all(split.reshape(n_cd, -1), CD, 0, 0, tiled=True)  15.6 us
    all_to_all x1, starting transfers between devices, local(): parts = lax.all_to_all(first.reshape(n_cd, -1, pairs), CD, 0, 0, tiled=True)  9.88 us
    all_to_all x2, waiting for transfers between devices, spread(): lax.all_to_all(copies, AB, 0, 0, tiled=True).reshape(-1, block.shape[1])  9.84 us
    all_to_all x1, starting transfers between devices, local(): mirror = lax.all_to_all(both, AB, split_axis=3, concat_axis=2, tiled=True)  8.65 us
  transfers between devices with their start and end apart: 15, of which 9 were waited for; matrix products, arithmetic and copies ran while one was open for 5% of the time, Pallas kernels for 0%

profile of v4, /device:TPU:1, one launch (start us, length us, event | category | flops | bytes accessed | tf_op | source)
XLA Modules:
  0.0 197.8 jit_solution(11136850726423827455)
XLA Ops:
  7.2 1.0 copy.138
  8.2 6.7 %all-gather = bf16[8,8,2048]{2,1,0:T(8,128)(2,1)} all-gather(bf16[4,8,2048]{2,1,0:T(8,128)(2,1)S(1)} %bitcast.84), channel_id=2, replica_groups=mesh['y'=8,'xl'=2,'z'=8,'xh'=2,'k'=2] {'xh'}, dimensions={0}, use_global_device_ids=true | all-gather | bytes 393216 | tf_op jit(solution)/shard_map/all_gather | solution.py:121
  14.9 0.8 pad_maximum_fusion.2
  16.2 1.1 reshape.216
  17.3 8.6 %all-to-all-start = ((f32[16,1,1024]{2,1,0:T(1,128)}), f32[16,1,1024]{2,1,0:T(1,128)S(1)}, u32[]{:S(2)}, u32[]{:S(2)}) async-start(f32[16,1,1024]{2,1,0:T(1,128)} %reshape.216), calls=%async_computation | async-start | bytes 131072 | tf_op jit(solution)/shard_map/all_to_all | solution.py:142
  26.0 3.3 %collective-permute-start = (bf16[4,8,2048]{2,1,0:T(8,128)(2,1)S(1)}, bf16[4,8,2048]{2,1,0:T(8,128)(2,1)S(1)}, u32[]{:S(2)}, u32[]{:S(2)}) collective-permute-start(bf16[4,8,2048]{2,1,0:T(8,128)(2,1)S(1)} %bitcast.85), channel_id=1, source_target_pairs={{0,32},{32,0},{1,33},{33,1},{2,34},{34,2},{3,35},{35,3},{4,36},{36... | collective-permute-start | bytes 393224 | tf_op jit(solution)/shard_map/ppermute | solution.py:120
  29.2 4.6 %all-to-all-done = f32[16,1,1024]{2,1,0:T(1,128)S(1)} async-done(((f32[16,1,1024]{2,1,0:T(1,128)}), f32[16,1,1024]{2,1,0:T(1,128)S(1)}, u32[]{:S(2)}, u32[]{:S(2)}) %all-to-all-start) | async-done | bytes 65568 | tf_op jit(solution)/shard_map/all_to_all | solution.py:142
  34.4 0.8 reduce
  39.0 15.6 %all-to-all-start.1 = ((f32[32,1,512]{2,1,0:T(1,128)}), f32[32,1,512]{2,1,0:T(1,128)S(1)}, u32[]{:S(2)}, u32[]{:S(2)}) async-start(f32[32,1,512]{2,1,0:T(1,128)} %copy.114), calls=%async_computation.1 | async-start | bytes 131072 | tf_op jit(solution)/shard_map/all_to_all | solution.py:17
  54.8 2.3 %collective-permute-start.1 = (bf16[2,4,8,2048]{3,2,1,0:T(8,128)(2,1)S(1)}, bf16[2,4,8,2048]{3,2,1,0:T(8,128)(2,1)S(1)}, u32[]{:S(2)}, u32[]{:S(2)}) collective-permute-start(bf16[2,4,8,2048]{3,2,1,0:T(8,128)(2,1)S(1)} %pad_maximum_fusion.1.refs_0_), channel_id=1, source_target_pairs={{0,256},{64,320},{128,384},{192,448},{256,0},{320,64},{384,128},{4... | collective-permute-start | bytes 786440 | tf_op jit(solution)/shard_map/ppermute | solution.py:129
  57.1 4.7 %collective-permute-start.2 = (bf16[2,4,8,2048]{3,2,1,0:T(8,128)(2,1)S(1)}, bf16[2,4,8,2048]{3,2,1,0:T(8,128)(2,1)S(1)}, u32[]{:S(2)}, u32[]{:S(2)}) collective-permute-start(bf16[2,4,8,2048]{3,2,1,0:T(8,128)(2,1)S(1)} %pad_maximum_fusion.1.refs_0_), channel_id=1, source_target_pairs={{0,192},{64,256},{128,320},{192,384},{256,448},{320,0},{384,64},{4... | collective-permute-start | bytes 786440 | tf_op jit(solution)/shard_map/ppermute | solution.py:129
  61.8 3.3 %all-to-all-done.1 = f32[32,1,512]{2,1,0:T(1,128)S(1)} async-done(((f32[32,1,512]{2,1,0:T(1,128)}), f32[32,1,512]{2,1,0:T(1,128)S(1)}, u32[]{:S(2)}, u32[]{:S(2)}) %all-to-all-start.1) | async-done | bytes 65568 | tf_op jit(solution)/shard_map/all_to_all | solution.py:17
  65.5 0.8 broadcast_in_dim.10
  66.3 3.5 %all-to-all-start.2 = ((bf16[16,32,256]{2,1,0:T(8,128)(2,1)}), bf16[16,32,256]{2,1,0:T(8,128)(2,1)S(1)}, u32[]{:S(2)}, u32[]{:S(2)}) async-start(bf16[16,32,256]{2,1,0:T(8,128)(2,1)} %broadcast_in_dim.10), calls=%async_computation.2 | async-start | bytes 524288 | tf_op jit(solution)/shard_map/all_to_all | solution.py:24
  69.8 6.2 %collective-permute-start.3 = (bf16[2,4,8,2048]{3,2,1,0:T(8,128)(2,1)S(1)}, bf16[2,4,8,2048]{3,2,1,0:T(8,128)(2,1)S(1)}, u32[]{:S(2)}, u32[]{:S(2)}) collective-permute-start(bf16[2,4,8,2048]{3,2,1,0:T(8,128)(2,1)S(1)} %pad_maximum_fusion.1.refs_0_), channel_id=1, source_target_pairs={{0,320},{64,384},{128,448},{192,0},{256,64},{320,128},{384,192},{4... | collective-permute-start | bytes 786440 | tf_op jit(solution)/shard_map/ppermute | solution.py:129
  76.0 2.2 %collective-permute-start.4 = (bf16[2,4,8,2048]{3,2,1,0:T(8,128)(2,1)S(1)}, bf16[2,4,8,2048]{3,2,1,0:T(8,128)(2,1)S(1)}, u32[]{:S(2)}, u32[]{:S(2)}) collective-permute-start(bf16[2,4,8,2048]{3,2,1,0:T(8,128)(2,1)S(1)} %pad_maximum_fusion.1.refs_0_), channel_id=1, source_target_pairs={{0,128},{64,192},{128,256},{192,320},{256,384},{320,448},{384,0},{... | collective-permute-start | bytes 786440 | tf_op jit(solution)/shard_map/ppermute | solution.py:129
  78.2 5.2 %collective-permute-start.5 = (bf16[2,4,8,2048]{3,2,1,0:T(8,128)(2,1)S(1)}, bf16[2,4,8,2048]{3,2,1,0:T(8,128)(2,1)S(1)}, u32[]{:S(2)}, u32[]{:S(2)}) collective-permute-start(bf16[2,4,8,2048]{3,2,1,0:T(8,128)(2,1)S(1)} %pad_maximum_fusion.1.refs_0_), channel_id=1, source_target_pairs={{0,384},{64,448},{128,0},{192,64},{256,128},{320,192},{384,256},{4... | collective-permute-start | bytes 786440 | tf_op jit(solution)/shard_map/ppermute | solution.py:129
  83.4 2.2 %collective-permute-start.6 = (bf16[2,4,8,2048]{3,2,1,0:T(8,128)(2,1)S(1)}, bf16[2,4,8,2048]{3,2,1,0:T(8,128)(2,1)S(1)}, u32[]{:S(2)}, u32[]{:S(2)}) collective-permute-start(bf16[2,4,8,2048]{3,2,1,0:T(8,128)(2,1)S(1)} %pad_maximum_fusion.1.refs_0_), channel_id=1, source_target_pairs={{0,64},{64,128},{128,192},{192,256},{256,320},{320,384},{384,448},... | collective-permute-start | bytes 786440 | tf_op jit(solution)/shard_map/ppermute | solution.py:129
  85.7 5.5 %collective-permute-done.2.refs_2_ = bf16[2,4,8,2048]{3,2,1,0:T(8,128)(2,1)S(1)} collective-permute-done((bf16[2,4,8,2048]{3,2,1,0:T(8,128)(2,1)S(1)}, bf16[2,4,8,2048]{3,2,1,0:T(8,128)(2,1)S(1)}, u32[]{:S(2)}, u32[]{:S(2)}) %collective-permute-start.2) | collective-permute-done | bytes 262176 | tf_op jit(solution)/shard_map/ppermute | solution.py:129
  91.2 1.9 collective-permute-start.7
  93.1 7.3 %collective-permute-done.4.refs_4_ = bf16[2,4,8,2048]{3,2,1,0:T(8,128)(2,1)S(1)} collective-permute-done((bf16[2,4,8,2048]{3,2,1,0:T(8,128)(2,1)S(1)}, bf16[2,4,8,2048]{3,2,1,0:T(8,128)(2,1)S(1)}, u32[]{:S(2)}, u32[]{:S(2)}) %collective-permute-start.4) | collective-permute-done | bytes 262176 | tf_op jit(solution)/shard_map/ppermute | solution.py:129
  100.4 7.8 %collective-permute-done.5.refs_5_ = bf16[2,4,8,2048]{3,2,1,0:T(8,128)(2,1)S(1)} collective-permute-done((bf16[2,4,8,2048]{3,2,1,0:T(8,128)(2,1)S(1)}, bf16[2,4,8,2048]{3,2,1,0:T(8,128)(2,1)S(1)}, u32[]{:S(2)}, u32[]{:S(2)}) %collective-permute-start.5) | collective-permute-done | bytes 262176 | tf_op jit(solution)/shard_map/ppermute | solution.py:129
  108.1 3.9 %collective-permute-done.6.refs_6_ = bf16[2,4,8,2048]{3,2,1,0:T(8,128)(2,1)S(1)} collective-permute-done((bf16[2,4,8,2048]{3,2,1,0:T(8,128)(2,1)S(1)}, bf16[2,4,8,2048]{3,2,1,0:T(8,128)(2,1)S(1)}, u32[]{:S(2)}, u32[]{:S(2)}) %collective-permute-start.6) | collective-permute-done | bytes 262176 | tf_op jit(solution)/shard_map/ppermute | solution.py:129
  113.0 7.3 %tiles_and_ladder.1 = (bf16[512,1024]{1,0:T(8,128)(2,1)}, bf16[1024,256]{1,0:T(8,128)(2,1)}) custom-call(s32[1]{0:T(128)} %bitcast.17.y_ref, bf16[8,2,2,32,2048]{4,3,2,1,0:T(8,128)(2,1)} %bitcast.74, bf16[512,256]{1,0:T(8,128)(2,1)} %bitcast.83, bf16[2,4,8,2048]{3,2,1,0:T(8,128)(2,1)} %copy-done.1, bf16[2,4,8,2048]{3,2,1,0:T(8,128)(2,1)} %copy-done.6, ...), custom_call_target="tpu_custom_call" | custom-call | tf_op jit(solution)/shard_map/tiles_and_ladder/pallas_call | solution.py:83
  120.3 9.9 %all-to-all-start.3 = ((bf16[32,32,256]{2,1,0:T(8,128)(2,1)}), bf16[32,32,256]{2,1,0:T(8,128)(2,1)S(1)}, u32[]{:S(2)}, u32[]{:S(2)}) async-start(bf16[32,32,256]{2,1,0:T(8,128)(2,1)} %bitcast.88), calls=%async_computation.3 | async-start | bytes 1048576 | tf_op jit(solution)/shard_map/all_to_all | solution.py:151
  131.0 16.1 %all-to-all-done.3 = bf16[32,32,256]{2,1,0:T(8,128)(2,1)S(1)} async-done(((bf16[32,32,256]{2,1,0:T(8,128)(2,1)}), bf16[32,32,256]{2,1,0:T(8,128)(2,1)S(1)}, u32[]{:S(2)}, u32[]{:S(2)}) %all-to-all-start.3) | async-done | bytes 524320 | tf_op jit(solution)/shard_map/all_to_all | solution.py:151
  147.2 0.7 broadcast_in_dim.11
  147.9 3.5 %all-to-all-start.4 = ((bf16[16,32,256]{2,1,0:T(8,128)(2,1)}), bf16[16,32,256]{2,1,0:T(8,128)(2,1)S(1)}, u32[]{:S(2)}, u32[]{:S(2)}) async-start(bf16[16,32,256]{2,1,0:T(8,128)(2,1)} %broadcast_in_dim.11), calls=%async_computation.4 | async-start | bytes 524288 | tf_op jit(solution)/shard_map/all_to_all | solution.py:24
  151.8 9.8 %all-to-all-done.4 = bf16[16,32,256]{2,1,0:T(8,128)(2,1)S(1)} async-done(((bf16[16,32,256]{2,1,0:T(8,128)(2,1)}), bf16[16,32,256]{2,1,0:T(8,128)(2,1)S(1)}, u32[]{:S(2)}, u32[]{:S(2)}) %all-to-all-start.4) | async-done | bytes 262176 | tf_op jit(solution)/shard_map/all_to_all | solution.py:24
  162.1 0.9 pad_maximum_fusion
  162.9 7.9 %all-to-all-start.5 = ((bf16[32,8,1088]{2,1,0:T(8,128)(2,1)}), bf16[32,8,1088]{2,1,0:T(8,128)(2,1)S(1)}, u32[]{:S(2)}, u32[]{:S(2)}) async-start(bf16[32,8,1088]{2,1,0:T(8,128)(2,1)} %pad_maximum_fusion), calls=%async_computation.5 | async-start | bytes 1179648 | tf_op jit(solution)/shard_map/all_to_all | solution.py:163
  171.0 18.3 %all-to-all-done.5 = bf16[32,8,1088]{2,1,0:T(8,128)(2,1)S(1)} async-done(((bf16[32,8,1088]{2,1,0:T(8,128)(2,1)}), bf16[32,8,1088]{2,1,0:T(8,128)(2,1)S(1)}, u32[]{:S(2)}, u32[]{:S(2)}) %all-to-all-start.5) | async-done | bytes 557088 | tf_op jit(solution)/shard_map/all_to_all | solution.py:163
  (83 shorter events, 9.5 us)
Async XLA Ops:
  7.2 104.9 %all-gather.4.cloned.1.call-start = ((), (), s32[]{:S(2)}) async-start(), calls=%async_computation.6 | async-start | bytes 4456448 | tf_op jit(solution)/shard_map/all_gather | solution.py:122
  17.3 16.6 %all-to-all-start = ((f32[16,1,1024]{2,1,0:T(1,128)}), f32[16,1,1024]{2,1,0:T(1,128)S(1)}, u32[]{:S(2)}, u32[]{:S(2)}) async-start(f32[16,1,1024]{2,1,0:T(1,128)} %reshape.216), calls=%async_computation | async-start | bytes 131072 | tf_op jit(solution)/shard_map/all_to_all | solution.py:142
  26.0 28.7 %collective-permute-start = (bf16[4,8,2048]{2,1,0:T(8,128)(2,1)S(1)}, bf16[4,8,2048]{2,1,0:T(8,128)(2,1)S(1)}, u32[]{:S(2)}, u32[]{:S(2)}) collective-permute-start(bf16[4,8,2048]{2,1,0:T(8,128)(2,1)S(1)} %bitcast.85), channel_id=1, source_target_pairs={{0,32},{32,0},{1,33},{33,1},{2,34},{34,2},{3,35},{35,3},{4,36},{36... | collective-permute-start | bytes 393224 | tf_op jit(solution)/shard_map/ppermute | solution.py:120
  35.8 1.1 copy-start.4
  35.8 1.1 copy-start.5
  37.8 16.9 %copy-start.3 = (bf16[8,4,2048]{2,1,0:T(4,128)(2,1)S(1)}, bf16[8,4,2048]{2,1,0:T(4,128)(2,1)}, u32[]{:S(2)}) copy-start(bf16[8,4,2048]{2,1,0:T(4,128)(2,1)} %param.5) | copy-start | bytes 393220
  39.0 26.1 %all-to-all-start.1 = ((f32[32,1,512]{2,1,0:T(1,128)}), f32[32,1,512]{2,1,0:T(1,128)S(1)}, u32[]{:S(2)}, u32[]{:S(2)}) async-start(f32[32,1,512]{2,1,0:T(1,128)} %copy.114), calls=%async_computation.1 | async-start | bytes 131072 | tf_op jit(solution)/shard_map/all_to_all | solution.py:17
  54.8 57.3 %copy-start.1 = (bf16[2,4,8,2048]{3,2,1,0:T(8,128)(2,1)}, bf16[2,4,8,2048]{3,2,1,0:T(8,128)(2,1)S(1)}, u32[]{:S(2)}) copy-start(bf16[2,4,8,2048]{3,2,1,0:T(8,128)(2,1)S(1)} %pad_maximum_fusion.1.refs_0_) | copy-start | bytes 786436
  54.8 28.6 %collective-permute-start.1 = (bf16[2,4,8,2048]{3,2,1,0:T(8,128)(2,1)S(1)}, bf16[2,4,8,2048]{3,2,1,0:T(8,128)(2,1)S(1)}, u32[]{:S(2)}, u32[]{:S(2)}) collective-permute-start(bf16[2,4,8,2048]{3,2,1,0:T(8,128)(2,1)S(1)} %pad_maximum_fusion.1.refs_0_), channel_id=1, source_target_pairs={{0,256},{64,320},{128,384},{192,448},{256,0},{320,64},{384,128},{4... | collective-permute-start | bytes 786440 | tf_op jit(solution)/shard_map/ppermute | solution.py:129
  57.1 34.0 %collective-permute-start.2 = (bf16[2,4,8,2048]{3,2,1,0:T(8,128)(2,1)S(1)}, bf16[2,4,8,2048]{3,2,1,0:T(8,128)(2,1)S(1)}, u32[]{:S(2)}, u32[]{:S(2)}) collective-permute-start(bf16[2,4,8,2048]{3,2,1,0:T(8,128)(2,1)S(1)} %pad_maximum_fusion.1.refs_0_), channel_id=1, source_target_pairs={{0,192},{64,256},{128,320},{192,384},{256,448},{320,0},{384,64},{4... | collective-permute-start | bytes 786440 | tf_op jit(solution)/shard_map/ppermute | solution.py:129
  66.3 45.8 %all-to-all-start.2 = ((bf16[16,32,256]{2,1,0:T(8,128)(2,1)}), bf16[16,32,256]{2,1,0:T(8,128)(2,1)S(1)}, u32[]{:S(2)}, u32[]{:S(2)}) async-start(bf16[16,32,256]{2,1,0:T(8,128)(2,1)} %broadcast_in_dim.10), calls=%async_computation.2 | async-start | bytes 524288 | tf_op jit(solution)/shard_map/all_to_all | solution.py:24
  69.8 23.3 %collective-permute-start.3 = (bf16[2,4,8,2048]{3,2,1,0:T(8,128)(2,1)S(1)}, bf16[2,4,8,2048]{3,2,1,0:T(8,128)(2,1)S(1)}, u32[]{:S(2)}, u32[]{:S(2)}) collective-permute-start(bf16[2,4,8,2048]{3,2,1,0:T(8,128)(2,1)S(1)} %pad_maximum_fusion.1.refs_0_), channel_id=1, source_target_pairs={{0,320},{64,384},{128,448},{192,0},{256,64},{320,128},{384,192},{4... | collective-permute-start | bytes 786440 | tf_op jit(solution)/shard_map/ppermute | solution.py:129
  76.0 24.3 %collective-permute-start.4 = (bf16[2,4,8,2048]{3,2,1,0:T(8,128)(2,1)S(1)}, bf16[2,4,8,2048]{3,2,1,0:T(8,128)(2,1)S(1)}, u32[]{:S(2)}, u32[]{:S(2)}) collective-permute-start(bf16[2,4,8,2048]{3,2,1,0:T(8,128)(2,1)S(1)} %pad_maximum_fusion.1.refs_0_), channel_id=1, source_target_pairs={{0,128},{64,192},{128,256},{192,320},{256,384},{320,448},{384,0},{... | collective-permute-start | bytes 786440 | tf_op jit(solution)/shard_map/ppermute | solution.py:129
  78.2 29.9 %collective-permute-start.5 = (bf16[2,4,8,2048]{3,2,1,0:T(8,128)(2,1)S(1)}, bf16[2,4,8,2048]{3,2,1,0:T(8,128)(2,1)S(1)}, u32[]{:S(2)}, u32[]{:S(2)}) collective-permute-start(bf16[2,4,8,2048]{3,2,1,0:T(8,128)(2,1)S(1)} %pad_maximum_fusion.1.refs_0_), channel_id=1, source_target_pairs={{0,384},{64,448},{128,0},{192,64},{256,128},{320,192},{384,256},{4... | collective-permute-start | bytes 786440 | tf_op jit(solution)/shard_map/ppermute | solution.py:129
  83.4 28.7 %copy-start.6 = (bf16[2,4,8,2048]{3,2,1,0:T(8,128)(2,1)}, bf16[2,4,8,2048]{3,2,1,0:T(8,128)(2,1)S(1)}, u32[]{:S(2)}) copy-start(bf16[2,4,8,2048]{3,2,1,0:T(8,128)(2,1)S(1)} %collective-permute-done.1.refs_1_) | copy-start | bytes 786436
  83.4 28.6 %collective-permute-start.6 = (bf16[2,4,8,2048]{3,2,1,0:T(8,128)(2,1)S(1)}, bf16[2,4,8,2048]{3,2,1,0:T(8,128)(2,1)S(1)}, u32[]{:S(2)}, u32[]{:S(2)}) collective-permute-start(bf16[2,4,8,2048]{3,2,1,0:T(8,128)(2,1)S(1)} %pad_maximum_fusion.1.refs_0_), channel_id=1, source_target_pairs={{0,64},{64,128},{128,192},{192,256},{256,320},{320,384},{384,448},... | collective-permute-start | bytes 786440 | tf_op jit(solution)/shard_map/ppermute | solution.py:129
  91.2 20.9 %copy-start.7 = (bf16[2,4,8,2048]{3,2,1,0:T(8,128)(2,1)}, bf16[2,4,8,2048]{3,2,1,0:T(8,128)(2,1)S(1)}, u32[]{:S(2)}) copy-start(bf16[2,4,8,2048]{3,2,1,0:T(8,128)(2,1)S(1)} %collective-permute-done.2.refs_2_) | copy-start | bytes 786436
  91.2 20.9 %collective-permute-start.7 = (bf16[2,4,8,2048]{3,2,1,0:T(8,128)(2,1)S(1)}, bf16[2,4,8,2048]{3,2,1,0:T(8,128)(2,1)S(1)}, u32[]{:S(2)}, u32[]{:S(2)}) collective-permute-start(bf16[2,4,8,2048]{3,2,1,0:T(8,128)(2,1)S(1)} %pad_maximum_fusion.1.refs_0_), channel_id=1, source_target_pairs={{0,448},{64,0},{128,64},{192,128},{256,192},{320,256},{384,320},{4... | collective-permute-start | bytes 786440 | tf_op jit(solution)/shard_map/ppermute | solution.py:129
  93.1 19.0 %copy-start.8 = (bf16[2,4,8,2048]{3,2,1,0:T(8,128)(2,1)}, bf16[2,4,8,2048]{3,2,1,0:T(8,128)(2,1)S(1)}, u32[]{:S(2)}) copy-start(bf16[2,4,8,2048]{3,2,1,0:T(8,128)(2,1)S(1)} %collective-permute-done.3.refs_3_) | copy-start | bytes 786436
  100.4 11.8 %copy-start.9 = (bf16[2,4,8,2048]{3,2,1,0:T(8,128)(2,1)}, bf16[2,4,8,2048]{3,2,1,0:T(8,128)(2,1)S(1)}, u32[]{:S(2)}) copy-start(bf16[2,4,8,2048]{3,2,1,0:T(8,128)(2,1)S(1)} %collective-permute-done.4.refs_4_) | copy-start | bytes 786436
  108.1 4.0 %copy-start.10 = (bf16[2,4,8,2048]{3,2,1,0:T(8,128)(2,1)}, bf16[2,4,8,2048]{3,2,1,0:T(8,128)(2,1)S(1)}, u32[]{:S(2)}) copy-start(bf16[2,4,8,2048]{3,2,1,0:T(8,128)(2,1)S(1)} %collective-permute-done.5.refs_5_) | copy-start | bytes 786436
  112.0 0.7 copy-start.11
  112.0 0.8 copy-start.12
  112.0 0.9 copy-start.2
  113.0 17.3 %copy-start.14 = (f32[128]{0:T(128)S(1)}, f32[128]{0:T(128)}, u32[]{:S(2)}) copy-start(f32[128]{0:T(128)} %param.9) | copy-start | bytes 1540
  113.0 17.6 %copy-start.13 = (f32[32]{0:T(128)S(1)}, f32[32]{0:T(128)}, u32[]{:S(2)}) copy-start(f32[32]{0:T(128)} %param.8) | copy-start | bytes 388
  120.3 26.7 %all-to-all-start.3 = ((bf16[32,32,256]{2,1,0:T(8,128)(2,1)}), bf16[32,32,256]{2,1,0:T(8,128)(2,1)S(1)}, u32[]{:S(2)}, u32[]{:S(2)}) async-start(bf16[32,32,256]{2,1,0:T(8,128)(2,1)} %bitcast.88), calls=%async_computation.3 | async-start | bytes 1048576 | tf_op jit(solution)/shard_map/all_to_all | solution.py:151
  130.7 30.8 %copy-start = (bf16[512,1024]{1,0:T(8,128)(2,1)S(1)}, bf16[512,1024]{1,0:T(8,128)(2,1)}, u32[]{:S(2)}) copy-start(bf16[512,1024]{1,0:T(8,128)(2,1)} %get-tuple-element.5) | copy-start | bytes 3145732
  147.9 13.7 %all-to-all-start.4 = ((bf16[16,32,256]{2,1,0:T(8,128)(2,1)}), bf16[16,32,256]{2,1,0:T(8,128)(2,1)S(1)}, u32[]{:S(2)}, u32[]{:S(2)}) async-start(bf16[16,32,256]{2,1,0:T(8,128)(2,1)} %broadcast_in_dim.11), calls=%async_computation.4 | async-start | bytes 524288 | tf_op jit(solution)/shard_map/all_to_all | solution.py:24
  162.9 26.4 %all-to-all-start.5 = ((bf16[32,8,1088]{2,1,0:T(8,128)(2,1)}), bf16[32,8,1088]{2,1,0:T(8,128)(2,1)S(1)}, u32[]{:S(2)}, u32[]{:S(2)}) async-start(bf16[32,8,1088]{2,1,0:T(8,128)(2,1)} %pad_maximum_fusion), calls=%async_computation.5 | async-start | bytes 1179648 | tf_op jit(solution)/shard_map/all_to_all | solution.py:163
Sparse Core Ops, SparseCore 0:
  15.0 52.6 all-gather.3

commit v5 on v4

--- a/solution.py
+++ b/solution.py
@@ -25,7 +25,7 @@
 
 
 LANES = 128
-SHIFTS = (0, 4, 3, -3, 2, -2, 1, -1)
+SHIFTS = ((0,), (4,), (2,), (-2,), (1, 5), (-1, 3))
 
 
 def tile_kernel(y_ref, left_ref, inward_ref, *refs):
@@ -34,15 +34,18 @@
     n_z, n_k, n_xh, block, aux_width = left_ref.shape
     a_local = 8
     rows = n_z * n_k * n_xh * block
-    n_xl, d_local, b_local, _ = block_refs[0].shape
+    _, n_xl, d_local, b_local, _ = block_refs[0].shape
+    n_y = piece_ref.shape[1]
 
     @pl.when(pl.program_id(0) == 0)
     def _():
-        for shift, block_ref in zip(SHIFTS, block_refs):
-            y = (y_ref[0] + n_blocks - shift) % n_blocks
-            for d in range(d_local):
-                for xl in range(n_xl):
-                    piece_ref[d, y, xl * b_local : (xl + 1) * b_local, :] = block_ref[xl, d]
+        for shifts, block_ref in zip(SHIFTS, block_refs):
+            for slot, shift in enumerate(shifts):
+                y = (y_ref[0] + n_y - shift) % n_y
+                for d in range(d_local):
+                    for xl in range(n_xl):
+                        rows_at = slice(xl * b_local, (xl + 1) * b_local)
+                        piece_ref[d, y, rows_at, :] = block_ref[slot, xl, d]
 
     left = jnp.concatenate(
         [left_ref[z, k, xh] for z in range(n_z) for xh in range(n_xh) for k in range(n_k)], axis=0
@@ -79,7 +82,8 @@
     contracted = inward.shape[0]
     wide = 8 * LANES
     part = contracted // steps
-    n_xl, d_local, b_local, _ = blocks[0].shape
+    _, n_xl, d_local, b_local, _ = blocks[0].shape
+    n_y = sum(block.shape[0] for block in blocks)
     return pl.pallas_call(
         tile_kernel,
         grid=(steps,),
@@ -88,7 +92,7 @@
             pl.BlockSpec((n_z // steps, n_k, n_xh, block, aux_width), lambda s: (s, 0, 0, 0, 0)),
             pl.BlockSpec((part, inward.shape[1]), lambda s: (s, 0)),
         ]
-        + [pl.BlockSpec(blocks[0].shape, lambda s: (0, 0, 0, 0), pipeline_mode=pl.Buffered(1)) for _ in blocks],
+        + [pl.BlockSpec(block.shape, lambda s: (0,) * 5, pipeline_mode=pl.Buffered(1)) for block in blocks],
         out_specs=[
             pl.BlockSpec((part, wide), lambda s: (s, 0)),
             pl.BlockSpec((wide, inward.shape[1]), lambda s: (0, 0)),
@@ -98,7 +102,7 @@
             jax.ShapeDtypeStruct((wide, inward.shape[1]), jnp.bfloat16),
         ],
         scratch_shapes=[
-            pltpu.VMEM((d_local, len(blocks), n_xl * b_local, aux_width), jnp.bfloat16),
+            pltpu.VMEM((d_local, n_y, n_xl * b_local, aux_width), jnp.bfloat16),
             pltpu.VMEM((d_local, 2 * part, LANES), jnp.float32),
             pltpu.VMEM((part // (8 * d_local), d_local, 8, wide), jnp.float32),
             pltpu.VMEM((2, wide, LANES), jnp.float32),
@@ -124,9 +128,14 @@
     even_member = lax.axis_index("xl") == 0
     pair = jnp.stack([jnp.where(even_member, turned, theirs), jnp.where(even_member, theirs, turned)])
     n_y = lax.axis_size("y")
-    y_blocks = [pair]
-    for shift in SHIFTS[1:]:
-        y_blocks.append(lax.ppermute(pair, "y", [(i, (i + shift) % n_y) for i in range(n_y)]))
+
+    def shifted(value, shift):
+        return lax.ppermute(value, "y", [(i, (i + shift) % n_y) for i in range(n_y)])
+
+    pair = pair[None]
+    opposite = shifted(pair, 4)
+    two = jnp.concatenate([pair, opposite])
+    y_blocks = [pair, opposite, shifted(pair, 2), shifted(pair, -2), shifted(two, 1), shifted(two, -1)]
 
     n_occ = occ_energy.shape[0]
     occ_pairs = (occ_energy[: pairs // n_occ, None] + occ_energy[None, :]).reshape(pairs)

time: 199 us -> 196 us (0.985)
  starting transfers between devices: 77.2 us -> 72.4 us
  waiting for transfers between devices: 76.6 us -> 78.8 us
    ppermute x7 -> x5, starting transfers between devices: 24.8 us -> 17.6 us  [shifted(): lax.ppermute(value, 'y', [(i, (i + shift) % n_y) for i in range(n_y)])]
    all_to_all x1, waiting for transfers between devices: 3.25 us -> 7.98 us  [pair_layout(): swapped = lax.all_to_all(split.reshape(n_cd, -1), CD, 0, 0, tiled=True)]
    ppermute x7 -> x5, waiting for transfers between devices: 24.4 us -> 21.9 us  [shifted(): lax.ppermute(value, 'y', [(i, (i + shift) % n_y) for i in range(n_y)])]
    unnamed x34 -> x30, local copies, waits for them, and re-layouts: 3.73 us -> 4.01 us
  transfers between devices with their start and end apart: 15 -> 13, of which waited for: 9 -> 8; matrix products, arithmetic and copies ran while one was open for 5% -> 5% of each run, Pallas kernels for 0% -> 0%
where the time goes in v5:
time: 196 us
  waiting for transfers between devices  78.8 us (40%)
  starting transfers between devices  72.4 us (37%)
  between operations  14.5 us (7%)
  local copies, waits for them, and re-layouts  11.5 us (6%)
  Pallas kernels  7.34 us (4%)
  blocking collectives  6.68 us (3%)
  other arithmetic  3.92 us (2%)
    ppermute x5, waiting for transfers between devices, shifted(): lax.ppermute(value, 'y', [(i, (i + shift) % n_y) for i in range(n_y)])  21.9 us
    all_to_all x1, waiting for transfers between devices, local(): parts = lax.all_to_all(message, CD, 0, 0, tiled=True)  18.3 us
    ppermute x5, starting transfers between devices, shifted(): lax.ppermute(value, 'y', [(i, (i + shift) % n_y) for i in range(n_y)])  17.6 us
    all_to_all x1, waiting for transfers between devices, local(): parts = lax.all_to_all(first.reshape(n_cd, -1, pairs), CD, 0, 0, tiled=True)  16.1 us
    all_to_all x1, starting transfers between devices, pair_layout(): swapped = lax.all_to_all(split.reshape(n_cd, -1), CD, 0, 0, tiled=True)  15.6 us
    all_to_all x1, starting transfers between devices, local(): parts = lax.all_to_all(first.reshape(n_cd, -1, pairs), CD, 0, 0, tiled=True)  11.6 us
    all_to_all x2, waiting for transfers between devices, spread(): lax.all_to_all(copies, AB, 0, 0, tiled=True).reshape(-1, block.shape[1])  9.92 us
    all_to_all x1, starting transfers between devices, local(): mirror = lax.all_to_all(both, AB, split_axis=3, concat_axis=2, tiled=True)  8.65 us
  transfers between devices with their start and end apart: 13, of which 8 were waited for; matrix products, arithmetic and copies ran while one was open for 5% of the time, Pallas kernels for 0%

profile of v5, /device:TPU:1, one launch (start us, length us, event | category | flops | bytes accessed | tf_op | source)
XLA Modules:
  0.0 195.6 jit_solution(15119799674771021141)
XLA Ops:
  7.2 1.0 copy.138
  8.2 6.7 %all-gather = bf16[8,8,2048]{2,1,0:T(8,128)(2,1)} all-gather(bf16[4,8,2048]{2,1,0:T(8,128)(2,1)S(1)} %bitcast.86), channel_id=2, replica_groups=mesh['y'=8,'xl'=2,'z'=8,'xh'=2,'k'=2] {'xh'}, dimensions={0}, use_global_device_ids=true | all-gather | bytes 393216 | tf_op jit(solution)/shard_map/all_gather | solution.py:125
  14.9 0.8 pad_maximum_fusion.2
  16.2 1.1 reshape.216
  17.3 8.6 %all-to-all-start = ((f32[16,1,1024]{2,1,0:T(1,128)}), f32[16,1,1024]{2,1,0:T(1,128)S(1)}, u32[]{:S(2)}, u32[]{:S(2)}) async-start(f32[16,1,1024]{2,1,0:T(1,128)} %reshape.216), calls=%async_computation | async-start | bytes 131072 | tf_op jit(solution)/shard_map/all_to_all | solution.py:151
  26.0 3.3 %collective-permute-start = (bf16[4,8,2048]{2,1,0:T(8,128)(2,1)S(1)}, bf16[4,8,2048]{2,1,0:T(8,128)(2,1)S(1)}, u32[]{:S(2)}, u32[]{:S(2)}) collective-permute-start(bf16[4,8,2048]{2,1,0:T(8,128)(2,1)S(1)} %bitcast.87), channel_id=1, source_target_pairs={{0,32},{32,0},{1,33},{33,1},{2,34},{34,2},{3,35},{35,3},{4,36},{36... | collective-permute-start | bytes 393224 | tf_op jit(solution)/shard_map/ppermute | solution.py:124
  29.2 4.6 %all-to-all-done = f32[16,1,1024]{2,1,0:T(1,128)S(1)} async-done(((f32[16,1,1024]{2,1,0:T(1,128)}), f32[16,1,1024]{2,1,0:T(1,128)S(1)}, u32[]{:S(2)}, u32[]{:S(2)}) %all-to-all-start) | async-done | bytes 65568 | tf_op jit(solution)/shard_map/all_to_all | solution.py:151
  34.4 0.8 reduce
  35.8 0.6 copy.108
  38.3 0.7 copy.114
  39.0 15.6 %all-to-all-start.1 = ((f32[32,1,512]{2,1,0:T(1,128)}), f32[32,1,512]{2,1,0:T(1,128)S(1)}, u32[]{:S(2)}, u32[]{:S(2)}) async-start(f32[32,1,512]{2,1,0:T(1,128)} %copy.114), calls=%async_computation.1 | async-start | bytes 131072 | tf_op jit(solution)/shard_map/all_to_all | solution.py:17
  54.8 2.3 %collective-permute-start.1 = (bf16[1,2,4,8,2048]{4,3,2,1,0:T(8,128)(2,1)S(1)}, bf16[1,2,4,8,2048]{4,3,2,1,0:T(8,128)(2,1)S(1)}, u32[]{:S(2)}, u32[]{:S(2)}) collective-permute-start(bf16[1,2,4,8,2048]{4,3,2,1,0:T(8,128)(2,1)S(1)} %maximum_bitcast_fusion.refs_0_), channel_id=1, source_target_pairs={{0,256},{64,320},{128,384},{192,448},{256,0},{320,64},{384,128},{4... | collective-permute-start | bytes 786440 | tf_op jit(solution)/shard_map/ppermute | solution.py:133
  57.1 8.0 %all-to-all-done.1 = f32[32,1,512]{2,1,0:T(1,128)S(1)} async-done(((f32[32,1,512]{2,1,0:T(1,128)}), f32[32,1,512]{2,1,0:T(1,128)S(1)}, u32[]{:S(2)}, u32[]{:S(2)}) %all-to-all-start.1) | async-done | bytes 65568 | tf_op jit(solution)/shard_map/all_to_all | solution.py:17
  65.4 5.0 %collective-permute-done.1.refs_1_ = bf16[1,2,4,8,2048]{4,3,2,1,0:T(8,128)(2,1)S(1)} collective-permute-done((bf16[1,2,4,8,2048]{4,3,2,1,0:T(8,128)(2,1)S(1)}, bf16[1,2,4,8,2048]{4,3,2,1,0:T(8,128)(2,1)S(1)}, u32[]{:S(2)}, u32[]{:S(2)}) %collective-permute-start.1) | collective-permute-done | bytes 262176 | tf_op jit(solution)/shard_map/ppermute | solution.py:133
  70.5 5.9 %collective-permute-start.4 = (bf16[2,2,4,8,2048]{4,3,2,1,0:T(8,128)(2,1)S(1)}, bf16[2,2,4,8,2048]{4,3,2,1,0:T(8,128)(2,1)S(1)}, u32[]{:S(2)}, u32[]{:S(2)}) collective-permute-start(bf16[2,2,4,8,2048]{4,3,2,1,0:T(8,128)(2,1)S(1)} %pad_maximum_fusion.1), channel_id=1, source_target_pairs={{0,64},{64,128},{128,192},{192,256},{256,320},{320,384},{384,448},... | collective-permute-start | bytes 1572872 | tf_op jit(solution)/shard_map/ppermute | solution.py:133
  76.4 1.9 collective-permute-start.5
  78.4 0.8 broadcast_in_dim.12
  79.2 3.5 %all-to-all-start.2 = ((bf16[16,32,256]{2,1,0:T(8,128)(2,1)}), bf16[16,32,256]{2,1,0:T(8,128)(2,1)S(1)}, u32[]{:S(2)}, u32[]{:S(2)}) async-start(bf16[16,32,256]{2,1,0:T(8,128)(2,1)} %broadcast_in_dim.12), calls=%async_computation.2 | async-start | bytes 524288 | tf_op jit(solution)/shard_map/all_to_all | solution.py:24
  82.7 4.1 %collective-permute-start.2 = (bf16[1,2,4,8,2048]{4,3,2,1,0:T(8,128)(2,1)S(1)}, bf16[1,2,4,8,2048]{4,3,2,1,0:T(8,128)(2,1)S(1)}, u32[]{:S(2)}, u32[]{:S(2)}) collective-permute-start(bf16[1,2,4,8,2048]{4,3,2,1,0:T(8,128)(2,1)S(1)} %maximum_bitcast_fusion.refs_0_), channel_id=1, source_target_pairs={{0,128},{64,192},{128,256},{192,320},{256,384},{320,448},{384,0},{... | collective-permute-start | bytes 786440 | tf_op jit(solution)/shard_map/ppermute | solution.py:133
  86.8 3.3 %collective-permute-start.3 = (bf16[1,2,4,8,2048]{4,3,2,1,0:T(8,128)(2,1)S(1)}, bf16[1,2,4,8,2048]{4,3,2,1,0:T(8,128)(2,1)S(1)}, u32[]{:S(2)}, u32[]{:S(2)}) collective-permute-start(bf16[1,2,4,8,2048]{4,3,2,1,0:T(8,128)(2,1)S(1)} %maximum_bitcast_fusion.refs_0_), channel_id=1, source_target_pairs={{0,384},{64,448},{128,0},{192,64},{256,128},{320,192},{384,256},{4... | collective-permute-start | bytes 786440 | tf_op jit(solution)/shard_map/ppermute | solution.py:133
  90.1 14.6 %collective-permute-done.2.refs_2_ = bf16[1,2,4,8,2048]{4,3,2,1,0:T(8,128)(2,1)S(1)} collective-permute-done((bf16[1,2,4,8,2048]{4,3,2,1,0:T(8,128)(2,1)S(1)}, bf16[1,2,4,8,2048]{4,3,2,1,0:T(8,128)(2,1)S(1)}, u32[]{:S(2)}, u32[]{:S(2)}) %collective-permute-start.2) | collective-permute-done | bytes 262176 | tf_op jit(solution)/shard_map/ppermute | solution.py:133
  104.7 2.3 %collective-permute-done.3.refs_3_ = bf16[1,2,4,8,2048]{4,3,2,1,0:T(8,128)(2,1)S(1)} collective-permute-done((bf16[1,2,4,8,2048]{4,3,2,1,0:T(8,128)(2,1)S(1)}, bf16[1,2,4,8,2048]{4,3,2,1,0:T(8,128)(2,1)S(1)}, u32[]{:S(2)}, u32[]{:S(2)}) %collective-permute-start.3) | collective-permute-done | bytes 262176 | tf_op jit(solution)/shard_map/ppermute | solution.py:133
  108.2 7.3 %tiles_and_ladder.1 = (bf16[512,1024]{1,0:T(8,128)(2,1)}, bf16[1024,256]{1,0:T(8,128)(2,1)}) custom-call(s32[1]{0:T(128)} %bitcast.17.y_ref, bf16[8,2,2,32,2048]{4,3,2,1,0:T(8,128)(2,1)} %bitcast.76, bf16[512,256]{1,0:T(8,128)(2,1)} %bitcast.85, bf16[1,2,4,8,2048]{4,3,2,1,0:T(8,128)(2,1)} %copy-done, bf16[1,2,4,8,2048]{4,3,2,1,0:T(8,128)(2,1)} %copy-done.3, ...), custom_call_target="tpu_custom_call" | custom-call | tf_op jit(solution)/shard_map/tiles_and_ladder/pallas_call | solution.py:87
  115.6 11.6 %all-to-all-start.3 = ((bf16[32,32,256]{2,1,0:T(8,128)(2,1)}), bf16[32,32,256]{2,1,0:T(8,128)(2,1)S(1)}, u32[]{:S(2)}, u32[]{:S(2)}) async-start(bf16[32,32,256]{2,1,0:T(8,128)(2,1)} %bitcast.90), calls=%async_computation.3 | async-start | bytes 1048576 | tf_op jit(solution)/shard_map/all_to_all | solution.py:160
  127.9 16.1 %all-to-all-done.3 = bf16[32,32,256]{2,1,0:T(8,128)(2,1)S(1)} async-done(((bf16[32,32,256]{2,1,0:T(8,128)(2,1)}), bf16[32,32,256]{2,1,0:T(8,128)(2,1)S(1)}, u32[]{:S(2)}, u32[]{:S(2)}) %all-to-all-start.3) | async-done | bytes 524320 | tf_op jit(solution)/shard_map/all_to_all | solution.py:160
  144.2 0.7 broadcast_in_dim.14
  144.9 4.1 %all-to-all-start.4 = ((bf16[16,32,256]{2,1,0:T(8,128)(2,1)}), bf16[16,32,256]{2,1,0:T(8,128)(2,1)S(1)}, u32[]{:S(2)}, u32[]{:S(2)}) async-start(bf16[16,32,256]{2,1,0:T(8,128)(2,1)} %broadcast_in_dim.14), calls=%async_computation.4 | async-start | bytes 524288 | tf_op jit(solution)/shard_map/all_to_all | solution.py:24
  149.3 9.9 %all-to-all-done.4 = bf16[16,32,256]{2,1,0:T(8,128)(2,1)S(1)} async-done(((bf16[16,32,256]{2,1,0:T(8,128)(2,1)}), bf16[16,32,256]{2,1,0:T(8,128)(2,1)S(1)}, u32[]{:S(2)}, u32[]{:S(2)}) %all-to-all-start.4) | async-done | bytes 262176 | tf_op jit(solution)/shard_map/all_to_all | solution.py:24
  159.6 0.9 pad_maximum_fusion
  160.5 8.1 %all-to-all-start.5 = ((bf16[32,8,1088]{2,1,0:T(8,128)(2,1)}), bf16[32,8,1088]{2,1,0:T(8,128)(2,1)S(1)}, u32[]{:S(2)}, u32[]{:S(2)}) async-start(bf16[32,8,1088]{2,1,0:T(8,128)(2,1)} %pad_maximum_fusion), calls=%async_computation.5 | async-start | bytes 1179648 | tf_op jit(solution)/shard_map/all_to_all | solution.py:172
  168.8 18.3 %all-to-all-done.5 = bf16[32,8,1088]{2,1,0:T(8,128)(2,1)S(1)} async-done(((bf16[32,8,1088]{2,1,0:T(8,128)(2,1)}), bf16[32,8,1088]{2,1,0:T(8,128)(2,1)S(1)}, u32[]{:S(2)}, u32[]{:S(2)}) %all-to-all-start.5) | async-done | bytes 557088 | tf_op jit(solution)/shard_map/all_to_all | solution.py:172
  188.1 0.7 fusion.10
  (76 shorter events, 7.8 us)
Async XLA Ops:
  7.2 99.9 %all-gather.4.cloned.1.call-start = ((), (), s32[]{:S(2)}) async-start(), calls=%async_computation.6 | async-start | bytes 4456448 | tf_op jit(solution)/shard_map/all_gather | solution.py:126
  17.3 16.6 %all-to-all-start = ((f32[16,1,1024]{2,1,0:T(1,128)}), f32[16,1,1024]{2,1,0:T(1,128)S(1)}, u32[]{:S(2)}, u32[]{:S(2)}) async-start(f32[16,1,1024]{2,1,0:T(1,128)} %reshape.216), calls=%async_computation | async-start | bytes 131072 | tf_op jit(solution)/shard_map/all_to_all | solution.py:151
  26.0 28.7 %collective-permute-start = (bf16[4,8,2048]{2,1,0:T(8,128)(2,1)S(1)}, bf16[4,8,2048]{2,1,0:T(8,128)(2,1)S(1)}, u32[]{:S(2)}, u32[]{:S(2)}) collective-permute-start(bf16[4,8,2048]{2,1,0:T(8,128)(2,1)S(1)} %bitcast.87), channel_id=1, source_target_pairs={{0,32},{32,0},{1,33},{33,1},{2,34},{34,2},{3,35},{35,3},{4,36},{36... | collective-permute-start | bytes 393224 | tf_op jit(solution)/shard_map/ppermute | solution.py:124
  35.8 1.1 copy-start.7
  35.8 1.1 copy-start.8
  37.8 16.9 %copy-start.4 = (bf16[8,4,2048]{2,1,0:T(4,128)(2,1)S(1)}, bf16[8,4,2048]{2,1,0:T(4,128)(2,1)}, u32[]{:S(2)}) copy-start(bf16[8,4,2048]{2,1,0:T(4,128)(2,1)} %param.5) | copy-start | bytes 393220
  39.0 26.1 %all-to-all-start.1 = ((f32[32,1,512]{2,1,0:T(1,128)}), f32[32,1,512]{2,1,0:T(1,128)S(1)}, u32[]{:S(2)}, u32[]{:S(2)}) async-start(f32[32,1,512]{2,1,0:T(1,128)} %copy.114), calls=%async_computation.1 | async-start | bytes 131072 | tf_op jit(solution)/shard_map/all_to_all | solution.py:17
  54.8 32.0 %copy-start = (bf16[1,2,4,8,2048]{4,3,2,1,0:T(8,128)(2,1)}, bf16[1,2,4,8,2048]{4,3,2,1,0:T(8,128)(2,1)S(1)}, u32[]{:S(2)}) copy-start(bf16[1,2,4,8,2048]{4,3,2,1,0:T(8,128)(2,1)S(1)} %maximum_bitcast_fusion.refs_0_) | copy-start | bytes 786436
  54.8 15.6 %collective-permute-start.1 = (bf16[1,2,4,8,2048]{4,3,2,1,0:T(8,128)(2,1)S(1)}, bf16[1,2,4,8,2048]{4,3,2,1,0:T(8,128)(2,1)S(1)}, u32[]{:S(2)}, u32[]{:S(2)}) collective-permute-start(bf16[1,2,4,8,2048]{4,3,2,1,0:T(8,128)(2,1)S(1)} %maximum_bitcast_fusion.refs_0_), channel_id=1, source_target_pairs={{0,256},{64,320},{128,384},{192,448},{256,0},{320,64},{384,128},{4... | collective-permute-start | bytes 786440 | tf_op jit(solution)/shard_map/ppermute | solution.py:133
  70.4 36.7 %copy-start.3 = (bf16[1,2,4,8,2048]{4,3,2,1,0:T(8,128)(2,1)}, bf16[1,2,4,8,2048]{4,3,2,1,0:T(8,128)(2,1)S(1)}, u32[]{:S(2)}) copy-start(bf16[1,2,4,8,2048]{4,3,2,1,0:T(8,128)(2,1)S(1)} %collective-permute-done.1.refs_1_) | copy-start | bytes 786436
  70.5 36.6 %collective-permute-start.4 = (bf16[2,2,4,8,2048]{4,3,2,1,0:T(8,128)(2,1)S(1)}, bf16[2,2,4,8,2048]{4,3,2,1,0:T(8,128)(2,1)S(1)}, u32[]{:S(2)}, u32[]{:S(2)}) collective-permute-start(bf16[2,2,4,8,2048]{4,3,2,1,0:T(8,128)(2,1)S(1)} %pad_maximum_fusion.1), channel_id=1, source_target_pairs={{0,64},{64,128},{128,192},{192,256},{256,320},{320,384},{384,448},... | collective-permute-start | bytes 1572872 | tf_op jit(solution)/shard_map/ppermute | solution.py:133
  76.4 30.6 %collective-permute-start.5 = (bf16[2,2,4,8,2048]{4,3,2,1,0:T(8,128)(2,1)S(1)}, bf16[2,2,4,8,2048]{4,3,2,1,0:T(8,128)(2,1)S(1)}, u32[]{:S(2)}, u32[]{:S(2)}) collective-permute-start(bf16[2,2,4,8,2048]{4,3,2,1,0:T(8,128)(2,1)S(1)} %pad_maximum_fusion.1), channel_id=1, source_target_pairs={{0,448},{64,0},{128,64},{192,128},{256,192},{320,256},{384,320},{4... | collective-permute-start | bytes 1572872 | tf_op jit(solution)/shard_map/ppermute | solution.py:133
  79.2 27.8 %all-to-all-start.2 = ((bf16[16,32,256]{2,1,0:T(8,128)(2,1)}), bf16[16,32,256]{2,1,0:T(8,128)(2,1)S(1)}, u32[]{:S(2)}, u32[]{:S(2)}) async-start(bf16[16,32,256]{2,1,0:T(8,128)(2,1)} %broadcast_in_dim.12), calls=%async_computation.2 | async-start | bytes 524288 | tf_op jit(solution)/shard_map/all_to_all | solution.py:24
  82.7 22.0 %collective-permute-start.2 = (bf16[1,2,4,8,2048]{4,3,2,1,0:T(8,128)(2,1)S(1)}, bf16[1,2,4,8,2048]{4,3,2,1,0:T(8,128)(2,1)S(1)}, u32[]{:S(2)}, u32[]{:S(2)}) collective-permute-start(bf16[1,2,4,8,2048]{4,3,2,1,0:T(8,128)(2,1)S(1)} %maximum_bitcast_fusion.refs_0_), channel_id=1, source_target_pairs={{0,128},{64,192},{128,256},{192,320},{256,384},{320,448},{384,0},{... | collective-permute-start | bytes 786440 | tf_op jit(solution)/shard_map/ppermute | solution.py:133
  86.8 20.2 %collective-permute-start.3 = (bf16[1,2,4,8,2048]{4,3,2,1,0:T(8,128)(2,1)S(1)}, bf16[1,2,4,8,2048]{4,3,2,1,0:T(8,128)(2,1)S(1)}, u32[]{:S(2)}, u32[]{:S(2)}) collective-permute-start(bf16[1,2,4,8,2048]{4,3,2,1,0:T(8,128)(2,1)S(1)} %maximum_bitcast_fusion.refs_0_), channel_id=1, source_target_pairs={{0,384},{64,448},{128,0},{192,64},{256,128},{320,192},{384,256},{4... | collective-permute-start | bytes 786440 | tf_op jit(solution)/shard_map/ppermute | solution.py:133
  104.7 2.4 %copy-start.9 = (bf16[1,2,4,8,2048]{4,3,2,1,0:T(8,128)(2,1)}, bf16[1,2,4,8,2048]{4,3,2,1,0:T(8,128)(2,1)S(1)}, u32[]{:S(2)}) copy-start(bf16[1,2,4,8,2048]{4,3,2,1,0:T(8,128)(2,1)S(1)} %collective-permute-done.2.refs_2_) | copy-start | bytes 786436
  107.0 0.7 copy-start.10
  107.0 0.8 copy-start.2
  107.0 1.0 copy-start.5
  107.0 1.2 copy-start.6
  108.2 19.0 %copy-start.12 = (f32[128]{0:T(128)S(1)}, f32[128]{0:T(128)}, u32[]{:S(2)}) copy-start(f32[128]{0:T(128)} %param.9) | copy-start | bytes 1540
  108.2 19.3 %copy-start.11 = (f32[32]{0:T(128)S(1)}, f32[32]{0:T(128)}, u32[]{:S(2)}) copy-start(f32[32]{0:T(128)} %param.8) | copy-start | bytes 388
  115.6 28.4 %all-to-all-start.3 = ((bf16[32,32,256]{2,1,0:T(8,128)(2,1)}), bf16[32,32,256]{2,1,0:T(8,128)(2,1)S(1)}, u32[]{:S(2)}, u32[]{:S(2)}) async-start(bf16[32,32,256]{2,1,0:T(8,128)(2,1)} %bitcast.90), calls=%async_computation.3 | async-start | bytes 1048576 | tf_op jit(solution)/shard_map/all_to_all | solution.py:160
  127.7 31.5 %copy-start.1 = (bf16[512,1024]{1,0:T(8,128)(2,1)S(1)}, bf16[512,1024]{1,0:T(8,128)(2,1)}, u32[]{:S(2)}) copy-start(bf16[512,1024]{1,0:T(8,128)(2,1)} %get-tuple-element.5) | copy-start | bytes 3145732
  144.9 14.3 %all-to-all-start.4 = ((bf16[16,32,256]{2,1,0:T(8,128)(2,1)}), bf16[16,32,256]{2,1,0:T(8,128)(2,1)S(1)}, u32[]{:S(2)}, u32[]{:S(2)}) async-start(bf16[16,32,256]{2,1,0:T(8,128)(2,1)} %broadcast_in_dim.14), calls=%async_computation.4 | async-start | bytes 524288 | tf_op jit(solution)/shard_map/all_to_all | solution.py:24
  160.5 26.6 %all-to-all-start.5 = ((bf16[32,8,1088]{2,1,0:T(8,128)(2,1)}), bf16[32,8,1088]{2,1,0:T(8,128)(2,1)S(1)}, u32[]{:S(2)}, u32[]{:S(2)}) async-start(bf16[32,8,1088]{2,1,0:T(8,128)(2,1)} %pad_maximum_fusion), calls=%async_computation.5 | async-start | bytes 1179648 | tf_op jit(solution)/shard_map/all_to_all | solution.py:172
Sparse Core Ops, SparseCore 0:
  15.0 52.6 all-gather.3

commit v6 on v5

--- a/solution.py
+++ b/solution.py
@@ -28,9 +28,9 @@
 SHIFTS = ((0,), (4,), (2,), (-2,), (1, 5), (-1, 3))
 
 
-def tile_kernel(y_ref, left_ref, inward_ref, *refs):
+def tile_kernel(at_ref, left_ref, inward_ref, *refs):
     n_blocks = len(SHIFTS)
-    block_refs, (tiles_ref, message_ref, piece_ref, gram_ref, tile_ref, sum_ref) = refs[:n_blocks], refs[n_blocks:]
+    block_refs, (tiles_ref, kept_ref, sent_ref, piece_ref, gram_ref, tile_ref, sum_ref) = refs[:n_blocks], refs[n_blocks:]
     n_z, n_k, n_xh, block, aux_width = left_ref.shape
     a_local = 8
     rows = n_z * n_k * n_xh * block
@@ -41,7 +41,7 @@
     def _():
         for shifts, block_ref in zip(SHIFTS, block_refs):
             for slot, shift in enumerate(shifts):
-                y = (y_ref[0] + n_y - shift) % n_y
+                y = (at_ref[0] + n_y - shift) % n_y
                 for d in range(d_local):
                     for xl in range(n_xl):
                         rows_at = slice(xl * b_local, (xl + 1) * b_local)
@@ -73,15 +73,21 @@
             at = pl.ds(a, LANES, stride=a_local)
             before = sum_ref[half, at, :]
             sum_ref[half, at, :] = jnp.where(first, out, before + out)
-        message_ref[:, lanes] = sum_ref[half].astype(jnp.bfloat16)
-
-
-def tiles_and_ladder(y_index, left, inward, blocks):
+        n_groups, size, _ = kept_ref.shape
+        for group in range(n_groups):
+            own = pl.multiple_of((2 * group + at_ref[1]) * size, size)
+            other = pl.multiple_of((2 * group + 1 - at_ref[1]) * size, size)
+            kept_ref[group, :, lanes] = sum_ref[half, pl.ds(own, size), :]
+            sent_ref[group, :, lanes] = sum_ref[half, pl.ds(other, size), :].astype(jnp.bfloat16)
+
+
+def tiles_and_ladder(place, left, inward, blocks):
     n_z, n_k, n_xh, block, aux_width = left.shape
     steps = 2
     contracted = inward.shape[0]
     wide = 8 * LANES
     part = contracted // steps
+    halves = (n_z * n_xh, wide // (n_z * n_xh * n_k), inward.shape[1])
     _, n_xl, d_local, b_local, _ = blocks[0].shape
     n_y = sum(block.shape[0] for block in blocks)
     return pl.pallas_call(
@@ -95,11 +101,13 @@
         + [pl.BlockSpec(block.shape, lambda s: (0,) * 5, pipeline_mode=pl.Buffered(1)) for block in blocks],
         out_specs=[
             pl.BlockSpec((part, wide), lambda s: (s, 0)),
-            pl.BlockSpec((wide, inward.shape[1]), lambda s: (0, 0)),
+            pl.BlockSpec(halves, lambda s: (0, 0, 0)),
+            pl.BlockSpec(halves, lambda s: (0, 0, 0)),
         ],
         out_shape=[
             jax.ShapeDtypeStruct((contracted, wide), jnp.bfloat16),
-            jax.ShapeDtypeStruct((wide, inward.shape[1]), jnp.bfloat16),
+            jax.ShapeDtypeStruct(halves, jnp.float32),
+            jax.ShapeDtypeStruct(halves, jnp.bfloat16),
         ],
         scratch_shapes=[
             pltpu.VMEM((d_local, n_y, n_xl * b_local, aux_width), jnp.bfloat16),
@@ -108,7 +116,7 @@
             pltpu.VMEM((2, wide, LANES), jnp.float32),
         ],
         name="tiles_and_ladder",
-    )(y_index.reshape(1), left, inward, *blocks)
+    )(place, left, inward, *blocks)
 
 
 def local(factors, amplitudes, driving, occ_energy, vir_energy):
@@ -156,8 +164,10 @@
     current, drive = blocks[0], blocks[1]
     inward = spread(current.astype(jnp.bfloat16), n_ab)
 
-    tiles, first = tiles_and_ladder(lax.axis_index("y"), left, inward, y_blocks)
-    parts = lax.all_to_all(first.reshape(n_cd, -1, pairs), CD, 0, 0, tiled=True)
+    place = jnp.stack([lax.axis_index("y"), lax.axis_index("k")])
+    tiles, kept, sent = tiles_and_ladder(place, left, inward, y_blocks)
+    chip = kept + lax.ppermute(sent, "k", [(0, 1), (1, 0)]).astype(jnp.float32)
+    parts = lax.all_to_all(chip.astype(jnp.bfloat16), CD[:2], 0, 0, tiled=True)
     ladder = jnp.sum(parts.astype(jnp.float32), axis=0)
     current = current - (drive + denom_block * current + ladder) / denom_block
 

time: 196 us -> 196 us (level)
  waiting for transfers between devices: 78.8 us -> 72.4 us
  starting transfers between devices: 72.4 us -> 75.7 us
  other arithmetic: 3.92 us -> 6.34 us
    ppermute x0 -> x1, starting transfers between devices: none -> 7.2 us  [local(): chip = kept + lax.ppermute(sent, 'k', [(0, 1), (1, 0)]).astype(jnp.float32)]
    all_to_all x1, waiting for transfers between devices: 16.1 us -> 11.7 us  [local(): parts = lax.all_to_all(chip.astype(jnp.bfloat16), CD[:2], 0, 0, tiled=True)]
    ppermute x5, waiting for transfers between devices: 21.9 us -> 18.9 us  [shifted(): lax.ppermute(value, 'y', [(i, (i + shift) % n_y) for i in range(n_y)])]
    all_to_all x1, starting transfers between devices: 11.6 us -> 9.06 us  [local(): parts = lax.all_to_all(chip.astype(jnp.bfloat16), CD[:2], 0, 0, tiled=True)]
  transfers between devices with their start and end apart: 13 -> 14, of which waited for: 8 -> 9; matrix products, arithmetic and copies ran while one was open for 5% -> 5% of each run, Pallas kernels for 0% -> 0%
where the time goes in v6:
time: 196 us; the launch traced here: 195 us
  starting transfers between devices  75.7 us (39%)
  waiting for transfers between devices  72.4 us (37%)
  between operations  14.5 us (7%)
  local copies, waits for them, and re-layouts  11.5 us (6%)
  Pallas kernels  7.71 us (4%)
  blocking collectives  6.68 us (3%)
  other arithmetic  6.34 us (3%)
    ppermute x5, waiting for transfers between devices, shifted(): lax.ppermute(value, 'y', [(i, (i + shift) % n_y) for i in range(n_y)])  18.9 us
    all_to_all x1, waiting for transfers between devices, local(): parts = lax.all_to_all(message, CD, 0, 0, tiled=True)  18.3 us
    ppermute x5, starting transfers between devices, shifted(): lax.ppermute(value, 'y', [(i, (i + shift) % n_y) for i in range(n_y)])  17.4 us
    all_to_all x1, starting transfers between devices, pair_layout(): swapped = lax.all_to_all(split.reshape(n_cd, -1), CD, 0, 0, tiled=True)  15.6 us
    all_to_all x1, waiting for transfers between devices, local(): parts = lax.all_to_all(chip.astype(jnp.bfloat16), CD[:2], 0, 0, tiled=True)  11.7 us
    all_to_all x2, waiting for transfers between devices, spread(): lax.all_to_all(copies, AB, 0, 0, tiled=True).reshape(-1, block.shape[1])  9.43 us
    all_to_all x1, starting transfers between devices, local(): parts = lax.all_to_all(chip.astype(jnp.bfloat16), CD[:2], 0, 0, tiled=True)  9.06 us
    all_to_all x1, starting transfers between devices, local(): mirror = lax.all_to_all(both, AB, split_axis=3, concat_axis=2, tiled=True)  8.65 us
  transfers between devices with their start and end apart: 14, of which 9 were waited for; matrix products, arithmetic and copies ran while one was open for 5% of the time, Pallas kernels for 0%

profile of v6, /device:TPU:1, one launch (start us, length us, event | category | flops | bytes accessed | tf_op | source)
XLA Modules:
  0.0 195.3 jit_solution(11917080888781124024)
XLA Ops:
  7.2 1.0 copy.138
  8.2 6.7 %all-gather = bf16[8,8,2048]{2,1,0:T(8,128)(2,1)} all-gather(bf16[4,8,2048]{2,1,0:T(8,128)(2,1)S(1)} %bitcast.86), channel_id=2, replica_groups=mesh['y'=8,'xl'=2,'z'=8,'xh'=2,'k'=2] {'xh'}, dimensions={0}, use_global_device_ids=true | all-gather | bytes 393216 | tf_op jit(solution)/shard_map/all_gather | solution.py:133
  14.9 0.8 pad_maximum_fusion.2
  16.2 1.2 reshape.208
  17.3 8.6 %all-to-all-start = ((f32[16,1,1024]{2,1,0:T(1,128)}), f32[16,1,1024]{2,1,0:T(1,128)S(1)}, u32[]{:S(2)}, u32[]{:S(2)}) async-start(f32[16,1,1024]{2,1,0:T(1,128)} %reshape.208), calls=%async_computation | async-start | bytes 131072 | tf_op jit(solution)/shard_map/all_to_all | solution.py:159
  26.0 3.3 %collective-permute-start = (bf16[4,8,2048]{2,1,0:T(8,128)(2,1)S(1)}, bf16[4,8,2048]{2,1,0:T(8,128)(2,1)S(1)}, u32[]{:S(2)}, u32[]{:S(2)}) collective-permute-start(bf16[4,8,2048]{2,1,0:T(8,128)(2,1)S(1)} %bitcast.87), channel_id=1, source_target_pairs={{0,32},{32,0},{1,33},{33,1},{2,34},{34,2},{3,35},{35,3},{4,36},{36... | collective-permute-start | bytes 393224 | tf_op jit(solution)/shard_map/ppermute | solution.py:132
  29.3 4.6 %all-to-all-done = f32[16,1,1024]{2,1,0:T(1,128)S(1)} async-done(((f32[16,1,1024]{2,1,0:T(1,128)}), f32[16,1,1024]{2,1,0:T(1,128)S(1)}, u32[]{:S(2)}, u32[]{:S(2)}) %all-to-all-start) | async-done | bytes 65568 | tf_op jit(solution)/shard_map/all_to_all | solution.py:159
  34.4 0.8 reduce
  39.0 15.6 %all-to-all-start.1 = ((f32[32,1,512]{2,1,0:T(1,128)}), f32[32,1,512]{2,1,0:T(1,128)S(1)}, u32[]{:S(2)}, u32[]{:S(2)}) async-start(f32[32,1,512]{2,1,0:T(1,128)} %copy.114), calls=%async_computation.1 | async-start | bytes 131072 | tf_op jit(solution)/shard_map/all_to_all | solution.py:17
  54.8 2.3 %collective-permute-start.1 = (bf16[1,2,4,8,2048]{4,3,2,1,0:T(8,128)(2,1)S(1)}, bf16[1,2,4,8,2048]{4,3,2,1,0:T(8,128)(2,1)S(1)}, u32[]{:S(2)}, u32[]{:S(2)}) collective-permute-start(bf16[1,2,4,8,2048]{4,3,2,1,0:T(8,128)(2,1)S(1)} %maximum_bitcast_fusion.refs_0_), channel_id=1, source_target_pairs={{0,256},{64,320},{128,384},{192,448},{256,0},{320,64},{384,128},{4... | collective-permute-start | bytes 786440 | tf_op jit(solution)/shard_map/ppermute | solution.py:141
  57.1 8.0 %all-to-all-done.1 = f32[32,1,512]{2,1,0:T(1,128)S(1)} async-done(((f32[32,1,512]{2,1,0:T(1,128)}), f32[32,1,512]{2,1,0:T(1,128)S(1)}, u32[]{:S(2)}, u32[]{:S(2)}) %all-to-all-start.1) | async-done | bytes 65568 | tf_op jit(solution)/shard_map/all_to_all | solution.py:17
  65.4 5.0 %collective-permute-done.1.refs_1_ = bf16[1,2,4,8,2048]{4,3,2,1,0:T(8,128)(2,1)S(1)} collective-permute-done((bf16[1,2,4,8,2048]{4,3,2,1,0:T(8,128)(2,1)S(1)}, bf16[1,2,4,8,2048]{4,3,2,1,0:T(8,128)(2,1)S(1)}, u32[]{:S(2)}, u32[]{:S(2)}) %collective-permute-start.1) | collective-permute-done | bytes 262176 | tf_op jit(solution)/shard_map/ppermute | solution.py:141
  70.5 2.1 %collective-permute-start.5 = (bf16[2,2,4,8,2048]{4,3,2,1,0:T(8,128)(2,1)S(1)}, bf16[2,2,4,8,2048]{4,3,2,1,0:T(8,128)(2,1)S(1)}, u32[]{:S(2)}, u32[]{:S(2)}) collective-permute-start(bf16[2,2,4,8,2048]{4,3,2,1,0:T(8,128)(2,1)S(1)} %pad_maximum_fusion.1), channel_id=1, source_target_pairs={{0,448},{64,0},{128,64},{192,128},{256,192},{320,256},{384,320},{4... | collective-permute-start | bytes 1572872 | tf_op jit(solution)/shard_map/ppermute | solution.py:141
  72.6 5.7 %collective-permute-start.4 = (bf16[2,2,4,8,2048]{4,3,2,1,0:T(8,128)(2,1)S(1)}, bf16[2,2,4,8,2048]{4,3,2,1,0:T(8,128)(2,1)S(1)}, u32[]{:S(2)}, u32[]{:S(2)}) collective-permute-start(bf16[2,2,4,8,2048]{4,3,2,1,0:T(8,128)(2,1)S(1)} %pad_maximum_fusion.1), channel_id=1, source_target_pairs={{0,64},{64,128},{128,192},{192,256},{256,320},{320,384},{384,448},... | collective-permute-start | bytes 1572872 | tf_op jit(solution)/shard_map/ppermute | solution.py:141
  78.4 0.8 broadcast_in_dim.12
  79.2 3.5 %all-to-all-start.2 = ((bf16[16,32,256]{2,1,0:T(8,128)(2,1)}), bf16[16,32,256]{2,1,0:T(8,128)(2,1)S(1)}, u32[]{:S(2)}, u32[]{:S(2)}) async-start(bf16[16,32,256]{2,1,0:T(8,128)(2,1)} %broadcast_in_dim.12), calls=%async_computation.2 | async-start | bytes 524288 | tf_op jit(solution)/shard_map/all_to_all | solution.py:24
  82.7 5.3 %collective-permute-start.3 = (bf16[1,2,4,8,2048]{4,3,2,1,0:T(8,128)(2,1)S(1)}, bf16[1,2,4,8,2048]{4,3,2,1,0:T(8,128)(2,1)S(1)}, u32[]{:S(2)}, u32[]{:S(2)}) collective-permute-start(bf16[1,2,4,8,2048]{4,3,2,1,0:T(8,128)(2,1)S(1)} %maximum_bitcast_fusion.refs_0_), channel_id=1, source_target_pairs={{0,384},{64,448},{128,0},{192,64},{256,128},{320,192},{384,256},{4... | collective-permute-start | bytes 786440 | tf_op jit(solution)/shard_map/ppermute | solution.py:141
  88.1 1.9 collective-permute-start.2
  90.6 12.1 %collective-permute-done.3.refs_3_ = bf16[1,2,4,8,2048]{4,3,2,1,0:T(8,128)(2,1)S(1)} collective-permute-done((bf16[1,2,4,8,2048]{4,3,2,1,0:T(8,128)(2,1)S(1)}, bf16[1,2,4,8,2048]{4,3,2,1,0:T(8,128)(2,1)S(1)}, u32[]{:S(2)}, u32[]{:S(2)}) %collective-permute-start.3) | collective-permute-done | bytes 262176 | tf_op jit(solution)/shard_map/ppermute | solution.py:141
  102.7 1.8 collective-permute-done.2.refs_2_
  105.8 7.7 %tiles_and_ladder.1 = (bf16[512,1024]{1,0:T(8,128)(2,1)}, f32[16,32,256]{2,1,0:T(8,128)}, bf16[16,32,256]{2,1,0:T(8,128)(2,1)}) custom-call(s32[2]{0:T(128)} %pad_add_fusion.at_ref, bf16[8,2,2,32,2048]{4,3,2,1,0:T(8,128)(2,1)} %bitcast.76, bf16[512,256]{1,0:T(8,128)(2,1)} %bitcast.85, bf16[1,2,4,8,2048]{4,3,2,1,0:T(8,128)(2,1)} %copy-done, ...), custom_call_target="tpu_custom_call" | custom-call | tf_op jit(solution)/shard_map/tiles_and_ladder/pallas_call | solution.py:93
  113.5 7.2 %collective-permute-start.6 = (bf16[16,32,256]{2,1,0:T(8,128)(2,1)}, bf16[16,32,256]{2,1,0:T(8,128)(2,1)S(1)}, u32[]{:S(2)}, u32[]{:S(2)}) collective-permute-start(bf16[16,32,256]{2,1,0:T(8,128)(2,1)} %get-tuple-element.6), channel_id=1, source_target_pairs={{0,1},{1,0},{2,3},{3,2},{4,5},{5,4},{6,7},{7,6},{8,9},{9,8},{10,11... | collective-permute-start | bytes 786440 | tf_op jit(solution)/shard_map/ppermute | solution.py:169
  120.7 1.4 collective-permute-done.6
  122.0 1.8 add_convert_fusion
  123.9 9.1 %all-to-all-start.3 = ((bf16[16,32,256]{2,1,0:T(8,128)(2,1)}), bf16[16,32,256]{2,1,0:T(8,128)(2,1)S(1)}, u32[]{:S(2)}, u32[]{:S(2)}) async-start(bf16[16,32,256]{2,1,0:T(8,128)(2,1)} %add_convert_fusion), calls=%async_computation.3 | async-start | bytes 524288 | tf_op jit(solution)/shard_map/all_to_all | solution.py:170
  133.7 11.7 %all-to-all-done.3 = bf16[16,32,256]{2,1,0:T(8,128)(2,1)S(1)} async-done(((bf16[16,32,256]{2,1,0:T(8,128)(2,1)}), bf16[16,32,256]{2,1,0:T(8,128)(2,1)S(1)}, u32[]{:S(2)}, u32[]{:S(2)}) %all-to-all-start.3) | async-done | bytes 262176 | tf_op jit(solution)/shard_map/all_to_all | solution.py:170
  145.6 0.7 broadcast_in_dim.14
  146.3 3.5 %all-to-all-start.4 = ((bf16[16,32,256]{2,1,0:T(8,128)(2,1)}), bf16[16,32,256]{2,1,0:T(8,128)(2,1)S(1)}, u32[]{:S(2)}, u32[]{:S(2)}) async-start(bf16[16,32,256]{2,1,0:T(8,128)(2,1)} %broadcast_in_dim.14), calls=%async_computation.4 | async-start | bytes 524288 | tf_op jit(solution)/shard_map/all_to_all | solution.py:24
  150.1 9.4 %all-to-all-done.4 = bf16[16,32,256]{2,1,0:T(8,128)(2,1)S(1)} async-done(((bf16[16,32,256]{2,1,0:T(8,128)(2,1)}), bf16[16,32,256]{2,1,0:T(8,128)(2,1)S(1)}, u32[]{:S(2)}, u32[]{:S(2)}) %all-to-all-start.4) | async-done | bytes 262176 | tf_op jit(solution)/shard_map/all_to_all | solution.py:24
  160.0 0.9 pad_maximum_fusion
  160.9 7.5 %all-to-all-start.5 = ((bf16[32,8,1088]{2,1,0:T(8,128)(2,1)}), bf16[32,8,1088]{2,1,0:T(8,128)(2,1)S(1)}, u32[]{:S(2)}, u32[]{:S(2)}) async-start(bf16[32,8,1088]{2,1,0:T(8,128)(2,1)} %pad_maximum_fusion), calls=%async_computation.5 | async-start | bytes 1179648 | tf_op jit(solution)/shard_map/all_to_all | solution.py:182
  168.5 18.3 %all-to-all-done.5 = bf16[32,8,1088]{2,1,0:T(8,128)(2,1)S(1)} async-done(((bf16[32,8,1088]{2,1,0:T(8,128)(2,1)}), bf16[32,8,1088]{2,1,0:T(8,128)(2,1)S(1)}, u32[]{:S(2)}, u32[]{:S(2)}) %all-to-all-start.5) | async-done | bytes 557088 | tf_op jit(solution)/shard_map/all_to_all | solution.py:182
  (80 shorter events, 10.4 us)
Async XLA Ops:
  7.2 97.5 %all-gather.4.cloned.1.call-start = ((), (), s32[]{:S(2)}) async-start(), calls=%async_computation.6 | async-start | bytes 4456448 | tf_op jit(solution)/shard_map/all_gather | solution.py:134
  17.3 16.6 %all-to-all-start = ((f32[16,1,1024]{2,1,0:T(1,128)}), f32[16,1,1024]{2,1,0:T(1,128)S(1)}, u32[]{:S(2)}, u32[]{:S(2)}) async-start(f32[16,1,1024]{2,1,0:T(1,128)} %reshape.208), calls=%async_computation | async-start | bytes 131072 | tf_op jit(solution)/shard_map/all_to_all | solution.py:159
  26.0 28.7 %collective-permute-start = (bf16[4,8,2048]{2,1,0:T(8,128)(2,1)S(1)}, bf16[4,8,2048]{2,1,0:T(8,128)(2,1)S(1)}, u32[]{:S(2)}, u32[]{:S(2)}) collective-permute-start(bf16[4,8,2048]{2,1,0:T(8,128)(2,1)S(1)} %bitcast.87), channel_id=1, source_target_pairs={{0,32},{32,0},{1,33},{33,1},{2,34},{34,2},{3,35},{35,3},{4,36},{36... | collective-permute-start | bytes 393224 | tf_op jit(solution)/shard_map/ppermute | solution.py:132
  35.8 1.1 copy-start.7
  35.8 1.1 copy-start.8
  37.8 16.9 %copy-start.4 = (bf16[8,4,2048]{2,1,0:T(4,128)(2,1)S(1)}, bf16[8,4,2048]{2,1,0:T(4,128)(2,1)}, u32[]{:S(2)}) copy-start(bf16[8,4,2048]{2,1,0:T(4,128)(2,1)} %param.5) | copy-start | bytes 393220
  39.0 26.1 %all-to-all-start.1 = ((f32[32,1,512]{2,1,0:T(1,128)}), f32[32,1,512]{2,1,0:T(1,128)S(1)}, u32[]{:S(2)}, u32[]{:S(2)}) async-start(f32[32,1,512]{2,1,0:T(1,128)} %copy.114), calls=%async_computation.1 | async-start | bytes 131072 | tf_op jit(solution)/shard_map/all_to_all | solution.py:17
  54.8 33.3 %copy-start = (bf16[1,2,4,8,2048]{4,3,2,1,0:T(8,128)(2,1)}, bf16[1,2,4,8,2048]{4,3,2,1,0:T(8,128)(2,1)S(1)}, u32[]{:S(2)}) copy-start(bf16[1,2,4,8,2048]{4,3,2,1,0:T(8,128)(2,1)S(1)} %maximum_bitcast_fusion.refs_0_) | copy-start | bytes 786436
  54.8 15.6 %collective-permute-start.1 = (bf16[1,2,4,8,2048]{4,3,2,1,0:T(8,128)(2,1)S(1)}, bf16[1,2,4,8,2048]{4,3,2,1,0:T(8,128)(2,1)S(1)}, u32[]{:S(2)}, u32[]{:S(2)}) collective-permute-start(bf16[1,2,4,8,2048]{4,3,2,1,0:T(8,128)(2,1)S(1)} %maximum_bitcast_fusion.refs_0_), channel_id=1, source_target_pairs={{0,256},{64,320},{128,384},{192,448},{256,0},{320,64},{384,128},{4... | collective-permute-start | bytes 786440 | tf_op jit(solution)/shard_map/ppermute | solution.py:141
  70.4 34.2 %copy-start.3 = (bf16[1,2,4,8,2048]{4,3,2,1,0:T(8,128)(2,1)}, bf16[1,2,4,8,2048]{4,3,2,1,0:T(8,128)(2,1)S(1)}, u32[]{:S(2)}) copy-start(bf16[1,2,4,8,2048]{4,3,2,1,0:T(8,128)(2,1)S(1)} %collective-permute-done.1.refs_1_) | copy-start | bytes 786436
  70.5 34.1 %collective-permute-start.5 = (bf16[2,2,4,8,2048]{4,3,2,1,0:T(8,128)(2,1)S(1)}, bf16[2,2,4,8,2048]{4,3,2,1,0:T(8,128)(2,1)S(1)}, u32[]{:S(2)}, u32[]{:S(2)}) collective-permute-start(bf16[2,2,4,8,2048]{4,3,2,1,0:T(8,128)(2,1)S(1)} %pad_maximum_fusion.1), channel_id=1, source_target_pairs={{0,448},{64,0},{128,64},{192,128},{256,192},{320,256},{384,320},{4... | collective-permute-start | bytes 1572872 | tf_op jit(solution)/shard_map/ppermute | solution.py:141
  72.6 32.0 %collective-permute-start.4 = (bf16[2,2,4,8,2048]{4,3,2,1,0:T(8,128)(2,1)S(1)}, bf16[2,2,4,8,2048]{4,3,2,1,0:T(8,128)(2,1)S(1)}, u32[]{:S(2)}, u32[]{:S(2)}) collective-permute-start(bf16[2,2,4,8,2048]{4,3,2,1,0:T(8,128)(2,1)S(1)} %pad_maximum_fusion.1), channel_id=1, source_target_pairs={{0,64},{64,128},{128,192},{192,256},{256,320},{320,384},{384,448},... | collective-permute-start | bytes 1572872 | tf_op jit(solution)/shard_map/ppermute | solution.py:141
  79.2 25.4 %all-to-all-start.2 = ((bf16[16,32,256]{2,1,0:T(8,128)(2,1)}), bf16[16,32,256]{2,1,0:T(8,128)(2,1)S(1)}, u32[]{:S(2)}, u32[]{:S(2)}) async-start(bf16[16,32,256]{2,1,0:T(8,128)(2,1)} %broadcast_in_dim.12), calls=%async_computation.2 | async-start | bytes 524288 | tf_op jit(solution)/shard_map/all_to_all | solution.py:24
  82.7 20.0 %collective-permute-start.3 = (bf16[1,2,4,8,2048]{4,3,2,1,0:T(8,128)(2,1)S(1)}, bf16[1,2,4,8,2048]{4,3,2,1,0:T(8,128)(2,1)S(1)}, u32[]{:S(2)}, u32[]{:S(2)}) collective-permute-start(bf16[1,2,4,8,2048]{4,3,2,1,0:T(8,128)(2,1)S(1)} %maximum_bitcast_fusion.refs_0_), channel_id=1, source_target_pairs={{0,384},{64,448},{128,0},{192,64},{256,128},{320,192},{384,256},{4... | collective-permute-start | bytes 786440 | tf_op jit(solution)/shard_map/ppermute | solution.py:141
  88.1 16.5 %collective-permute-start.2 = (bf16[1,2,4,8,2048]{4,3,2,1,0:T(8,128)(2,1)S(1)}, bf16[1,2,4,8,2048]{4,3,2,1,0:T(8,128)(2,1)S(1)}, u32[]{:S(2)}, u32[]{:S(2)}) collective-permute-start(bf16[1,2,4,8,2048]{4,3,2,1,0:T(8,128)(2,1)S(1)} %maximum_bitcast_fusion.refs_0_), channel_id=1, source_target_pairs={{0,128},{64,192},{128,256},{192,320},{256,384},{320,448},{384,0},{... | collective-permute-start | bytes 786440 | tf_op jit(solution)/shard_map/ppermute | solution.py:141
  102.7 1.9 copy-start.9
  104.6 0.7 copy-start.10
  104.6 0.8 copy-start.2
  104.6 1.0 copy-start.5
  104.6 1.2 copy-start.6
  113.5 19.5 %copy-start.12 = (f32[128]{0:T(128)S(1)}, f32[128]{0:T(128)}, u32[]{:S(2)}) copy-start(f32[128]{0:T(128)} %param.9) | copy-start | bytes 1540
  113.5 19.8 %copy-start.11 = (f32[32]{0:T(128)S(1)}, f32[32]{0:T(128)}, u32[]{:S(2)}) copy-start(f32[32]{0:T(128)} %param.8) | copy-start | bytes 388
  113.5 8.6 %collective-permute-start.6 = (bf16[16,32,256]{2,1,0:T(8,128)(2,1)}, bf16[16,32,256]{2,1,0:T(8,128)(2,1)S(1)}, u32[]{:S(2)}, u32[]{:S(2)}) collective-permute-start(bf16[16,32,256]{2,1,0:T(8,128)(2,1)} %get-tuple-element.6), channel_id=1, source_target_pairs={{0,1},{1,0},{2,3},{3,2},{4,5},{5,4},{6,7},{7,6},{8,9},{9,8},{10,11... | collective-permute-start | bytes 786440 | tf_op jit(solution)/shard_map/ppermute | solution.py:169
  123.9 21.6 %all-to-all-start.3 = ((bf16[16,32,256]{2,1,0:T(8,128)(2,1)}), bf16[16,32,256]{2,1,0:T(8,128)(2,1)S(1)}, u32[]{:S(2)}, u32[]{:S(2)}) async-start(bf16[16,32,256]{2,1,0:T(8,128)(2,1)} %add_convert_fusion), calls=%async_computation.3 | async-start | bytes 524288 | tf_op jit(solution)/shard_map/all_to_all | solution.py:170
  133.0 26.6 %copy-start.1 = (bf16[512,1024]{1,0:T(8,128)(2,1)S(1)}, bf16[512,1024]{1,0:T(8,128)(2,1)}, u32[]{:S(2)}) copy-start(bf16[512,1024]{1,0:T(8,128)(2,1)} %get-tuple-element.7) | copy-start | bytes 3145732
  146.3 13.2 %all-to-all-start.4 = ((bf16[16,32,256]{2,1,0:T(8,128)(2,1)}), bf16[16,32,256]{2,1,0:T(8,128)(2,1)S(1)}, u32[]{:S(2)}, u32[]{:S(2)}) async-start(bf16[16,32,256]{2,1,0:T(8,128)(2,1)} %broadcast_in_dim.14), calls=%async_computation.4 | async-start | bytes 524288 | tf_op jit(solution)/shard_map/all_to_all | solution.py:24
  160.9 25.9 %all-to-all-start.5 = ((bf16[32,8,1088]{2,1,0:T(8,128)(2,1)}), bf16[32,8,1088]{2,1,0:T(8,128)(2,1)S(1)}, u32[]{:S(2)}, u32[]{:S(2)}) async-start(bf16[32,8,1088]{2,1,0:T(8,128)(2,1)} %pad_maximum_fusion), calls=%async_computation.5 | async-start | bytes 1179648 | tf_op jit(solution)/shard_map/all_to_all | solution.py:182
Sparse Core Ops, SparseCore 0:
  15.0 52.6 all-gather.3

commit v7 on v6

--- a/solution.py
+++ b/solution.py
@@ -10,13 +10,11 @@
 CD = ("z", "xh", "k")
 
 
-def pair_layout(stacked, n_cd):
-    count, rows, a_local, virtuals = stacked.shape
-    width = virtuals // n_cd
-    split = stacked.reshape(count, rows, a_local, n_cd, width).transpose(3, 0, 4, 2, 1)
-    swapped = lax.all_to_all(split.reshape(n_cd, -1), CD, 0, 0, tiled=True)
-    swapped = swapped.reshape(n_cd, count, width * a_local, rows).transpose(1, 2, 0, 3)
-    return swapped.reshape(count, width * a_local, n_cd * rows)
+def pair_layout(messages, count, rows):
+    n_cd = messages.shape[0]
+    swapped = lax.all_to_all(messages, CD, 0, 0, tiled=True)
+    swapped = swapped.reshape(n_cd, count, -1, rows).transpose(1, 2, 0, 3)
+    return swapped.reshape(count, -1, n_cd * rows)
 
 
 def spread(block, n_ab):
@@ -130,7 +128,9 @@
 
     turned = factors.transpose(1, 0, 2)
     theirs = lax.ppermute(turned, "xl", [(0, 1), (1, 0)])
-    columns = lax.all_gather(turned[None], "xh", axis=0, tiled=True)
+    across = lax.ppermute(turned, "xh", [(0, 1), (1, 0)])
+    low_member = lax.axis_index("xh") == 0
+    columns = jnp.stack([jnp.where(low_member, turned, across), jnp.where(low_member, across, turned)])
     left = lax.all_gather(columns[None], ("z", "k"), axis=0, tiled=True)
     left = left.reshape(n_z, n_k, n_xh, d_local * a_local, aux_width)
     even_member = lax.axis_index("xl") == 0
@@ -155,12 +155,12 @@
     denom_block = vir_block - occ_pairs[None, :]
 
     rounded = amplitudes.astype(jnp.bfloat16).astype(jnp.float32)
-    both = jnp.stack([amplitudes, driving])
-    mirror = lax.all_to_all(both, AB, split_axis=3, concat_axis=2, tiled=True)
-    mirror = mirror.transpose(0, 1, 3, 2)
-    rounded_mirror = mirror[0].astype(jnp.bfloat16).astype(jnp.float32)
-    even = 0.5 * jnp.stack([rounded + rounded_mirror, both[1] + mirror[1]])
-    blocks = pair_layout(even, n_cd)
+    both = jnp.stack([rounded, driving])
+    own = both.reshape(2, rows, a_local, n_cd, d_local).transpose(3, 0, 4, 2, 1).reshape(n_cd, -1, 128)
+    outgoing = both.reshape(2, rows, n_cd // n_ab, d_local, n_ab, a_local).transpose(4, 2, 0, 3, 5, 1)
+    mirror = lax.all_to_all(outgoing.reshape(n_ab, -1, 128), AB, 0, 0, tiled=True)
+    even = 0.5 * (own + mirror.reshape(own.shape))
+    blocks = pair_layout(even, 2, rows)
     current, drive = blocks[0], blocks[1]
     inward = spread(current.astype(jnp.bfloat16), n_ab)
 

time: 196 us -> 196 us (level)
  blocking collectives: 6.68 us -> 0 us
  waiting for transfers between devices: 72.4 us -> 77.6 us
  starting transfers between devices: 75.7 us -> 79.4 us
  local copies, waits for them, and re-layouts: 11.5 us -> 9.46 us
    all_gather x1 -> x0, blocking collectives: 6.68 us -> none  [local(): columns = lax.all_gather(turned[None], 'xh', axis=0, tiled=True)]
    ppermute x0 -> x1, starting transfers between devices: none -> 4.36 us  [local(): across = lax.ppermute(turned, 'xh', [(0, 1), (1, 0)])]
    ppermute x0 -> x1, waiting for transfers between devices: none -> 3.2 us  [local(): across = lax.ppermute(turned, 'xh', [(0, 1), (1, 0)])]
    all_to_all x5 -> x1, local copies, waits for them, and re-layouts: 2.48 us -> 0.13 us  [pair_layout(): swapped = lax.all_to_all(messages, CD, 0, 0, tiled=True)]
    unnamed x30 -> x27, local copies, waits for them, and re-layouts: 4 us -> 2.51 us
  transfers between devices with their start and end apart: 14 -> 15, of which waited for: 9 -> 10; matrix products, arithmetic and copies ran while one was open for 5% -> 3% of each run, Pallas kernels for 0% -> 0%
where the time goes in v7:
time: 196 us
  starting transfers between devices  79.4 us (41%)
  waiting for transfers between devices  77.6 us (40%)
  between operations  14.5 us (7%)
  local copies, waits for them, and re-layouts  9.46 us (5%)
  Pallas kernels  7.7 us (4%)
  other arithmetic  6.43 us (3%)
    ppermute x5, waiting for transfers between devices, shifted(): lax.ppermute(value, 'y', [(i, (i + shift) % n_y) for i in range(n_y)])  19.1 us
    all_to_all x1, waiting for transfers between devices, local(): parts = lax.all_to_all(message, CD, 0, 0, tiled=True)  18.3 us
    ppermute x5, starting transfers between devices, shifted(): lax.ppermute(value, 'y', [(i, (i + shift) % n_y) for i in range(n_y)])  17.4 us
    all_to_all x1, starting transfers between devices, pair_layout(): swapped = lax.all_to_all(messages, CD, 0, 0, tiled=True)  15.3 us
    all_to_all x1, waiting for transfers between devices, local(): parts = lax.all_to_all(chip.astype(jnp.bfloat16), CD[:2], 0, 0, tiled=True)  11.7 us
    all_to_all x2, waiting for transfers between devices, spread(): lax.all_to_all(copies, AB, 0, 0, tiled=True).reshape(-1, block.shape[1])  9.43 us
    all_to_all x1, starting transfers between devices, local(): parts = lax.all_to_all(chip.astype(jnp.bfloat16), CD[:2], 0, 0, tiled=True)  9.06 us
    all_to_all x1, waiting for transfers between devices, pair_layout(): swapped = lax.all_to_all(messages, CD, 0, 0, tiled=True)  7.88 us
  transfers between devices with their start and end apart: 15, of which 10 were waited for; matrix products, arithmetic and copies ran while one was open for 3% of the time, Pallas kernels for 0%

profile of v7, /device:TPU:1, one launch (start us, length us, event | category | flops | bytes accessed | tf_op | source)
XLA Modules:
  0.0 195.5 jit_solution(14688468911615937914)
XLA Ops:
  7.2 1.0 copy.116
  8.2 3.9 %collective-permute-start.1 = (bf16[4,8,2048]{2,1,0:T(8,128)(2,1)S(1)}, bf16[4,8,2048]{2,1,0:T(8,128)(2,1)S(1)}, u32[]{:S(2)}, u32[]{:S(2)}) collective-permute-start(bf16[4,8,2048]{2,1,0:T(8,128)(2,1)S(1)} %bitcast.79), channel_id=1, source_target_pairs={{0,32},{32,0},{1,33},{33,1},{2,34},{34,2},{3,35},{35,3},{4,36},{36... | collective-permute-start | bytes 393224 | tf_op jit(solution)/shard_map/ppermute | solution.py:130
  12.2 4.4 %collective-permute-start = (bf16[4,8,2048]{2,1,0:T(8,128)(2,1)S(1)}, bf16[4,8,2048]{2,1,0:T(8,128)(2,1)S(1)}, u32[]{:S(2)}, u32[]{:S(2)}) collective-permute-start(bf16[4,8,2048]{2,1,0:T(8,128)(2,1)S(1)} %bitcast.80), channel_id=1, source_target_pairs={{0,2},{2,0},{1,3},{3,1},{4,6},{6,4},{5,7},{7,5},{8,10},{10,8},{9,1... | collective-permute-start | bytes 393224 | tf_op jit(solution)/shard_map/ppermute | solution.py:131
  16.6 3.2 %collective-permute-done = bf16[4,8,2048]{2,1,0:T(8,128)(2,1)S(1)} collective-permute-done((bf16[4,8,2048]{2,1,0:T(8,128)(2,1)S(1)}, bf16[4,8,2048]{2,1,0:T(8,128)(2,1)S(1)}, u32[]{:S(2)}, u32[]{:S(2)}) %collective-permute-start) | collective-permute-done | bytes 131104 | tf_op jit(solution)/shard_map/ppermute | solution.py:131
  19.8 1.0 select_bitcast_fusion.1
  20.8 0.7 pad_maximum_fusion.2
  22.6 0.8 copy.84
  23.4 7.6 %all-to-all-start = ((f32[16,8,128]{2,1,0:T(8,128)}), f32[16,8,128]{2,1,0:T(8,128)S(1)}, u32[]{:S(2)}, u32[]{:S(2)}) async-start(f32[16,8,128]{2,1,0:T(8,128)} %copy.84), calls=%async_computation | async-start | bytes 131072 | tf_op jit(solution)/shard_map/all_to_all | solution.py:161
  32.5 6.5 %all-to-all-done = f32[16,8,128]{2,1,0:T(8,128)S(1)} async-done(((f32[16,8,128]{2,1,0:T(8,128)}), f32[16,8,128]{2,1,0:T(8,128)S(1)}, u32[]{:S(2)}, u32[]{:S(2)}) %all-to-all-start) | async-done | bytes 65568 | tf_op jit(solution)/shard_map/all_to_all | solution.py:161
  39.7 15.3 %all-to-all-start.1 = ((f32[32,4,128]{2,1,0:T(4,128)}), f32[32,4,128]{2,1,0:T(4,128)S(1)}, u32[]{:S(2)}, u32[]{:S(2)}) async-start(f32[32,4,128]{2,1,0:T(4,128)} %copy.87), calls=%async_computation.1 | async-start | bytes 131072 | tf_op jit(solution)/shard_map/all_to_all | solution.py:15
  55.1 2.3 %collective-permute-start.2 = (bf16[1,2,4,8,2048]{4,3,2,1,0:T(8,128)(2,1)S(1)}, bf16[1,2,4,8,2048]{4,3,2,1,0:T(8,128)(2,1)S(1)}, u32[]{:S(2)}, u32[]{:S(2)}) collective-permute-start(bf16[1,2,4,8,2048]{4,3,2,1,0:T(8,128)(2,1)S(1)} %maximum_bitcast_fusion.2.refs_0_), channel_id=1, source_target_pairs={{0,256},{64,320},{128,384},{192,448},{256,0},{320,64},{384,128},{4... | collective-permute-start | bytes 786440 | tf_op jit(solution)/shard_map/ppermute | solution.py:141
  57.4 7.9 %all-to-all-done.1 = f32[32,4,128]{2,1,0:T(4,128)S(1)} async-done(((f32[32,4,128]{2,1,0:T(4,128)}), f32[32,4,128]{2,1,0:T(4,128)S(1)}, u32[]{:S(2)}, u32[]{:S(2)}) %all-to-all-start.1) | async-done | bytes 65568 | tf_op jit(solution)/shard_map/all_to_all | solution.py:15
  65.6 5.1 %collective-permute-done.2.refs_1_ = bf16[1,2,4,8,2048]{4,3,2,1,0:T(8,128)(2,1)S(1)} collective-permute-done((bf16[1,2,4,8,2048]{4,3,2,1,0:T(8,128)(2,1)S(1)}, bf16[1,2,4,8,2048]{4,3,2,1,0:T(8,128)(2,1)S(1)}, u32[]{:S(2)}, u32[]{:S(2)}) %collective-permute-start.2) | collective-permute-done | bytes 262176 | tf_op jit(solution)/shard_map/ppermute | solution.py:141
  70.7 2.0 %collective-permute-start.6 = (bf16[2,2,4,8,2048]{4,3,2,1,0:T(8,128)(2,1)S(1)}, bf16[2,2,4,8,2048]{4,3,2,1,0:T(8,128)(2,1)S(1)}, u32[]{:S(2)}, u32[]{:S(2)}) collective-permute-start(bf16[2,2,4,8,2048]{4,3,2,1,0:T(8,128)(2,1)S(1)} %pad_maximum_fusion.1), channel_id=1, source_target_pairs={{0,448},{64,0},{128,64},{192,128},{256,192},{320,256},{384,320},{4... | collective-permute-start | bytes 1572872 | tf_op jit(solution)/shard_map/ppermute | solution.py:141
  72.8 5.8 %collective-permute-start.5 = (bf16[2,2,4,8,2048]{4,3,2,1,0:T(8,128)(2,1)S(1)}, bf16[2,2,4,8,2048]{4,3,2,1,0:T(8,128)(2,1)S(1)}, u32[]{:S(2)}, u32[]{:S(2)}) collective-permute-start(bf16[2,2,4,8,2048]{4,3,2,1,0:T(8,128)(2,1)S(1)} %pad_maximum_fusion.1), channel_id=1, source_target_pairs={{0,64},{64,128},{128,192},{192,256},{256,320},{320,384},{384,448},... | collective-permute-start | bytes 1572872 | tf_op jit(solution)/shard_map/ppermute | solution.py:141
  78.7 0.8 broadcast_in_dim.9
  79.4 3.5 %all-to-all-start.2 = ((bf16[16,32,256]{2,1,0:T(8,128)(2,1)}), bf16[16,32,256]{2,1,0:T(8,128)(2,1)S(1)}, u32[]{:S(2)}, u32[]{:S(2)}) async-start(bf16[16,32,256]{2,1,0:T(8,128)(2,1)} %broadcast_in_dim.9), calls=%async_computation.2 | async-start | bytes 524288 | tf_op jit(solution)/shard_map/all_to_all | solution.py:22
  83.0 5.3 %collective-permute-start.4 = (bf16[1,2,4,8,2048]{4,3,2,1,0:T(8,128)(2,1)S(1)}, bf16[1,2,4,8,2048]{4,3,2,1,0:T(8,128)(2,1)S(1)}, u32[]{:S(2)}, u32[]{:S(2)}) collective-permute-start(bf16[1,2,4,8,2048]{4,3,2,1,0:T(8,128)(2,1)S(1)} %maximum_bitcast_fusion.2.refs_0_), channel_id=1, source_target_pairs={{0,384},{64,448},{128,0},{192,64},{256,128},{320,192},{384,256},{4... | collective-permute-start | bytes 786440 | tf_op jit(solution)/shard_map/ppermute | solution.py:141
  88.3 1.9 collective-permute-start.3
  90.8 12.0 %collective-permute-done.4.refs_3_ = bf16[1,2,4,8,2048]{4,3,2,1,0:T(8,128)(2,1)S(1)} collective-permute-done((bf16[1,2,4,8,2048]{4,3,2,1,0:T(8,128)(2,1)S(1)}, bf16[1,2,4,8,2048]{4,3,2,1,0:T(8,128)(2,1)S(1)}, u32[]{:S(2)}, u32[]{:S(2)}) %collective-permute-start.4) | collective-permute-done | bytes 262176 | tf_op jit(solution)/shard_map/ppermute | solution.py:141
  102.8 2.0 %collective-permute-done.3.refs_2_ = bf16[1,2,4,8,2048]{4,3,2,1,0:T(8,128)(2,1)S(1)} collective-permute-done((bf16[1,2,4,8,2048]{4,3,2,1,0:T(8,128)(2,1)S(1)}, bf16[1,2,4,8,2048]{4,3,2,1,0:T(8,128)(2,1)S(1)}, u32[]{:S(2)}, u32[]{:S(2)}) %collective-permute-start.3) | collective-permute-done | bytes 262176 | tf_op jit(solution)/shard_map/ppermute | solution.py:141
  106.0 7.7 %tiles_and_ladder.1 = (bf16[512,1024]{1,0:T(8,128)(2,1)}, f32[16,32,256]{2,1,0:T(8,128)}, bf16[16,32,256]{2,1,0:T(8,128)(2,1)}) custom-call(s32[2]{0:T(128)} %pad_add_fusion.at_ref, bf16[8,2,2,32,2048]{4,3,2,1,0:T(8,128)(2,1)} %bitcast.63, bf16[512,256]{1,0:T(8,128)(2,1)} %bitcast.72, bf16[1,2,4,8,2048]{4,3,2,1,0:T(8,128)(2,1)} %copy-done, ...), custom_call_target="tpu_custom_call" | custom-call | tf_op jit(solution)/shard_map/tiles_and_ladder/pallas_call | solution.py:91
  113.8 7.2 %collective-permute-start.7 = (bf16[16,32,256]{2,1,0:T(8,128)(2,1)}, bf16[16,32,256]{2,1,0:T(8,128)(2,1)S(1)}, u32[]{:S(2)}, u32[]{:S(2)}) collective-permute-start(bf16[16,32,256]{2,1,0:T(8,128)(2,1)} %get-tuple-element.6), channel_id=1, source_target_pairs={{0,1},{1,0},{2,3},{3,2},{4,5},{5,4},{6,7},{7,6},{8,9},{9,8},{10,11... | collective-permute-start | bytes 786440 | tf_op jit(solution)/shard_map/ppermute | solution.py:169
  120.9 1.4 collective-permute-done.7
  122.3 1.8 add_convert_fusion
  124.1 9.1 %all-to-all-start.3 = ((bf16[16,32,256]{2,1,0:T(8,128)(2,1)}), bf16[16,32,256]{2,1,0:T(8,128)(2,1)S(1)}, u32[]{:S(2)}, u32[]{:S(2)}) async-start(bf16[16,32,256]{2,1,0:T(8,128)(2,1)} %add_convert_fusion), calls=%async_computation.3 | async-start | bytes 524288 | tf_op jit(solution)/shard_map/all_to_all | solution.py:170
  134.0 11.7 %all-to-all-done.3 = bf16[16,32,256]{2,1,0:T(8,128)(2,1)S(1)} async-done(((bf16[16,32,256]{2,1,0:T(8,128)(2,1)}), bf16[16,32,256]{2,1,0:T(8,128)(2,1)S(1)}, u32[]{:S(2)}, u32[]{:S(2)}) %all-to-all-start.3) | async-done | bytes 262176 | tf_op jit(solution)/shard_map/all_to_all | solution.py:170
  146.6 3.5 %all-to-all-start.4 = ((bf16[16,32,256]{2,1,0:T(8,128)(2,1)}), bf16[16,32,256]{2,1,0:T(8,128)(2,1)S(1)}, u32[]{:S(2)}, u32[]{:S(2)}) async-start(bf16[16,32,256]{2,1,0:T(8,128)(2,1)} %broadcast_in_dim.11), calls=%async_computation.4 | async-start | bytes 524288 | tf_op jit(solution)/shard_map/all_to_all | solution.py:22
  150.4 9.4 %all-to-all-done.4 = bf16[16,32,256]{2,1,0:T(8,128)(2,1)S(1)} async-done(((bf16[16,32,256]{2,1,0:T(8,128)(2,1)}), bf16[16,32,256]{2,1,0:T(8,128)(2,1)S(1)}, u32[]{:S(2)}, u32[]{:S(2)}) %all-to-all-start.4) | async-done | bytes 262176 | tf_op jit(solution)/shard_map/all_to_all | solution.py:22
  160.3 0.9 pad_maximum_fusion
  161.1 7.5 %all-to-all-start.5 = ((bf16[32,8,1088]{2,1,0:T(8,128)(2,1)}), bf16[32,8,1088]{2,1,0:T(8,128)(2,1)S(1)}, u32[]{:S(2)}, u32[]{:S(2)}) async-start(bf16[32,8,1088]{2,1,0:T(8,128)(2,1)} %pad_maximum_fusion), calls=%async_computation.5 | async-start | bytes 1179648 | tf_op jit(solution)/shard_map/all_to_all | solution.py:182
  168.7 18.3 %all-to-all-done.5 = bf16[32,8,1088]{2,1,0:T(8,128)(2,1)S(1)} async-done(((bf16[32,8,1088]{2,1,0:T(8,128)(2,1)}), bf16[32,8,1088]{2,1,0:T(8,128)(2,1)S(1)}, u32[]{:S(2)}, u32[]{:S(2)}) %all-to-all-start.5) | async-done | bytes 557088 | tf_op jit(solution)/shard_map/all_to_all | solution.py:182
  (79 shorter events, 9.4 us)
Async XLA Ops:
  7.2 14.4 %copy-start.9 = (f32[8,8,128]{2,1,0:T(8,128)S(1)}, f32[8,8,128]{2,1,0:T(8,128)}, u32[]{:S(2)}) copy-start(f32[8,8,128]{2,1,0:T(8,128)} %param.6) | copy-start | bytes 98308
  7.2 97.7 %all-gather.3.cloned.1.call-start = ((), (), s32[]{:S(2)}) async-start(), calls=%async_computation.6 | async-start | bytes 4456448 | tf_op jit(solution)/shard_map/all_gather | solution.py:134
  8.2 13.6 %copy-start.6 = (f32[8,8,128]{2,1,0:T(8,128)S(1)}, f32[8,8,128]{2,1,0:T(8,128)}, u32[]{:S(2)}) copy-start(f32[8,8,128]{2,1,0:T(8,128)} %param.7) | copy-start | bytes 98308
  8.2 8.3 %collective-permute-start.1 = (bf16[4,8,2048]{2,1,0:T(8,128)(2,1)S(1)}, bf16[4,8,2048]{2,1,0:T(8,128)(2,1)S(1)}, u32[]{:S(2)}, u32[]{:S(2)}) collective-permute-start(bf16[4,8,2048]{2,1,0:T(8,128)(2,1)S(1)} %bitcast.79), channel_id=1, source_target_pairs={{0,32},{32,0},{1,33},{33,1},{2,34},{34,2},{3,35},{35,3},{4,36},{36... | collective-permute-start | bytes 393224 | tf_op jit(solution)/shard_map/ppermute | solution.py:130
  12.2 7.6 %collective-permute-start = (bf16[4,8,2048]{2,1,0:T(8,128)(2,1)S(1)}, bf16[4,8,2048]{2,1,0:T(8,128)(2,1)S(1)}, u32[]{:S(2)}, u32[]{:S(2)}) collective-permute-start(bf16[4,8,2048]{2,1,0:T(8,128)(2,1)S(1)} %bitcast.80), channel_id=1, source_target_pairs={{0,2},{2,0},{1,3},{3,1},{4,6},{6,4},{5,7},{7,5},{8,10},{10,8},{9,1... | collective-permute-start | bytes 393224 | tf_op jit(solution)/shard_map/ppermute | solution.py:131
  23.4 15.6 %all-to-all-start = ((f32[16,8,128]{2,1,0:T(8,128)}), f32[16,8,128]{2,1,0:T(8,128)S(1)}, u32[]{:S(2)}, u32[]{:S(2)}) async-start(f32[16,8,128]{2,1,0:T(8,128)} %copy.84), calls=%async_computation | async-start | bytes 131072 | tf_op jit(solution)/shard_map/all_to_all | solution.py:161
  39.7 25.6 %all-to-all-start.1 = ((f32[32,4,128]{2,1,0:T(4,128)}), f32[32,4,128]{2,1,0:T(4,128)S(1)}, u32[]{:S(2)}, u32[]{:S(2)}) async-start(f32[32,4,128]{2,1,0:T(4,128)} %copy.87), calls=%async_computation.1 | async-start | bytes 131072 | tf_op jit(solution)/shard_map/all_to_all | solution.py:15
  55.1 33.3 %copy-start = (bf16[1,2,4,8,2048]{4,3,2,1,0:T(8,128)(2,1)}, bf16[1,2,4,8,2048]{4,3,2,1,0:T(8,128)(2,1)S(1)}, u32[]{:S(2)}) copy-start(bf16[1,2,4,8,2048]{4,3,2,1,0:T(8,128)(2,1)S(1)} %maximum_bitcast_fusion.2.refs_0_) | copy-start | bytes 786436
  55.1 15.6 %collective-permute-start.2 = (bf16[1,2,4,8,2048]{4,3,2,1,0:T(8,128)(2,1)S(1)}, bf16[1,2,4,8,2048]{4,3,2,1,0:T(8,128)(2,1)S(1)}, u32[]{:S(2)}, u32[]{:S(2)}) collective-permute-start(bf16[1,2,4,8,2048]{4,3,2,1,0:T(8,128)(2,1)S(1)} %maximum_bitcast_fusion.2.refs_0_), channel_id=1, source_target_pairs={{0,256},{64,320},{128,384},{192,448},{256,0},{320,64},{384,128},{4... | collective-permute-start | bytes 786440 | tf_op jit(solution)/shard_map/ppermute | solution.py:141
  70.7 34.2 %copy-start.3 = (bf16[1,2,4,8,2048]{4,3,2,1,0:T(8,128)(2,1)}, bf16[1,2,4,8,2048]{4,3,2,1,0:T(8,128)(2,1)S(1)}, u32[]{:S(2)}) copy-start(bf16[1,2,4,8,2048]{4,3,2,1,0:T(8,128)(2,1)S(1)} %collective-permute-done.2.refs_1_) | copy-start | bytes 786436
  70.7 34.1 %collective-permute-start.6 = (bf16[2,2,4,8,2048]{4,3,2,1,0:T(8,128)(2,1)S(1)}, bf16[2,2,4,8,2048]{4,3,2,1,0:T(8,128)(2,1)S(1)}, u32[]{:S(2)}, u32[]{:S(2)}) collective-permute-start(bf16[2,2,4,8,2048]{4,3,2,1,0:T(8,128)(2,1)S(1)} %pad_maximum_fusion.1), channel_id=1, source_target_pairs={{0,448},{64,0},{128,64},{192,128},{256,192},{320,256},{384,320},{4... | collective-permute-start | bytes 1572872 | tf_op jit(solution)/shard_map/ppermute | solution.py:141
  72.8 32.1 %collective-permute-start.5 = (bf16[2,2,4,8,2048]{4,3,2,1,0:T(8,128)(2,1)S(1)}, bf16[2,2,4,8,2048]{4,3,2,1,0:T(8,128)(2,1)S(1)}, u32[]{:S(2)}, u32[]{:S(2)}) collective-permute-start(bf16[2,2,4,8,2048]{4,3,2,1,0:T(8,128)(2,1)S(1)} %pad_maximum_fusion.1), channel_id=1, source_target_pairs={{0,64},{64,128},{128,192},{192,256},{256,320},{320,384},{384,448},... | collective-permute-start | bytes 1572872 | tf_op jit(solution)/shard_map/ppermute | solution.py:141
  79.4 25.4 %all-to-all-start.2 = ((bf16[16,32,256]{2,1,0:T(8,128)(2,1)}), bf16[16,32,256]{2,1,0:T(8,128)(2,1)S(1)}, u32[]{:S(2)}, u32[]{:S(2)}) async-start(bf16[16,32,256]{2,1,0:T(8,128)(2,1)} %broadcast_in_dim.9), calls=%async_computation.2 | async-start | bytes 524288 | tf_op jit(solution)/shard_map/all_to_all | solution.py:22
  83.0 19.8 %collective-permute-start.4 = (bf16[1,2,4,8,2048]{4,3,2,1,0:T(8,128)(2,1)S(1)}, bf16[1,2,4,8,2048]{4,3,2,1,0:T(8,128)(2,1)S(1)}, u32[]{:S(2)}, u32[]{:S(2)}) collective-permute-start(bf16[1,2,4,8,2048]{4,3,2,1,0:T(8,128)(2,1)S(1)} %maximum_bitcast_fusion.2.refs_0_), channel_id=1, source_target_pairs={{0,384},{64,448},{128,0},{192,64},{256,128},{320,192},{384,256},{4... | collective-permute-start | bytes 786440 | tf_op jit(solution)/shard_map/ppermute | solution.py:141
  88.3 16.5 %collective-permute-start.3 = (bf16[1,2,4,8,2048]{4,3,2,1,0:T(8,128)(2,1)S(1)}, bf16[1,2,4,8,2048]{4,3,2,1,0:T(8,128)(2,1)S(1)}, u32[]{:S(2)}, u32[]{:S(2)}) collective-permute-start(bf16[1,2,4,8,2048]{4,3,2,1,0:T(8,128)(2,1)S(1)} %maximum_bitcast_fusion.2.refs_0_), channel_id=1, source_target_pairs={{0,128},{64,192},{128,256},{192,320},{256,384},{320,448},{384,0},{... | collective-permute-start | bytes 786440 | tf_op jit(solution)/shard_map/ppermute | solution.py:141
  102.8 2.1 %copy-start.7 = (bf16[1,2,4,8,2048]{4,3,2,1,0:T(8,128)(2,1)}, bf16[1,2,4,8,2048]{4,3,2,1,0:T(8,128)(2,1)S(1)}, u32[]{:S(2)}) copy-start(bf16[1,2,4,8,2048]{4,3,2,1,0:T(8,128)(2,1)S(1)} %collective-permute-done.4.refs_3_) | copy-start | bytes 786436
  104.8 0.7 copy-start.8
  104.8 0.8 copy-start.2
  104.8 1.0 copy-start.4
  104.9 1.2 copy-start.5
  113.7 19.5 %copy-start.11 = (f32[128]{0:T(128)S(1)}, f32[128]{0:T(128)}, u32[]{:S(2)}) copy-start(f32[128]{0:T(128)} %param.9) | copy-start | bytes 1540
  113.7 19.8 %copy-start.10 = (f32[32]{0:T(128)S(1)}, f32[32]{0:T(128)}, u32[]{:S(2)}) copy-start(f32[32]{0:T(128)} %param.8) | copy-start | bytes 388
  113.8 8.5 %collective-permute-start.7 = (bf16[16,32,256]{2,1,0:T(8,128)(2,1)}, bf16[16,32,256]{2,1,0:T(8,128)(2,1)S(1)}, u32[]{:S(2)}, u32[]{:S(2)}) collective-permute-start(bf16[16,32,256]{2,1,0:T(8,128)(2,1)} %get-tuple-element.6), channel_id=1, source_target_pairs={{0,1},{1,0},{2,3},{3,2},{4,5},{5,4},{6,7},{7,6},{8,9},{9,8},{10,11... | collective-permute-start | bytes 786440 | tf_op jit(solution)/shard_map/ppermute | solution.py:169
  124.1 21.6 %all-to-all-start.3 = ((bf16[16,32,256]{2,1,0:T(8,128)(2,1)}), bf16[16,32,256]{2,1,0:T(8,128)(2,1)S(1)}, u32[]{:S(2)}, u32[]{:S(2)}) async-start(bf16[16,32,256]{2,1,0:T(8,128)(2,1)} %add_convert_fusion), calls=%async_computation.3 | async-start | bytes 524288 | tf_op jit(solution)/shard_map/all_to_all | solution.py:170
  133.2 26.6 %copy-start.1 = (bf16[512,1024]{1,0:T(8,128)(2,1)S(1)}, bf16[512,1024]{1,0:T(8,128)(2,1)}, u32[]{:S(2)}) copy-start(bf16[512,1024]{1,0:T(8,128)(2,1)} %get-tuple-element.7) | copy-start | bytes 3145732
  146.6 13.2 %all-to-all-start.4 = ((bf16[16,32,256]{2,1,0:T(8,128)(2,1)}), bf16[16,32,256]{2,1,0:T(8,128)(2,1)S(1)}, u32[]{:S(2)}, u32[]{:S(2)}) async-start(bf16[16,32,256]{2,1,0:T(8,128)(2,1)} %broadcast_in_dim.11), calls=%async_computation.4 | async-start | bytes 524288 | tf_op jit(solution)/shard_map/all_to_all | solution.py:22
  161.1 25.9 %all-to-all-start.5 = ((bf16[32,8,1088]{2,1,0:T(8,128)(2,1)}), bf16[32,8,1088]{2,1,0:T(8,128)(2,1)S(1)}, u32[]{:S(2)}, u32[]{:S(2)}) async-start(bf16[32,8,1088]{2,1,0:T(8,128)(2,1)} %pad_maximum_fusion), calls=%async_computation.5 | async-start | bytes 1179648 | tf_op jit(solution)/shard_map/all_to_all | solution.py:182
Sparse Core Ops, SparseCore 0:
  21.6 51.7 all-gather.2

commit v8 on v7

--- a/solution.py
+++ b/solution.py
@@ -26,9 +26,10 @@
 SHIFTS = ((0,), (4,), (2,), (-2,), (1, 5), (-1, 3))
 
 
-def tile_kernel(at_ref, left_ref, inward_ref, *refs):
+def tile_kernel(y_ref, left_ref, *refs):
     n_blocks = len(SHIFTS)
-    block_refs, (tiles_ref, kept_ref, sent_ref, piece_ref, gram_ref, tile_ref, sum_ref) = refs[:n_blocks], refs[n_blocks:]
+    block_refs = refs[:n_blocks]
+    tiles_ref, turned_ref, piece_ref, gram_ref, tile_ref, wide_ref = refs[n_blocks:]
     n_z, n_k, n_xh, block, aux_width = left_ref.shape
     a_local = 8
     rows = n_z * n_k * n_xh * block
@@ -39,7 +40,7 @@
     def _():
         for shifts, block_ref in zip(SHIFTS, block_refs):
             for slot, shift in enumerate(shifts):
-                y = (at_ref[0] + n_y - shift) % n_y
+                y = (y_ref[0] + n_y - shift) % n_y
                 for d in range(d_local):
                     for xl in range(n_xl):
                         rows_at = slice(xl * b_local, (xl + 1) * b_local)
@@ -49,72 +50,92 @@
         [left_ref[z, k, xh] for z in range(n_z) for xh in range(n_xh) for k in range(n_k)], axis=0
     )
     gram = lax.dot_general(
-        left, piece_ref[...].reshape(d_local * LANES, aux_width), (((1,), (1,)), ((), ())), preferred_element_type=jnp.float32
+        left,
+        piece_ref[...].reshape(d_local * LANES, aux_width),
+        (((1,), (1,)), ((), ())),
+        preferred_element_type=jnp.float32,
     )
     for d in range(d_local):
         gram_ref[d] = gram[:, d * LANES : (d + 1) * LANES]
     groups = rows // (a_local * 8)
+    part = groups * d_local * 8
     for a in range(a_local):
+        lanes = slice(a * LANES, (a + 1) * LANES)
         for d in range(d_local):
-            part = gram_ref[d, pl.ds(a, rows // a_local, stride=a_local), :]
-            tile_ref[:, d, :, a * LANES : (a + 1) * LANES] = part.reshape(groups, 8, LANES)
-    tiles = tile_ref[...].reshape(groups * d_local * 8, a_local * LANES).astype(jnp.bfloat16)
-    tiles_ref[...] = tiles
-    first = pl.program_id(0) == 0
-    product = lax.dot_general(
-        tiles, inward_ref[...], (((0,), (0,)), ((), ())), preferred_element_type=jnp.float32
-    )
-    for half in range(2):
-        lanes = slice(half * LANES, (half + 1) * LANES)
-        for a in range(a_local):
-            out = product[a * LANES : (a + 1) * LANES, lanes]
+            piece = gram_ref[d, pl.ds(a, rows // a_local, stride=a_local), :]
+            tile_ref[:, d, :, lanes] = piece.reshape(groups, 8, LANES)
+        turned = tile_ref[:, :, :, lanes].reshape(part, LANES).T
+        for half in range(part // LANES):
             at = pl.ds(a, LANES, stride=a_local)
-            before = sum_ref[half, at, :]
-            sum_ref[half, at, :] = jnp.where(first, out, before + out)
-        n_groups, size, _ = kept_ref.shape
-        for group in range(n_groups):
-            own = pl.multiple_of((2 * group + at_ref[1]) * size, size)
-            other = pl.multiple_of((2 * group + 1 - at_ref[1]) * size, size)
-            kept_ref[group, :, lanes] = sum_ref[half, pl.ds(own, size), :]
-            sent_ref[group, :, lanes] = sum_ref[half, pl.ds(other, size), :].astype(jnp.bfloat16)
-
-
-def tiles_and_ladder(place, left, inward, blocks):
+            wide_ref[half, at, :] = turned[:, half * LANES : (half + 1) * LANES]
+    tiles_ref[...] = tile_ref[...].reshape(part, a_local * LANES).astype(jnp.bfloat16)
+    for half in range(part // LANES):
+        turned_ref[:, half * LANES : (half + 1) * LANES] = wide_ref[half].astype(jnp.bfloat16)
+
+
+def integral_tiles(y_index, left, blocks):
     n_z, n_k, n_xh, block, aux_width = left.shape
     steps = 2
-    contracted = inward.shape[0]
+    _, n_xl, d_local, b_local, _ = blocks[0].shape
+    n_y = sum(value.shape[0] for value in blocks)
     wide = 8 * LANES
+    contracted = n_z * n_k * n_xh * block * d_local // 8
     part = contracted // steps
-    halves = (n_z * n_xh, wide // (n_z * n_xh * n_k), inward.shape[1])
-    _, n_xl, d_local, b_local, _ = blocks[0].shape
-    n_y = sum(block.shape[0] for block in blocks)
     return pl.pallas_call(
         tile_kernel,
         grid=(steps,),
         in_specs=[
             pl.BlockSpec(memory_space=pltpu.SMEM),
             pl.BlockSpec((n_z // steps, n_k, n_xh, block, aux_width), lambda s: (s, 0, 0, 0, 0)),
-            pl.BlockSpec((part, inward.shape[1]), lambda s: (s, 0)),
         ]
-        + [pl.BlockSpec(block.shape, lambda s: (0,) * 5, pipeline_mode=pl.Buffered(1)) for block in blocks],
+        + [pl.BlockSpec(value.shape, lambda s: (0,) * 5, pipeline_mode=pl.Buffered(1)) for value in blocks],
         out_specs=[
             pl.BlockSpec((part, wide), lambda s: (s, 0)),
-            pl.BlockSpec(halves, lambda s: (0, 0, 0)),
-            pl.BlockSpec(halves, lambda s: (0, 0, 0)),
+            pl.BlockSpec((wide, part), lambda s: (0, s)),
         ],
         out_shape=[
             jax.ShapeDtypeStruct((contracted, wide), jnp.bfloat16),
-            jax.ShapeDtypeStruct(halves, jnp.float32),
-            jax.ShapeDtypeStruct(halves, jnp.bfloat16),
+            jax.ShapeDtypeStruct((wide, contracted), jnp.bfloat16),
         ],
         scratch_shapes=[
             pltpu.VMEM((d_local, n_y, n_xl * b_local, aux_width), jnp.bfloat16),
             pltpu.VMEM((d_local, 2 * part, LANES), jnp.float32),
             pltpu.VMEM((part // (8 * d_local), d_local, 8, wide), jnp.float32),
-            pltpu.VMEM((2, wide, LANES), jnp.float32),
-        ],
-        name="tiles_and_ladder",
-    )(place, left, inward, *blocks)
+            pltpu.VMEM((part // LANES, wide, LANES), jnp.float32),
+        ],
+        name="integral_tiles",
+    )(y_index.reshape(1), left, *blocks)
+
+
+def ladder_kernel(k_ref, turned_ref, inward_ref, kept_ref, sent_ref, sum_ref):
+    sum_ref[...] = jnp.dot(turned_ref[...], inward_ref[...], preferred_element_type=jnp.float32)
+    n_groups, size, _ = kept_ref.shape
+    for group in range(n_groups):
+        own = pl.multiple_of((2 * group + k_ref[0]) * size, size)
+        other = pl.multiple_of((2 * group + 1 - k_ref[0]) * size, size)
+        kept_ref[group] = sum_ref[pl.ds(own, size), :]
+        sent_ref[group] = sum_ref[pl.ds(other, size), :].astype(jnp.bfloat16)
+
+
+def first_ladder(k_index, turned, inward, groups):
+    wide, pairs = turned.shape[0], inward.shape[1]
+    halves = (groups, wide // (2 * groups), pairs)
+    whole = pl.BlockSpec(memory_space=pltpu.VMEM)
+    return pl.pallas_call(
+        ladder_kernel,
+        in_specs=[pl.BlockSpec(memory_space=pltpu.SMEM), whole, whole],
+        out_specs=[whole, whole],
+        out_shape=[
+            pltpu.VMEM(halves, jnp.float32),
+            pltpu.VMEM(halves, jnp.bfloat16),
+        ],
+        scratch_shapes=[pltpu.VMEM((wide, pairs), jnp.float32)],
+        name="first_ladder",
+    )(
+        k_index.reshape(1),
+        pltpu.with_memory_space_constraint(turned, pltpu.VMEM),
+        pltpu.with_memory_space_constraint(inward, pltpu.VMEM),
+    )
 
 
 def local(factors, amplitudes, driving, occ_energy, vir_energy):
@@ -164,8 +185,8 @@
     current, drive = blocks[0], blocks[1]
     inward = spread(current.astype(jnp.bfloat16), n_ab)
 
-    place = jnp.stack([lax.axis_index("y"), lax.axis_index("k")])
-    tiles, kept, sent = tiles_and_ladder(place, left, inward, y_blocks)
+    tiles, turned_tiles = integral_tiles(lax.axis_index("y"), left, y_blocks)
+    kept, sent = first_ladder(lax.axis_index("k"), turned_tiles, inward, n_z * n_xh)
     chip = kept + lax.ppermute(sent, "k", [(0, 1), (1, 0)]).astype(jnp.float32)
     parts = lax.all_to_all(chip.astype(jnp.bfloat16), CD[:2], 0, 0, tiled=True)
     ladder = jnp.sum(parts.astype(jnp.float32), axis=0)

time: 196 us -> 194 us (0.990)
  starting transfers between devices: 79.4 us -> 75.8 us
  waiting for transfers between devices: 77.6 us -> 80.4 us
    ppermute x1, waiting for transfers between devices: 0.01 us -> 3.37 us  [local(): theirs = lax.ppermute(turned, 'xl', [(0, 1), (1, 0)])]
    ppermute x1, waiting for transfers between devices: 3.2 us -> 0.1 us  [local(): across = lax.ppermute(turned, 'xh', [(0, 1), (1, 0)])]
    ppermute x1, starting transfers between devices: 7.18 us -> 4.13 us  [local(): chip = kept + lax.ppermute(sent, 'k', [(0, 1), (1, 0)]).astype(jnp.float32)]
    ppermute x5, waiting for transfers between devices: 19.1 us -> 22 us  [shifted(): lax.ppermute(value, 'y', [(i, (i + shift) % n_y) for i in range(n_y)])]
    pallas_call x1 -> x2, Pallas kernels: 7.7 us -> 7.08 us  [the longest x1 6.58 us: integral_tiles(): pl.pallas_call(tile_kernel, grid=(steps,), in_specs=[pl.BlockSpec(memory_...]
  transfers between devices with their start and end apart: 15 -> 15, of which waited for: 10 -> 11; matrix products, arithmetic and copies ran while one was open for 3% -> 3% of each run, Pallas kernels for 0% -> 3%
where the time goes in v8:
time: 194 us; the launch traced here: 193 us
  waiting for transfers between devices  80.4 us (41%)
  starting transfers between devices  75.8 us (39%)
  between operations  14.5 us (7%)
  local copies, waits for them, and re-layouts  10.5 us (5%)
  Pallas kernels  7.08 us (4%)
  other arithmetic  4.8 us (2%)
    ppermute x5, waiting for transfers between devices, shifted(): lax.ppermute(value, 'y', [(i, (i + shift) % n_y) for i in range(n_y)])  22 us
    all_to_all x1, waiting for transfers between devices, local(): parts = lax.all_to_all(message, CD, 0, 0, tiled=True)  18.3 us
    ppermute x5, starting transfers between devices, shifted(): lax.ppermute(value, 'y', [(i, (i + shift) % n_y) for i in range(n_y)])  17.6 us
    all_to_all x1, starting transfers between devices, pair_layout(): swapped = lax.all_to_all(messages, CD, 0, 0, tiled=True)  14 us
    all_to_all x1, waiting for transfers between devices, local(): parts = lax.all_to_all(chip.astype(jnp.bfloat16), CD[:2], 0, 0, tiled=True)  11.7 us
    all_to_all x2, waiting for transfers between devices, spread(): lax.all_to_all(copies, AB, 0, 0, tiled=True).reshape(-1, block.shape[1])  9.35 us
    all_to_all x1, starting transfers between devices, local(): parts = lax.all_to_all(chip.astype(jnp.bfloat16), CD[:2], 0, 0, tiled=True)  9.03 us
    all_to_all x1, starting transfers between devices, local(): lax.all_to_all(outgoing.reshape(n_ab, -1, 128), AB, 0, 0, tiled=True)  8.39 us
  transfers between devices with their start and end apart: 15, of which 11 were waited for; matrix products, arithmetic and copies ran while one was open for 3% of the time, Pallas kernels for 3%

profile of v8, /device:TPU:1, one launch (start us, length us, event | category | flops | bytes accessed | tf_op | source)
XLA Modules:
  0.0 193.5 jit_solution(4806498255839538658)
XLA Ops:
  7.2 1.0 copy.116
  8.2 5.5 %collective-permute-start = (bf16[4,8,2048]{2,1,0:T(8,128)(2,1)S(1)}, bf16[4,8,2048]{2,1,0:T(8,128)(2,1)S(1)}, u32[]{:S(2)}, u32[]{:S(2)}) collective-permute-start(bf16[4,8,2048]{2,1,0:T(8,128)(2,1)S(1)} %bitcast.79), channel_id=1, source_target_pairs={{0,2},{2,0},{1,3},{3,1},{4,6},{6,4},{5,7},{7,5},{8,10},{10,8},{9,1... | collective-permute-start | bytes 393224 | tf_op jit(solution)/shard_map/ppermute | solution.py:152
  13.7 2.2 %collective-permute-start.1 = (bf16[4,8,2048]{2,1,0:T(8,128)(2,1)S(1)}, bf16[4,8,2048]{2,1,0:T(8,128)(2,1)S(1)}, u32[]{:S(2)}, u32[]{:S(2)}) collective-permute-start(bf16[4,8,2048]{2,1,0:T(8,128)(2,1)S(1)} %bitcast.80), channel_id=1, source_target_pairs={{0,32},{32,0},{1,33},{33,1},{2,34},{34,2},{3,35},{35,3},{4,36},{36... | collective-permute-start | bytes 393224 | tf_op jit(solution)/shard_map/ppermute | solution.py:151
  16.0 3.4 %collective-permute-done.1 = bf16[4,8,2048]{2,1,0:T(8,128)(2,1)S(1)} collective-permute-done((bf16[4,8,2048]{2,1,0:T(8,128)(2,1)S(1)}, bf16[4,8,2048]{2,1,0:T(8,128)(2,1)S(1)}, u32[]{:S(2)}, u32[]{:S(2)}) %collective-permute-start.1) | collective-permute-done | bytes 131104 | tf_op jit(solution)/shard_map/ppermute | solution.py:151
  19.4 1.0 select_bitcast_fusion.1
  22.3 0.8 copy.84
  23.1 8.4 %all-to-all-start = ((f32[16,8,128]{2,1,0:T(8,128)}), f32[16,8,128]{2,1,0:T(8,128)S(1)}, u32[]{:S(2)}, u32[]{:S(2)}) async-start(f32[16,8,128]{2,1,0:T(8,128)} %copy.84), calls=%async_computation | async-start | bytes 131072 | tf_op jit(solution)/shard_map/all_to_all | solution.py:182
  32.9 6.5 %all-to-all-done = f32[16,8,128]{2,1,0:T(8,128)S(1)} async-done(((f32[16,8,128]{2,1,0:T(8,128)}), f32[16,8,128]{2,1,0:T(8,128)S(1)}, u32[]{:S(2)}, u32[]{:S(2)}) %all-to-all-start) | async-done | bytes 65568 | tf_op jit(solution)/shard_map/all_to_all | solution.py:182
  40.1 14.0 %all-to-all-start.1 = ((f32[32,4,128]{2,1,0:T(4,128)}), f32[32,4,128]{2,1,0:T(4,128)S(1)}, u32[]{:S(2)}, u32[]{:S(2)}) async-start(f32[32,4,128]{2,1,0:T(4,128)} %copy.87), calls=%async_computation.1 | async-start | bytes 131072 | tf_op jit(solution)/shard_map/all_to_all | solution.py:15
  54.1 2.3 %collective-permute-start.2 = (bf16[1,2,4,8,2048]{4,3,2,1,0:T(8,128)(2,1)S(1)}, bf16[1,2,4,8,2048]{4,3,2,1,0:T(8,128)(2,1)S(1)}, u32[]{:S(2)}, u32[]{:S(2)}) collective-permute-start(bf16[1,2,4,8,2048]{4,3,2,1,0:T(8,128)(2,1)S(1)} %maximum_bitcast_fusion.2.refs_0_), channel_id=1, source_target_pairs={{0,256},{64,320},{128,384},{192,448},{256,0},{320,64},{384,128},{4... | collective-permute-start | bytes 786440 | tf_op jit(solution)/shard_map/ppermute | solution.py:162
  56.4 7.9 %all-to-all-done.1 = f32[32,4,128]{2,1,0:T(4,128)S(1)} async-done(((f32[32,4,128]{2,1,0:T(4,128)}), f32[32,4,128]{2,1,0:T(4,128)S(1)}, u32[]{:S(2)}, u32[]{:S(2)}) %all-to-all-start.1) | async-done | bytes 65568 | tf_op jit(solution)/shard_map/all_to_all | solution.py:15
  64.6 5.1 %collective-permute-done.2.refs_1_ = bf16[1,2,4,8,2048]{4,3,2,1,0:T(8,128)(2,1)S(1)} collective-permute-done((bf16[1,2,4,8,2048]{4,3,2,1,0:T(8,128)(2,1)S(1)}, bf16[1,2,4,8,2048]{4,3,2,1,0:T(8,128)(2,1)S(1)}, u32[]{:S(2)}, u32[]{:S(2)}) %collective-permute-start.2) | collective-permute-done | bytes 262176 | tf_op jit(solution)/shard_map/ppermute | solution.py:162
  69.8 5.9 %collective-permute-start.5 = (bf16[2,2,4,8,2048]{4,3,2,1,0:T(8,128)(2,1)S(1)}, bf16[2,2,4,8,2048]{4,3,2,1,0:T(8,128)(2,1)S(1)}, u32[]{:S(2)}, u32[]{:S(2)}) collective-permute-start(bf16[2,2,4,8,2048]{4,3,2,1,0:T(8,128)(2,1)S(1)} %pad_maximum_fusion.1), channel_id=1, source_target_pairs={{0,64},{64,128},{128,192},{192,256},{256,320},{320,384},{384,448},... | collective-permute-start | bytes 1572872 | tf_op jit(solution)/shard_map/ppermute | solution.py:162
  75.7 1.9 collective-permute-start.6
  77.7 0.7 broadcast_in_dim.10
  78.5 3.5 %all-to-all-start.2 = ((bf16[16,32,256]{2,1,0:T(8,128)(2,1)}), bf16[16,32,256]{2,1,0:T(8,128)(2,1)S(1)}, u32[]{:S(2)}, u32[]{:S(2)}) async-start(bf16[16,32,256]{2,1,0:T(8,128)(2,1)} %broadcast_in_dim.10), calls=%async_computation.2 | async-start | bytes 524288 | tf_op jit(solution)/shard_map/all_to_all | solution.py:22
  82.0 4.1 %collective-permute-start.3 = (bf16[1,2,4,8,2048]{4,3,2,1,0:T(8,128)(2,1)S(1)}, bf16[1,2,4,8,2048]{4,3,2,1,0:T(8,128)(2,1)S(1)}, u32[]{:S(2)}, u32[]{:S(2)}) collective-permute-start(bf16[1,2,4,8,2048]{4,3,2,1,0:T(8,128)(2,1)S(1)} %maximum_bitcast_fusion.2.refs_0_), channel_id=1, source_target_pairs={{0,128},{64,192},{128,256},{192,320},{256,384},{320,448},{384,0},{... | collective-permute-start | bytes 786440 | tf_op jit(solution)/shard_map/ppermute | solution.py:162
  86.1 3.3 %collective-permute-start.4 = (bf16[1,2,4,8,2048]{4,3,2,1,0:T(8,128)(2,1)S(1)}, bf16[1,2,4,8,2048]{4,3,2,1,0:T(8,128)(2,1)S(1)}, u32[]{:S(2)}, u32[]{:S(2)}) collective-permute-start(bf16[1,2,4,8,2048]{4,3,2,1,0:T(8,128)(2,1)S(1)} %maximum_bitcast_fusion.2.refs_0_), channel_id=1, source_target_pairs={{0,384},{64,448},{128,0},{192,64},{256,128},{320,192},{384,256},{4... | collective-permute-start | bytes 786440 | tf_op jit(solution)/shard_map/ppermute | solution.py:162
  89.4 14.6 %collective-permute-done.3.refs_2_ = bf16[1,2,4,8,2048]{4,3,2,1,0:T(8,128)(2,1)S(1)} collective-permute-done((bf16[1,2,4,8,2048]{4,3,2,1,0:T(8,128)(2,1)S(1)}, bf16[1,2,4,8,2048]{4,3,2,1,0:T(8,128)(2,1)S(1)}, u32[]{:S(2)}, u32[]{:S(2)}) %collective-permute-start.3) | collective-permute-done | bytes 262176 | tf_op jit(solution)/shard_map/ppermute | solution.py:162
  104.1 2.3 %collective-permute-done.4.refs_3_ = bf16[1,2,4,8,2048]{4,3,2,1,0:T(8,128)(2,1)S(1)} collective-permute-done((bf16[1,2,4,8,2048]{4,3,2,1,0:T(8,128)(2,1)S(1)}, bf16[1,2,4,8,2048]{4,3,2,1,0:T(8,128)(2,1)S(1)}, u32[]{:S(2)}, u32[]{:S(2)}) %collective-permute-start.4) | collective-permute-done | bytes 262176 | tf_op jit(solution)/shard_map/ppermute | solution.py:162
  107.4 6.6 %integral_tiles.1 = (bf16[512,1024]{1,0:T(8,128)(2,1)}, bf16[1024,512]{1,0:T(8,128)(2,1)}) custom-call(s32[1]{0:T(128)} %bitcast.13.y_ref, bf16[8,2,2,32,2048]{4,3,2,1,0:T(8,128)(2,1)} %bitcast.64, bf16[1,2,4,8,2048]{4,3,2,1,0:T(8,128)(2,1)} %copy-done.1, bf16[1,2,4,8,2048]{4,3,2,1,0:T(8,128)(2,1)} %copy-done.3, bf16[1,2,4,8,2048]{4,3,2,1,0:T(8,128)(2,1)} %copy-done.7, ...), custom_call_target="tpu_custom_call" | custom-call | tf_op jit(solution)/shard_map/integral_tiles/pallas_call | solution.py:84
  114.0 1.2 copy-done
  115.7 4.1 %collective-permute-start.7 = (bf16[16,32,256]{2,1,0:T(8,128)(2,1)S(1)}, bf16[16,32,256]{2,1,0:T(8,128)(2,1)S(1)}, u32[]{:S(2)}, u32[]{:S(2)}) collective-permute-start(bf16[16,32,256]{2,1,0:T(8,128)(2,1)S(1)} %get-tuple-element.8), channel_id=1, source_target_pairs={{0,1},{1,0},{2,3},{3,2},{4,5},{5,4},{6,7},{7,6},{8,9},{9,8},{10,11... | collective-permute-start | bytes 786440 | tf_op jit(solution)/shard_map/ppermute | solution.py:190
  119.8 1.1 collective-permute-done.7
  121.0 0.8 add_convert_fusion
  121.8 9.0 %all-to-all-start.3 = ((bf16[16,32,256]{2,1,0:T(8,128)(2,1)}), bf16[16,32,256]{2,1,0:T(8,128)(2,1)S(1)}, u32[]{:S(2)}, u32[]{:S(2)}) async-start(bf16[16,32,256]{2,1,0:T(8,128)(2,1)} %add_convert_fusion), calls=%async_computation.3 | async-start | bytes 524288 | tf_op jit(solution)/shard_map/all_to_all | solution.py:191
  131.6 11.7 %all-to-all-done.3 = bf16[16,32,256]{2,1,0:T(8,128)(2,1)S(1)} async-done(((bf16[16,32,256]{2,1,0:T(8,128)(2,1)}), bf16[16,32,256]{2,1,0:T(8,128)(2,1)S(1)}, u32[]{:S(2)}, u32[]{:S(2)}) %all-to-all-start.3) | async-done | bytes 262176 | tf_op jit(solution)/shard_map/all_to_all | solution.py:191
  144.2 4.1 %all-to-all-start.4 = ((bf16[16,32,256]{2,1,0:T(8,128)(2,1)}), bf16[16,32,256]{2,1,0:T(8,128)(2,1)S(1)}, u32[]{:S(2)}, u32[]{:S(2)}) async-start(bf16[16,32,256]{2,1,0:T(8,128)(2,1)} %broadcast_in_dim.11), calls=%async_computation.4 | async-start | bytes 524288 | tf_op jit(solution)/shard_map/all_to_all | solution.py:22
  148.5 9.3 %all-to-all-done.4 = bf16[16,32,256]{2,1,0:T(8,128)(2,1)S(1)} async-done(((bf16[16,32,256]{2,1,0:T(8,128)(2,1)}), bf16[16,32,256]{2,1,0:T(8,128)(2,1)S(1)}, u32[]{:S(2)}, u32[]{:S(2)}) %all-to-all-start.4) | async-done | bytes 262176 | tf_op jit(solution)/shard_map/all_to_all | solution.py:22
  158.3 0.9 pad_maximum_fusion
  159.2 7.4 %all-to-all-start.5 = ((bf16[32,8,1088]{2,1,0:T(8,128)(2,1)}), bf16[32,8,1088]{2,1,0:T(8,128)(2,1)S(1)}, u32[]{:S(2)}, u32[]{:S(2)}) async-start(bf16[32,8,1088]{2,1,0:T(8,128)(2,1)} %pad_maximum_fusion), calls=%async_computation.5 | async-start | bytes 1179648 | tf_op jit(solution)/shard_map/all_to_all | solution.py:203
  166.7 18.3 %all-to-all-done.5 = bf16[32,8,1088]{2,1,0:T(8,128)(2,1)S(1)} async-done(((bf16[32,8,1088]{2,1,0:T(8,128)(2,1)}), bf16[32,8,1088]{2,1,0:T(8,128)(2,1)S(1)}, u32[]{:S(2)}, u32[]{:S(2)}) %all-to-all-start.5) | async-done | bytes 557088 | tf_op jit(solution)/shard_map/all_to_all | solution.py:203
  (79 shorter events, 10.0 us)
Async XLA Ops:
  7.2 14.0 %copy-start.9 = (f32[8,8,128]{2,1,0:T(8,128)S(1)}, f32[8,8,128]{2,1,0:T(8,128)}, u32[]{:S(2)}) copy-start(f32[8,8,128]{2,1,0:T(8,128)} %param.6) | copy-start | bytes 98308
  7.2 99.2 %all-gather.3.cloned.1.call-start = ((), (), s32[]{:S(2)}) async-start(), calls=%async_computation.6 | async-start | bytes 4456448 | tf_op jit(solution)/shard_map/all_gather | solution.py:155
  8.2 13.3 %copy-start.6 = (f32[8,8,128]{2,1,0:T(8,128)S(1)}, f32[8,8,128]{2,1,0:T(8,128)}, u32[]{:S(2)}) copy-start(f32[8,8,128]{2,1,0:T(8,128)} %param.7) | copy-start | bytes 98308
  8.2 7.8 %collective-permute-start = (bf16[4,8,2048]{2,1,0:T(8,128)(2,1)S(1)}, bf16[4,8,2048]{2,1,0:T(8,128)(2,1)S(1)}, u32[]{:S(2)}, u32[]{:S(2)}) collective-permute-start(bf16[4,8,2048]{2,1,0:T(8,128)(2,1)S(1)} %bitcast.79), channel_id=1, source_target_pairs={{0,2},{2,0},{1,3},{3,1},{4,6},{6,4},{5,7},{7,5},{8,10},{10,8},{9,1... | collective-permute-start | bytes 393224 | tf_op jit(solution)/shard_map/ppermute | solution.py:152
  13.7 5.7 %collective-permute-start.1 = (bf16[4,8,2048]{2,1,0:T(8,128)(2,1)S(1)}, bf16[4,8,2048]{2,1,0:T(8,128)(2,1)S(1)}, u32[]{:S(2)}, u32[]{:S(2)}) collective-permute-start(bf16[4,8,2048]{2,1,0:T(8,128)(2,1)S(1)} %bitcast.80), channel_id=1, source_target_pairs={{0,32},{32,0},{1,33},{33,1},{2,34},{34,2},{3,35},{35,3},{4,36},{36... | collective-permute-start | bytes 393224 | tf_op jit(solution)/shard_map/ppermute | solution.py:151
  23.1 16.3 %all-to-all-start = ((f32[16,8,128]{2,1,0:T(8,128)}), f32[16,8,128]{2,1,0:T(8,128)S(1)}, u32[]{:S(2)}, u32[]{:S(2)}) async-start(f32[16,8,128]{2,1,0:T(8,128)} %copy.84), calls=%async_computation | async-start | bytes 131072 | tf_op jit(solution)/shard_map/all_to_all | solution.py:182
  40.1 24.2 %all-to-all-start.1 = ((f32[32,4,128]{2,1,0:T(4,128)}), f32[32,4,128]{2,1,0:T(4,128)S(1)}, u32[]{:S(2)}, u32[]{:S(2)}) async-start(f32[32,4,128]{2,1,0:T(4,128)} %copy.87), calls=%async_computation.1 | async-start | bytes 131072 | tf_op jit(solution)/shard_map/all_to_all | solution.py:15
  54.1 32.0 %copy-start.1 = (bf16[1,2,4,8,2048]{4,3,2,1,0:T(8,128)(2,1)}, bf16[1,2,4,8,2048]{4,3,2,1,0:T(8,128)(2,1)S(1)}, u32[]{:S(2)}) copy-start(bf16[1,2,4,8,2048]{4,3,2,1,0:T(8,128)(2,1)S(1)} %maximum_bitcast_fusion.2.refs_0_) | copy-start | bytes 786436
  54.1 15.6 %collective-permute-start.2 = (bf16[1,2,4,8,2048]{4,3,2,1,0:T(8,128)(2,1)S(1)}, bf16[1,2,4,8,2048]{4,3,2,1,0:T(8,128)(2,1)S(1)}, u32[]{:S(2)}, u32[]{:S(2)}) collective-permute-start(bf16[1,2,4,8,2048]{4,3,2,1,0:T(8,128)(2,1)S(1)} %maximum_bitcast_fusion.2.refs_0_), channel_id=1, source_target_pairs={{0,256},{64,320},{128,384},{192,448},{256,0},{320,64},{384,128},{4... | collective-permute-start | bytes 786440 | tf_op jit(solution)/shard_map/ppermute | solution.py:162
  69.7 36.6 %copy-start.3 = (bf16[1,2,4,8,2048]{4,3,2,1,0:T(8,128)(2,1)}, bf16[1,2,4,8,2048]{4,3,2,1,0:T(8,128)(2,1)S(1)}, u32[]{:S(2)}) copy-start(bf16[1,2,4,8,2048]{4,3,2,1,0:T(8,128)(2,1)S(1)} %collective-permute-done.2.refs_1_) | copy-start | bytes 786436
  69.8 36.5 %collective-permute-start.5 = (bf16[2,2,4,8,2048]{4,3,2,1,0:T(8,128)(2,1)S(1)}, bf16[2,2,4,8,2048]{4,3,2,1,0:T(8,128)(2,1)S(1)}, u32[]{:S(2)}, u32[]{:S(2)}) collective-permute-start(bf16[2,2,4,8,2048]{4,3,2,1,0:T(8,128)(2,1)S(1)} %pad_maximum_fusion.1), channel_id=1, source_target_pairs={{0,64},{64,128},{128,192},{192,256},{256,320},{320,384},{384,448},... | collective-permute-start | bytes 1572872 | tf_op jit(solution)/shard_map/ppermute | solution.py:162
  75.7 30.6 %collective-permute-start.6 = (bf16[2,2,4,8,2048]{4,3,2,1,0:T(8,128)(2,1)S(1)}, bf16[2,2,4,8,2048]{4,3,2,1,0:T(8,128)(2,1)S(1)}, u32[]{:S(2)}, u32[]{:S(2)}) collective-permute-start(bf16[2,2,4,8,2048]{4,3,2,1,0:T(8,128)(2,1)S(1)} %pad_maximum_fusion.1), channel_id=1, source_target_pairs={{0,448},{64,0},{128,64},{192,128},{256,192},{320,256},{384,320},{4... | collective-permute-start | bytes 1572872 | tf_op jit(solution)/shard_map/ppermute | solution.py:162
  78.5 35.5 %all-to-all-start.2 = ((bf16[16,32,256]{2,1,0:T(8,128)(2,1)}), bf16[16,32,256]{2,1,0:T(8,128)(2,1)S(1)}, u32[]{:S(2)}, u32[]{:S(2)}) async-start(bf16[16,32,256]{2,1,0:T(8,128)(2,1)} %broadcast_in_dim.10), calls=%async_computation.2 | async-start | bytes 524288 | tf_op jit(solution)/shard_map/all_to_all | solution.py:22
  82.0 22.0 %collective-permute-start.3 = (bf16[1,2,4,8,2048]{4,3,2,1,0:T(8,128)(2,1)S(1)}, bf16[1,2,4,8,2048]{4,3,2,1,0:T(8,128)(2,1)S(1)}, u32[]{:S(2)}, u32[]{:S(2)}) collective-permute-start(bf16[1,2,4,8,2048]{4,3,2,1,0:T(8,128)(2,1)S(1)} %maximum_bitcast_fusion.2.refs_0_), channel_id=1, source_target_pairs={{0,128},{64,192},{128,256},{192,320},{256,384},{320,448},{384,0},{... | collective-permute-start | bytes 786440 | tf_op jit(solution)/shard_map/ppermute | solution.py:162
  86.1 20.2 %collective-permute-start.4 = (bf16[1,2,4,8,2048]{4,3,2,1,0:T(8,128)(2,1)S(1)}, bf16[1,2,4,8,2048]{4,3,2,1,0:T(8,128)(2,1)S(1)}, u32[]{:S(2)}, u32[]{:S(2)}) collective-permute-start(bf16[1,2,4,8,2048]{4,3,2,1,0:T(8,128)(2,1)S(1)} %maximum_bitcast_fusion.2.refs_0_), channel_id=1, source_target_pairs={{0,384},{64,448},{128,0},{192,64},{256,128},{320,192},{384,256},{4... | collective-permute-start | bytes 786440 | tf_op jit(solution)/shard_map/ppermute | solution.py:162
  104.1 2.3 %copy-start.7 = (bf16[1,2,4,8,2048]{4,3,2,1,0:T(8,128)(2,1)}, bf16[1,2,4,8,2048]{4,3,2,1,0:T(8,128)(2,1)S(1)}, u32[]{:S(2)}) copy-start(bf16[1,2,4,8,2048]{4,3,2,1,0:T(8,128)(2,1)S(1)} %collective-permute-done.3.refs_2_) | copy-start | bytes 786436
  106.3 0.7 copy-start.8
  106.3 0.9 copy-start.4
  106.3 1.0 copy-start.5
  114.0 1.2 copy-start
  115.2 15.6 %copy-start.11 = (f32[128]{0:T(128)S(1)}, f32[128]{0:T(128)}, u32[]{:S(2)}) copy-start(f32[128]{0:T(128)} %param.9) | copy-start | bytes 1540
  115.2 16.0 %copy-start.10 = (f32[32]{0:T(128)S(1)}, f32[32]{0:T(128)}, u32[]{:S(2)}) copy-start(f32[32]{0:T(128)} %param.8) | copy-start | bytes 388
  115.7 5.3 %collective-permute-start.7 = (bf16[16,32,256]{2,1,0:T(8,128)(2,1)S(1)}, bf16[16,32,256]{2,1,0:T(8,128)(2,1)S(1)}, u32[]{:S(2)}, u32[]{:S(2)}) collective-permute-start(bf16[16,32,256]{2,1,0:T(8,128)(2,1)S(1)} %get-tuple-element.8), channel_id=1, source_target_pairs={{0,1},{1,0},{2,3},{3,2},{4,5},{5,4},{6,7},{7,6},{8,9},{9,8},{10,11... | collective-permute-start | bytes 786440 | tf_op jit(solution)/shard_map/ppermute | solution.py:190
  121.8 21.5 %all-to-all-start.3 = ((bf16[16,32,256]{2,1,0:T(8,128)(2,1)}), bf16[16,32,256]{2,1,0:T(8,128)(2,1)S(1)}, u32[]{:S(2)}, u32[]{:S(2)}) async-start(bf16[16,32,256]{2,1,0:T(8,128)(2,1)} %add_convert_fusion), calls=%async_computation.3 | async-start | bytes 524288 | tf_op jit(solution)/shard_map/all_to_all | solution.py:191
  130.8 27.0 %copy-start.2 = (bf16[512,1024]{1,0:T(8,128)(2,1)S(1)}, bf16[512,1024]{1,0:T(8,128)(2,1)}, u32[]{:S(2)}) copy-start(bf16[512,1024]{1,0:T(8,128)(2,1)} %get-tuple-element.9) | copy-start | bytes 3145732
  144.2 13.7 %all-to-all-start.4 = ((bf16[16,32,256]{2,1,0:T(8,128)(2,1)}), bf16[16,32,256]{2,1,0:T(8,128)(2,1)S(1)}, u32[]{:S(2)}, u32[]{:S(2)}) async-start(bf16[16,32,256]{2,1,0:T(8,128)(2,1)} %broadcast_in_dim.11), calls=%async_computation.4 | async-start | bytes 524288 | tf_op jit(solution)/shard_map/all_to_all | solution.py:22
  159.2 25.8 %all-to-all-start.5 = ((bf16[32,8,1088]{2,1,0:T(8,128)(2,1)}), bf16[32,8,1088]{2,1,0:T(8,128)(2,1)S(1)}, u32[]{:S(2)}, u32[]{:S(2)}) async-start(bf16[32,8,1088]{2,1,0:T(8,128)(2,1)} %pad_maximum_fusion), calls=%async_computation.5 | async-start | bytes 1179648 | tf_op jit(solution)/shard_map/all_to_all | solution.py:203
Sparse Core Ops, SparseCore 0:
  21.3 51.1 all-gather.2
